TPU v7x, 32 devices: a whole 2x2x4 slice. The times are simulated.
32 devices in a mesh: dp: 8 (over z, y), tensor: 4 (over x, core).
Axes of the slice: x: 2, y: 2, z: 4, core: 2. Of those that a mesh axis runs over, the one named last changes fastest.
Arguments:
- inputs: bfloat16 [16384, 2048], P(('dp', 'tensor')), may hold values from -6 to 6
- lengths: int32 [8], P('dp'), may hold values from 128 to 2048, as said below
- ln1_gain: bfloat16 [2048], replicated, may hold values from 0.5 to 1.5
- ln1_bias: bfloat16 [2048], replicated, may hold values from -1 to 1
- ln2_gain: bfloat16 [2048], replicated, may hold values from 0.5 to 1.5
- ln2_bias: bfloat16 [2048], replicated, may hold values from -1 to 1
- w_qkv: bfloat16 [2048, 6144], P(None, 'tensor'), may hold values from -0.1875 to 0.1875
- b_qkv: bfloat16 [6144], P('tensor'), may hold values from -1 to 1
- w_dense: bfloat16 [2048, 2048], P('tensor'), may hold values from -0.5 to 0.5
- b_dense: bfloat16 [2048], replicated, may hold values from -1 to 1
- w_fc1: bfloat16 [2048, 8192], P(None, 'tensor'), may hold values from -0.125 to 0.125
- b_fc1: bfloat16 [8192], P('tensor'), may hold values from -1 to 1
- w_fc2: bfloat16 [8192, 2048], P('tensor'), may hold values from -0.09375 to 0.09375
- b_fc2: bfloat16 [2048], replicated, may hold values from -1 to 1
- out_grad: bfloat16 [16384, 2048], P(('dp', 'tensor')), may hold values from -6 to 6
Outputs:
- outputs: bfloat16 [16384, 2048], P(('dp', 'tensor'))
- in_grad: float32 [16384, 2048], P(('dp', 'tensor'))
- g_ln1_gain: float32 [2048], replicated
- g_ln1_bias: float32 [2048], replicated
- g_ln2_gain: float32 [2048], replicated
- g_ln2_bias: float32 [2048], replicated
- g_w_qkv: float32 [2048, 6144], P(None, 'tensor')
- g_b_qkv: float32 [6144], P('tensor')
- g_w_dense: float32 [2048, 2048], P('tensor')
- g_b_dense: float32 [2048], replicated
- g_w_fc1: float32 [2048, 8192], P(None, 'tensor')
- g_b_fc1: float32 [8192], P('tensor')
- g_w_fc2: float32 [8192, 2048], P('tensor')
- g_b_fc2: float32 [2048], replicated
Inputs may be any that keep to these rules, and one draw needn't show every extreme that they name: `lengths`: tokens of a sequence at places from its length on are padding; at least one sequence has length exactly 2048 and one exactly 128.
All inputs are finite; a program needn't handle non-finite values.
Results may differ from a plain program's by a relative error of at most 0.014.
The roundings to bfloat16 on the way count: a program that leaves them out, or rounds other values in their place, can miss the bound.
Values may be sent and summed in bfloat16 or wider, within the bound.
No kernel may reach another device: no remote copies, remote signals or barrier semaphores. Data moves between devices by JAX's collectives and lax.ppermute only.
A program may use at most 320 MiB of HBM per device.

v0:
```python
from functools import partial

import jax
import jax.numpy as jnp
from jax import lax
from jax.sharding import PartitionSpec as P

HD = 128
ROT = 32
SEQ = 2048


def layer_norm(values, gain_vec, offset):
    average = jnp.mean(values, axis=-1, keepdims=True)
    centred = values - average
    spread = jnp.mean(centred * centred, axis=-1, keepdims=True)
    return centred * lax.rsqrt(spread + 1e-05) * gain_vec + offset


def rotary_tables(positions):
    places = jnp.arange(positions, dtype=jnp.float32)
    halves = jnp.arange(ROT // 2, dtype=jnp.float32)
    inverse = 10000.0 ** (-2.0 * halves / ROT)
    angles = places[:, None] * inverse[None, :]
    angles = jnp.concatenate([angles, angles], axis=1)
    return (jnp.cos(angles), jnp.sin(angles))


def rotate(block_data, cos_table, sin_table):
    turned = block_data[..., :ROT]
    front_half = turned[..., : ROT // 2]
    back_half = turned[..., ROT // 2 :]
    swapped = jnp.concatenate([-back_half, front_half], axis=-1)
    result = turned * cos_table[:, None, :] + swapped * sin_table[:, None, :]
    return jnp.concatenate([result, block_data[..., ROT:]], axis=-1)


def contract_rows(left, right):
    return lax.dot_general(
        left, right, (((0,), (0,)), ((), ())), preferred_element_type=jnp.float32
    )


def times_transposed(left, right):
    return lax.dot_general(
        left, right, (((1,), (1,)), ((), ())), preferred_element_type=jnp.float32
    )


def shards(
    inputs,
    lengths,
    ln1_gain,
    ln1_bias,
    ln2_gain,
    ln2_bias,
    w_qkv,
    b_qkv,
    w_dense,
    b_dense,
    w_fc1,
    b_fc1,
    w_fc2,
    b_fc2,
    out_grad,
):
    own_rows = inputs.shape[0]
    width = inputs.shape[1]
    seq_count = lengths.shape[0]
    heads_here = w_dense.shape[0] // HD
    group_rows = own_rows * lax.axis_size("tensor")
    block = min(512, SEQ)
    block_count = SEQ // block
    scale = HD ** (-0.5)
    row_floats = inputs.astype(jnp.float32)
    gain_first = ln1_gain.astype(jnp.float32)
    gain_second = ln2_gain.astype(jnp.float32)
    normed_one, back_one = jax.vjp(layer_norm, row_floats, gain_first, ln1_bias.astype(jnp.float32))
    normed_two, back_two = jax.vjp(
        layer_norm, row_floats, gain_second, ln2_bias.astype(jnp.float32)
    )
    whole_one, whole_two = (
        lax.all_gather(normed_one.astype(jnp.bfloat16), "tensor", axis=0, tiled=True),
        lax.all_gather(normed_two.astype(jnp.bfloat16), "tensor", axis=0, tiled=True),
    )
    packed = jnp.dot(whole_one, w_qkv, preferred_element_type=jnp.float32) + b_qkv.astype(
        jnp.float32
    )
    packed = packed.reshape(seq_count, SEQ, heads_here, 3, HD)
    cos_table, sin_table = rotary_tables(SEQ)

    def prepare(raw_query, raw_keys):
        return (
            rotate(raw_query, cos_table, sin_table) * scale,
            rotate(raw_keys, cos_table, sin_table),
        )

    turned_query, turned_keys = prepare(packed[:, :, :, 0], packed[:, :, :, 1])
    queries = turned_query.astype(jnp.bfloat16).transpose(0, 2, 1, 3)
    key_rows = turned_keys.astype(jnp.bfloat16).transpose(0, 2, 1, 3)
    value_rows = packed[:, :, :, 2].astype(jnp.bfloat16).transpose(0, 2, 1, 3)
    places = jnp.arange(SEQ)
    key_valid = places[None, :] < lengths[:, None]
    validity = key_valid.astype(jnp.float32)

    def block_scores(start):
        query_block = lax.dynamic_slice_in_dim(queries, start, block, 2)
        scores = jnp.einsum(
            "bhqd,bhkd->bhqk", query_block, key_rows, preferred_element_type=jnp.float32
        )
        query_places = start + jnp.arange(block)
        allowed = (places[None, :] <= query_places[:, None])[None, None] & key_valid[
            :, None, None, :
        ]
        return (query_block, jnp.where(allowed, scores, -1e30))

    def forward_block(start):
        _, masked = block_scores(start)
        highest = jnp.max(masked, axis=3, keepdims=True)
        weights = jnp.exp(masked - highest)
        totals = jnp.sum(weights, axis=3, keepdims=True)
        attn_probs = weights / totals
        context_block = jnp.einsum(
            "bhqk,bhkd->bhqd",
            attn_probs.astype(jnp.bfloat16),
            value_rows,
            preferred_element_type=jnp.float32,
        )
        return (context_block, highest, totals)

    starts = jnp.arange(block_count) * block
    context_blocks, highest_all, totals_all = lax.map(forward_block, starts)
    context = (
        context_blocks.transpose(1, 0, 3, 2, 4).reshape(seq_count, SEQ, heads_here, HD)
        * validity[:, :, None, None]
    )
    context = context.astype(jnp.bfloat16).reshape(group_rows, heads_here * HD)
    hidden = jnp.dot(whole_two, w_fc1, preferred_element_type=jnp.float32) + b_fc1.astype(
        jnp.float32
    )
    active = jax.nn.gelu(hidden, approximate=False).astype(jnp.bfloat16)
    branches = lax.psum_scatter(
        jnp.dot(context, w_dense, preferred_element_type=jnp.float32)
        + jnp.dot(active, w_fc2, preferred_element_type=jnp.float32),
        "tensor",
        scatter_dimension=0,
        tiled=True,
    )
    outputs = (
        row_floats + branches + b_dense.astype(jnp.float32) + b_fc2.astype(jnp.float32)
    ).astype(jnp.bfloat16)
    grad_rows = lax.all_gather(out_grad, "tensor", axis=0, tiled=True)
    out_bias_grad = jnp.sum(grad_rows, axis=0, dtype=jnp.float32)
    dense_grad = contract_rows(context, grad_rows)
    fc2_grad = contract_rows(active, grad_rows)
    _, gelu_back = jax.vjp(partial(jax.nn.gelu, approximate=False), hidden)
    hidden_grad = gelu_back(times_transposed(grad_rows, w_fc2))[0].astype(jnp.bfloat16)
    fc1_grad = contract_rows(whole_two, hidden_grad)
    fc1_bias_grad = jnp.sum(hidden_grad, axis=0, dtype=jnp.float32)
    context_grad = (
        times_transposed(grad_rows, w_dense)
        .astype(jnp.bfloat16)
        .reshape(seq_count, SEQ, heads_here, HD)
    )
    context_grad = (context_grad * validity[:, :, None, None].astype(jnp.bfloat16)).transpose(
        0, 2, 1, 3
    )

    def backward_block(carry, element):
        key_grad, value_grad = carry
        start, highest, totals = element
        query_block, masked = block_scores(start)
        attn_probs = jnp.exp(masked - highest) / totals
        grad_block = lax.dynamic_slice_in_dim(context_grad, start, block, 2)
        probs_grad = jnp.einsum(
            "bhqd,bhkd->bhqk", grad_block, value_rows, preferred_element_type=jnp.float32
        )
        centre = jnp.sum(attn_probs * probs_grad, axis=3, keepdims=True)
        score_grad = (attn_probs * (probs_grad - centre)).astype(jnp.bfloat16)
        query_grad = jnp.einsum(
            "bhqk,bhkd->bhqd", score_grad, key_rows, preferred_element_type=jnp.float32
        )
        key_grad = key_grad + jnp.einsum(
            "bhqk,bhqd->bhkd", score_grad, query_block, preferred_element_type=jnp.float32
        )
        value_grad = value_grad + jnp.einsum(
            "bhqk,bhqd->bhkd",
            attn_probs.astype(jnp.bfloat16),
            grad_block,
            preferred_element_type=jnp.float32,
        )
        return ((key_grad, value_grad), query_grad)

    zero_grads = jnp.zeros((seq_count, heads_here, SEQ, HD), jnp.float32)
    (key_grad, value_grad), query_blocks = lax.scan(
        backward_block, (zero_grads, zero_grads), (starts, highest_all, totals_all)
    )
    query_grad = query_blocks.transpose(1, 0, 3, 2, 4).reshape(seq_count, SEQ, heads_here, HD)
    _, prepare_back = jax.vjp(prepare, packed[:, :, :, 0], packed[:, :, :, 1])
    raw_query_grad, raw_key_grad = prepare_back((query_grad, key_grad.transpose(0, 2, 1, 3)))
    packed_grad = jnp.stack(
        [raw_query_grad, raw_key_grad, value_grad.transpose(0, 2, 1, 3)], axis=3
    )
    packed_grad = packed_grad.astype(jnp.bfloat16).reshape(group_rows, 3 * heads_here * HD)
    qkv_grad = contract_rows(whole_one, packed_grad)
    qkv_bias_grad = jnp.sum(packed_grad, axis=0, dtype=jnp.float32)
    normed_grads = lax.psum_scatter(
        jnp.concatenate(
            [times_transposed(packed_grad, w_qkv), times_transposed(hidden_grad, w_fc1)], axis=1
        ).astype(jnp.bfloat16),
        "tensor",
        scatter_dimension=0,
        tiled=True,
    ).astype(jnp.float32)
    input_one, gain_one, bias_one = back_one(normed_grads[:, :width])
    input_two, gain_two, bias_two = back_two(normed_grads[:, width:])
    in_grad = out_grad.astype(jnp.float32) + input_one + input_two
    gain_one, bias_one, gain_two, bias_two = lax.psum(
        (gain_one, bias_one, gain_two, bias_two), ("dp", "tensor")
    )
    qkv_grad, qkv_bias_grad, dense_grad, fc1_grad, fc1_bias_grad, fc2_grad, out_bias_grad = (
        lax.psum(qkv_grad.astype(jnp.bfloat16), "dp").astype(jnp.float32),
        lax.psum(qkv_bias_grad.astype(jnp.bfloat16), "dp").astype(jnp.float32),
        lax.psum(dense_grad.astype(jnp.bfloat16), "dp").astype(jnp.float32),
        lax.psum(fc1_grad.astype(jnp.bfloat16), "dp").astype(jnp.float32),
        lax.psum(fc1_bias_grad.astype(jnp.bfloat16), "dp").astype(jnp.float32),
        lax.psum(fc2_grad.astype(jnp.bfloat16), "dp").astype(jnp.float32),
        lax.psum(out_bias_grad.astype(jnp.bfloat16), "dp").astype(jnp.float32),
    )
    return (
        outputs,
        in_grad,
        gain_one,
        bias_one,
        gain_two,
        bias_two,
        qkv_grad,
        qkv_bias_grad,
        dense_grad,
        out_bias_grad,
        fc1_grad,
        fc1_bias_grad,
        fc2_grad,
        out_bias_grad,
    )


def solution(mesh):
    placed = (
        P(("dp", "tensor"), None),
        P("dp"),
        P(),
        P(),
        P(),
        P(),
        P(None, "tensor"),
        P("tensor"),
        P("tensor", None),
        P(),
        P(None, "tensor"),
        P("tensor"),
        P("tensor", None),
        P(),
        P(("dp", "tensor"), None),
    )
    return jax.shard_map(
        shards,
        mesh=mesh,
        in_specs=placed,
        out_specs=(
            P(("dp", "tensor"), None),
            P(("dp", "tensor"), None),
            P(),
            P(),
            P(),
            P(),
            P(None, "tensor"),
            P("tensor"),
            P("tensor", None),
            P(),
            P(None, "tensor"),
            P("tensor"),
            P("tensor", None),
            P(),
        ),
        check_vma=False,
    )
```

profile of v0, /device:TPU:0, one launch (start us, length us, event | category | flops | bytes accessed | tf_op | source)
XLA Modules:
  0.0 1759.7 jit_solution(367036084671340730)
XLA Ops:
  24.6 52.4 %all-gather.4.cloned.1.call-done = bf16[2048,2048]{1,0:T(8,128)(2,1)} async-done(((bf16[512,2048]{1,0:T(8,128)(2,1)}), bf16[2048,2048]{1,0:T(8,128)(2,1)}) %all-gather.4.cloned.1.call-update) | async-done | bytes 8388624 | tf_op jit(solution)/shard_map/all_gather | solution.py:83
  77.1 18.0 %convolution_add_fusion = f32[2048,1536]{0,1:T(8,128)S(1)} fusion(bf16[2048,2048]{1,0:T(8,128)(2,1)} %all-gather.4.cloned.1.call-done, bf16[2048,1536]{1,0:T(8,128)(2,1)} %param.25, f32[1536]{0:T(1024)S(1)} %convert_element_type.182), kind=kOutput, calls=%fused_computation.75 | convolution fusion | flops 12888047616 | bytes 27269120 | tf_op jit(solution)/shard_map/dot_general | solution.py:86
  138.8 11.6 fusion.82
  156.3 76.0 %while.30 = (s32[]{:T(128)}, f32[4,1,4,512,128]{4,3,2,1,0:T(8,128)}, f32[4,1,4,512,1]{3,2,4,1,0:T(4,128)S(1)}, f32[4,1,4,512,1]{3,2,4,1,0:T(4,128)S(1)}, s32[4]{...) while((s32[]{:T(128)}, ...), condition=%wide.region_5.6_spmd.clone, body=%wide.region_2.5_spmd.clone.sunk | while | flops 2187328000 | bytes 68764360 | solution.py:132
  248.5 269.3 %while.31 = (s32[]{:T(128)}, f32[1,4,2048,128]{3,2,1,0:T(8,128)}, f32[1,4,2048,128]{3,2,1,0:T(8,128)}, f32[4,1,4,512,128]{4,3,0,2,1:T(8,128)}, s32[4]{0:T(128)S(...) while((s32[]{:T(128)}, f32[1,4,2048,128]{3,2,1,0:T(8,128)}, ...), condition=%wide.region_9.10_spmd.clone, body=%wide.region_7.9_spmd.clone.sunk | while | flops 5412749824 | bytes 204546864 | solution.py:195
  263.8 12.9 multiply_reduce_fusion.2
  276.7 14.9 multiply_convert_fusion.3
  329.0 12.9 multiply_reduce_fusion.2
  342.0 14.9 multiply_convert_fusion.3
  369.9 11.9 bitcast_add_fusion.5
  396.9 12.9 multiply_reduce_fusion.2
  409.8 14.9 multiply_convert_fusion.3
  437.7 11.9 bitcast_add_fusion.5
  464.7 12.9 multiply_reduce_fusion.2
  477.6 14.9 multiply_convert_fusion.3
  505.6 11.9 bitcast_add_fusion.5
  570.9 21.5 %fusion.100 = f32[2048,2048]{1,0:T(8,128)S(1)} fusion(bf16[2048,2048]{1,0:T(8,128)(2,1)} %all-gather.6.cloned.1.call-done, bf16[2048,2048]{1,0:T(8,128)(2,1)} %param.29), kind=kOutput, calls=%fused_computation.164 | convolution fusion | flops 17179869184 | bytes 33554432 | tf_op jit(solution)/shard_map/dot_general | solution.py:138
  592.4 61.6 %fusion.96 = (bf16[2048]{0:T(1024)(128)(2,1)}, bf16[2048,2048]{1,0:T(8,128)(2,1)}, f32[2048,2048]{1,0:T(8,128)}) fusion(f32[2048,2048]{1,0:T(8,128)S(1)} %fusion.100, f32[2048]{0:T(1024)S(1)} %copy-done.29, bf16[2048,2048]{1,0:T(8,128)(2,1)} %all-gather.8.cloned.1.call-done, bf16[2048,2048]{1,0:T(8,128)(2,1)} %param.31), kind=kOutput, calls=%fused_computation.161 | convolution fusion | flops 17490245632 | bytes 58732544 | tf_op jit(solution)/shard_map/dot_general | solution.py:45
  653.9 11.1 multiply_convert_fusion.1
  665.1 19.6 %convolution_convert_fusion.4 = bf16[2048,1536]{1,0:T(8,128)(2,1)} fusion(bf16[2048,2048]{1,0:T(8,128)(2,1)} %all-gather.4.cloned.1.call-done, bf16[2048,1536]{0,1:T(8,128)(2,1)} %bitcast.188), kind=kOutput, calls=%fused_computation.81 | convolution fusion | flops 12888047616 | bytes 20971520 | tf_op jit(solution)/shard_map/dot_general | solution.py:39
  684.7 20.7 %convolution_convert_fusion = bf16[2048,2048]{1,0:T(8,128)(2,1)} fusion(bf16[2048,2048]{1,0:T(8,128)(2,1)S(1)} %copy-done.17, bf16[2048,2048]{1,0:T(8,128)(2,1)S(1)} %bitcast.187), kind=kOutput, calls=%fused_computation.77 | convolution fusion | flops 17184063488 | bytes 25165824 | tf_op jit(solution)/shard_map/dot_general | solution.py:39
  705.3 22.6 %convolution_convert_fusion.1 = bf16[2048,2048]{1,0:T(8,128)(2,1)} fusion(bf16[2048,2048]{1,0:T(8,128)(2,1)S(1)} %copy-done.44, bf16[2048,2048]{1,0:T(8,128)(2,1)} %get-tuple-element.273), kind=kOutput, calls=%fused_computation.78 | convolution fusion | flops 17184063488 | bytes 25165824 | tf_op jit(solution)/shard_map/dot_general | solution.py:39
  734.1 17.8 %convolution_convert_fusion.3 = bf16[2048,2048]{1,0:T(8,128)(2,1)S(1)} fusion(bf16[2048,1536]{0,1:T(8,128)(2,1)} %bitcast.189, bf16[2048,1536]{1,0:T(8,128)(2,1)} %param.25), kind=kOutput, calls=%fused_computation.80 | convolution fusion | flops 12889096192 | bytes 20971520 | tf_op jit(solution)/shard_map/dot_general | solution.py:45
  751.9 22.4 %convolution_convert_fusion.2 = bf16[2048,2048]{1,0:T(8,128)(2,1)S(1)} fusion(bf16[2048,2048]{1,0:T(8,128)(2,1)} %get-tuple-element.273, bf16[2048,2048]{1,0:T(8,128)(2,1)} %param.29), kind=kOutput, calls=%fused_computation.79 | convolution fusion | flops 17184063488 | bytes 25165824 | tf_op jit(solution)/shard_map/dot_general | solution.py:45
  791.9 26.5 %convolution_add_fusion.1 = f32[2048,2048]{1,0:T(8,128)} fusion(f32[2048,2048]{1,0:T(8,128)} %fusion.92, bf16[2048,2048]{1,0:T(8,128)(2,1)} %multiply_convert_fusion.1, bf16[2048,2048]{1,0:T(8,128)(2,1)} %param.31), kind=kOutput, calls=%fused_computation.76 | convolution fusion | flops 17184063488 | bytes 50331648 | tf_op jit(solution)/shard_map/dot_general | solution.py:144
  824.0 39.7 %all-reduce.9 = (bf16[1536]{0:T(1024)(128)(2,1)S(1)}, bf16[2048]{0:T(1024)(128)(2,1)S(1)}, bf16[2048]{0:T(1024)(128)(2,1)S(1)}) all-reduce(bf16[1536]{0:T(1024)(128)(2,1)S(1)} %reduce_sum.171, bf16[2048]{0:T(1024)(128)(2,1)S(1)} %reduce_sum.172, bf16[2048]{0:T(1024)(128)(2,1)S(1)} %copy-done.43), channel_id=1, replica_groups=mesh['dp'=8,'tensor'=4] {'dp'}, use_global_device_ids=true, to_apply=%region_25.26 | all-reduce | flops 5632 | bytes 22528 | tf_op jit(solution)/shard_map/psum | solution.py:223
  864.9 620.7 %all-reduce.13.cloned.1.call-done = (bf16[2048,1536]{1,0:T(8,128)(2,1)}, bf16[512,2048]{1,0:T(8,128)(2,1)}, bf16[2048,2048]{1,0:T(8,128)(2,1)}, bf16[2048,2048]{1,0:T(8,128)(2,1)}) async-done(((bf16[2048,1536]{1,0:T(8,128)(2,1)}, bf16[512,2048]{1,0:T(8,128)(2,1)}, bf16[2048,2048]{1,0:T(8,128)(2,1)}, bf16[2048,2048]{1,0:T(8,128)(2,1)}), (bf16[2048,1536]{1,0:T(8,128)(2,1)}, bf16[512,2048]{1,0:T(8,128)(2,1)}, ...) | async-done | bytes 25165840 | tf_op jit(solution)/shard_map/psum | solution.py:222
  1485.7 14.5 convert_element_type.209
  1500.1 14.6 convert_element_type.212
  1526.8 86.6 %reduce-scatter.5.cloned.1.call-done = bf16[512,4096]{1,0:T(8,128)(2,1)} async-done(((bf16[2048,4096]{1,0:T(8,128)(2,1)}), bf16[512,4096]{1,0:T(8,128)(2,1)}) %reduce-scatter.5.cloned.1.call-update) | async-done | bytes 4194320 | tf_op jit(solution)/shard_map/reduce_scatter | solution.py:207
  1623.6 40.6 %all-reduce.8 = (f32[2048]{0:T(1024)}, f32[2048]{0:T(1024)}, f32[2048]{0:T(1024)}, f32[2048]{0:T(1024)}) all-reduce(f32[2048]{0:T(1024)S(1)} %get-tuple-element.210, f32[2048]{0:T(1024)S(1)} %get-tuple-element.216, f32[2048]{0:T(1024)S(1)} %get-tuple-element.209, ...), channel_id=1, replica_groups=mesh['dp'=8,'tensor'=4] {'dp','tensor'}, use_global_device_ids=true, to_apply=%region_16.17 | all-reduce | flops 8192 | bytes 65536 | tf_op jit(solution)/shard_map/psum | solution.py:218
  1664.2 78.4 %reduce-scatter.3.cloned.1.call-done = f32[512,2048]{1,0:T(8,128)} async-done(((f32[2048,2048]{1,0:T(8,128)}), f32[512,2048]{1,0:T(8,128)}) %reduce-scatter.3.cloned.1.call-update) | async-done | bytes 4194320 | tf_op jit(solution)/shard_map/reduce_scatter | solution.py:142
  (269 shorter events, 379.8 us)
Async XLA Ops:
  7.2 225.1 %copy-start = (bf16[512,2048]{1,0:T(8,128)(2,1)S(1)}, bf16[512,2048]{1,0:T(8,128)(2,1)}, u32[]{:S(2)}) copy-start(bf16[512,2048]{1,0:T(8,128)(2,1)} %param.27) | copy-start | bytes 6291460
  7.2 69.8 %all-gather.4.cloned.1.call-start = ((), (), s32[]{:S(2)}) async-start(), calls=%async_computation.2 | async-start | bytes 10485760 | tf_op jit(solution)/shard_map/all_gather | solution.py:83
  15.9 216.3 %all-gather.8.cloned.1.call-start = ((), (), s32[]{:S(2)}) async-start(), calls=%async_computation.5 | async-start | bytes 10485760 | tf_op jit(solution)/shard_map/all_gather | solution.py:152
  16.7 554.2 %all-gather.6.cloned.1.call-start = ((), (), s32[]{:S(2)}) async-start(), calls=%async_computation.3 | async-start | bytes 10485760 | tf_op jit(solution)/shard_map/all_gather | solution.py:84
  17.4 1468.3 %all-reduce.13.cloned.1.call-start = ((), (), s32[]{:S(2)}) async-start(), calls=%async_computation.7 | async-start | bytes 50331648 | tf_op jit(solution)/shard_map/psum | solution.py:222
  20.8 118.0 %copy-start.13 = (f32[2048,32]{1,0:T(8,128)}, f32[2048,32]{1,0:T(8,128)S(1)}, u32[]{:S(2)}) copy-start(f32[2048,32]{1,0:T(8,128)S(1)} %copy.71) | copy-start | bytes 786436
  138.8 11.6 copy-start.16
  251.2 12.5 copy-start.3
  291.6 8.5 copy-start.4
  316.5 12.5 copy-start.3
  356.8 9.8 copy-start.1
  356.8 9.8 copy-start.4
  384.3 12.5 copy-start.3
  424.7 9.8 copy-start.1
  424.7 9.8 copy-start.4
  452.1 12.5 copy-start.3
  492.5 9.8 copy-start.1
  492.5 9.8 copy-start.4
  570.8 21.5 %copy-start.29 = (f32[2048]{0:T(1024)S(1)}, f32[2048]{0:T(1024)}, u32[]{:S(2)}) copy-start(f32[2048]{0:T(1024)} %convert_element_type.190) | copy-start | bytes 24580
  653.9 30.7 %slice-start = ((s8[8388608]{0:T(1024)(128)(4,1)}), s8[4194304]{0:T(1024)(128)(4,1)S(1)}, s32[]{:S(2)}) async-start(s8[8388608]{0:T(1024)(128)(4,1)} %bitcast.186), calls=%async_computation.8 | async-start | bytes 8388608
  665.1 19.6 %slice-start.1 = ((s8[8388608]{0:T(1024)(128)(4,1)}), s8[4194304]{0:T(1024)(128)(4,1)S(1)}, s32[]{:S(2)}) async-start(s8[8388608]{0:T(1024)(128)(4,1)} %bitcast.186), calls=%async_computation.9 | async-start | bytes 8388608
  665.1 19.6 %copy-start.17 = (bf16[2048,2048]{1,0:T(8,128)(2,1)S(1)}, bf16[2048,2048]{1,0:T(8,128)(2,1)}, u32[]{:S(2)}) copy-start(bf16[2048,2048]{1,0:T(8,128)(2,1)} %multiply_convert_fusion.1) | copy-start | bytes 25165828
  684.7 20.7 %copy-start.44 = (bf16[2048,2048]{1,0:T(8,128)(2,1)S(1)}, bf16[2048,2048]{1,0:T(8,128)(2,1)}, u32[]{:S(2)}) copy-start(bf16[2048,2048]{1,0:T(8,128)(2,1)} %all-gather.6.cloned.1.call-done) | copy-start | bytes 25165828
  705.3 22.6 %copy-start.18 = (f32[1,4,512,4,128]{4,3,2,1,0:T(4,128)S(1)}, f32[1,4,512,4,128]{4,3,2,1,0:T(4,128)}, u32[]{:S(2)}) copy-start(f32[1,4,512,4,128]{4,3,2,1,0:T(4,128)} %copy.75) | copy-start | bytes 12582916
  705.3 22.6 %copy-start.34 = (f32[2048]{0:T(1024)S(1)}, f32[2048]{0:T(1024)}, u32[]{:S(2)}) copy-start(f32[2048]{0:T(1024)} %fusion.88) | copy-start | bytes 24580
  734.0 879.3 %reduce-scatter.5.cloned.1.call-start = ((), (), s32[]{:S(2)}) async-start(), calls=%async_computation.6 | async-start | bytes 20971520 | tf_op jit(solution)/shard_map/reduce_scatter | solution.py:207
  780.9 961.7 %reduce-scatter.3.cloned.1.call-start = ((), (), s32[]{:S(2)}) async-start(), calls=%async_computation.4 | async-start | bytes 20971520 | tf_op jit(solution)/shard_map/reduce_scatter | solution.py:142
  863.7 888.3 %copy-start.26 = (f32[2048]{0:T(1024)}, f32[2048]{0:T(1024)S(1)}, u32[]{:S(2)}) copy-start(f32[2048]{0:T(1024)S(1)} %convert_element_type.207) | copy-start | bytes 24580
  1514.8 9.5 copy-start.19
  1526.8 90.0 %copy-start.21 = (f32[2048]{0:T(1024)S(1)}, f32[2048]{0:T(1024)}, u32[]{:S(2)}) copy-start(f32[2048]{0:T(1024)} %copy-done.20) | copy-start | bytes 24580
  1526.8 90.0 %copy-start.23 = (f32[2048]{0:T(1024)S(1)}, f32[2048]{0:T(1024)}, u32[]{:S(2)}) copy-start(f32[2048]{0:T(1024)} %copy-done.22) | copy-start | bytes 24580
  1526.8 90.0 %copy-start.25 = (f32[512]{0:T(512)S(1)}, f32[512]{0:T(512)}, u32[]{:S(2)}) copy-start(f32[512]{0:T(512)} %copy-done.24) | copy-start | bytes 6148
  (33 other events, 129.2 us)
Sparse Core Ops, SparseCore 0:
  16.0 60.9 all-gather.3
  78.6 58.2 all-gather.7
  139.1 58.2 all-gather.5
  734.1 751.4 all-reduce.12
  1488.3 125.0 reduce-scatter.4
  1615.8 126.8 reduce-scatter.2
where the time goes:
time: 1760 us
  waiting for transfers between devices  840 us (48%)
  matrix products  489 us (28%)
  other arithmetic  246 us (14%)
  blocking collectives  80.3 us (5%)
  local copies, waits for them, and re-layouts  71.8 us (4%)
    psum x1, waiting for transfers between devices, shards(): lax.psum(qkv_grad.astype(jnp.bfloat16), 'dp').astype(jnp.float32)  621 us
    dot_general x4, matrix products, times_transposed(): lax.dot_general(left, right, (((1,), (1,)), ((), ())), preferred_element_...  111 us
    reduce_scatter x1, waiting for transfers between devices, shards(): lax.psum_scatter(jnp.concatenate([times_transposed(packed_grad, w_qkv), t...  86.6 us
    reduce_scatter x1, waiting for transfers between devices, shards(): lax.psum_scatter(jnp.dot(context, w_dense, preferred_element_type=jnp.flo...  78.4 us
    dot_general x8, matrix products, block_scores(): jnp.einsum('bhqd,bhkd->bhqk', query_block, key_rows, preferred_element_ty...  69.6 us
    dot_general x4, matrix products, contract_rows(): lax.dot_general(left, right, (((0,), (0,)), ((), ())), preferred_element_...  68.9 us
    convert_element_type x4, other arithmetic, backward_block(): score_grad = (attn_probs * (probs_grad - centre)).astype(jnp.bfloat16)  59.4 us
    all_gather x1, waiting for transfers between devices, shards(): lax.all_gather(normed_one.astype(jnp.bfloat16), 'tensor', axis=0, tiled=T...  52.4 us
  transfers between devices with their start and end apart: 6, of which 4 were waited for; matrix products, arithmetic and copies ran while one was open for 35% of the time, Pallas kernels for 0%

commit v1 on v0

v1 whole, which is shorter than its diff:
```python
from functools import partial

import jax
import jax.numpy as jnp
from jax import lax
from jax.experimental import pallas as pl
from jax.experimental.pallas import tpu as pltpu
from jax.sharding import PartitionSpec as P

HD = 128
ROT = 32
SEQ = 2048
BLOCK = 512
EPS = 1e-05
F32 = jnp.float32
BF16 = jnp.bfloat16


def dot_nn(left, right):
    return lax.dot_general(left, right, (((1,), (0,)), ((), ())), preferred_element_type=F32)


def dot_nt(left, right):
    return lax.dot_general(left, right, (((1,), (1,)), ((), ())), preferred_element_type=F32)


def dot_tn(left, right):
    return lax.dot_general(left, right, (((0,), (0,)), ((), ())), preferred_element_type=F32)


def rotary_tables():
    places = jnp.arange(SEQ, dtype=F32)
    lanes = jnp.arange(HD)
    inverse = 10000.0 ** (-2.0 * (lanes % (ROT // 2)).astype(F32) / ROT)
    angles = places[:, None] * inverse[None, :]
    cosines, sines = jnp.cos(angles), jnp.sin(angles)
    turned = (lanes < ROT)[None, :]
    front = (lanes < ROT // 2)[None, :]
    cos_table = jnp.where(turned, cosines, 1.0)
    low_table = jnp.where(front, -sines, 0.0)
    high_table = jnp.where(turned & ~front, sines, 0.0)
    return cos_table, low_table, high_table


def shifted_mix(rows, low_rows, high_rows):
    half = ROT // 2
    return pltpu.roll(rows, HD - half, 1) * low_rows + pltpu.roll(rows, half, 1) * high_rows


def diagonal(shape):
    return lax.broadcasted_iota(jnp.int32, shape, 0) <= lax.broadcasted_iota(jnp.int32, shape, 1)


def attend_kernel(
    length_ref, packed_ref, cos_ref, low_ref, high_ref, q_ref, k_ref, v_ref, ctx_ref, lse_ref, vt_ref
):
    length = length_ref[0]
    scale = HD ** (-0.5)
    for index in range(SEQ // BLOCK):
        rows = pl.ds(index * BLOCK, BLOCK)
        cos_rows, low_rows, high_rows = cos_ref[rows, :], low_ref[rows, :], high_ref[rows, :]
        raw_query = packed_ref[rows, 0:HD]
        raw_key = packed_ref[rows, HD : 2 * HD]
        value = packed_ref[rows, 2 * HD : 3 * HD]
        query = (raw_query * cos_rows + shifted_mix(raw_query, low_rows, high_rows)) * scale
        q_ref[rows, :] = query.astype(BF16)
        key = raw_key * cos_rows + shifted_mix(raw_key, low_rows, high_rows)
        k_ref[rows, :] = key.astype(BF16)
        v_ref[rows, :] = value.astype(BF16)
        vt_ref[:, rows] = jnp.transpose(value).astype(BF16)
    for index in range(SEQ // BLOCK):
        before = index * BLOCK
        rows = pl.ds(before, BLOCK)

        @pl.when(before < length)
        def _(before=before, rows=rows):
            query = q_ref[rows, :]
            near = jnp.where(diagonal((BLOCK, BLOCK)), dot_nt(k_ref[rows, :], query), -1e30)
            highest = jnp.max(near, axis=0, keepdims=True)
            if before:
                far = dot_nt(k_ref[0:before, :], query)
                highest = jnp.maximum(highest, jnp.max(far, axis=0, keepdims=True))
            near = jnp.exp(near - highest)
            totals = jnp.sum(near, axis=0, keepdims=True)
            if before:
                far = jnp.exp(far - highest)
                totals = totals + jnp.sum(far, axis=0, keepdims=True)
            inverse = 1.0 / totals
            turned = dot_nn(vt_ref[:, rows], (near * inverse).astype(BF16))
            if before:
                turned = turned + dot_nn(vt_ref[:, 0:before], (far * inverse).astype(BF16))
            context = jnp.transpose(turned)
            places = before + lax.broadcasted_iota(jnp.int32, (BLOCK, HD), 0)
            ctx_ref[rows, :] = jnp.where(places < length, context, 0.0).astype(BF16)
            lse_ref[0, :, rows] = highest + jnp.log(totals)

        @pl.when(before >= length)
        def _(rows=rows):
            ctx_ref[rows, :] = jnp.zeros((BLOCK, HD), BF16)
            lse_ref[0, :, rows] = jnp.zeros((1, BLOCK), F32)


def attend(packed, length, tables):
    heads = packed.shape[1] // (3 * HD)
    table_spec = pl.BlockSpec((SEQ, HD), lambda h, n: (0, 0), pipeline_mode=pl.Buffered(1))
    head_spec = pl.BlockSpec((SEQ, HD), lambda h, n: (0, h))
    rows = jax.ShapeDtypeStruct((SEQ, heads * HD), BF16)
    pairs = heads * SEQ * SEQ // 2
    return pl.pallas_call(
        attend_kernel,
        out_shape=(rows, rows, rows, rows, jax.ShapeDtypeStruct((heads, 1, SEQ), F32)),
        grid_spec=pltpu.PrefetchScalarGridSpec(
            num_scalar_prefetch=1,
            grid=(heads,),
            in_specs=[pl.BlockSpec((SEQ, 3 * HD), lambda h, n: (0, h))] + [table_spec] * 3,
            out_specs=[head_spec] * 4 + [pl.BlockSpec((1, 1, SEQ), lambda h, n: (h, 0, 0))],
            scratch_shapes=[pltpu.VMEM((HD, SEQ), BF16)],
        ),
        compiler_params=pltpu.CompilerParams(vmem_limit_bytes=56 << 20),
        cost_estimate=pl.CostEstimate(
            flops=4 * pairs * HD, transcendentals=pairs, bytes_accessed=heads * SEQ * HD * 20
        ),
        name="attend",
    )(length, packed, *tables)


def attend_back_kernel(
    length_ref,
    q_ref,
    k_ref,
    v_ref,
    grad_ref,
    lse_ref,
    cos_ref,
    low_ref,
    high_ref,
    out_ref,
    kt_ref,
    dk_ref,
    dv_ref,
):
    length = length_ref[0]
    scale = HD ** (-0.5)
    kt_ref[...] = jnp.transpose(k_ref[...].astype(F32)).astype(BF16)
    dk_ref[...] = jnp.zeros_like(dk_ref)
    dv_ref[...] = jnp.zeros_like(dv_ref)

    def unturn(rows, grad):
        return grad * cos_ref[rows, :] - shifted_mix(grad, low_ref[rows, :], high_ref[rows, :])

    for index in range(SEQ // BLOCK):
        before = index * BLOCK
        rows = pl.ds(before, BLOCK)

        @pl.when(before < length)
        def _(before=before, rows=rows):
            query = q_ref[rows, :]
            places = before + lax.broadcasted_iota(jnp.int32, (BLOCK, HD), 0)
            grad = jnp.where(places < length, grad_ref[rows, :].astype(F32), 0.0).astype(BF16)
            lse = lse_ref[0, :, rows]
            parts = [rows] + ([pl.ds(0, before)] if before else [])
            probs, grads = [], []
            for number, keys in enumerate(parts):
                scores = dot_nt(k_ref[keys, :], query)
                if number == 0:
                    scores = jnp.where(diagonal((BLOCK, BLOCK)), scores, -1e30)
                probs.append(jnp.exp(scores - lse))
                grads.append(dot_nt(v_ref[keys, :], grad))
            centre = sum(
                jnp.sum(prob * prob_grad, axis=0, keepdims=True)
                for prob, prob_grad in zip(probs, grads)
            )
            turned = jnp.zeros((HD, BLOCK), F32)
            for keys, prob, prob_grad in zip(parts, probs, grads):
                score_grad = (prob * (prob_grad - centre)).astype(BF16)
                dv_ref[keys, :] += dot_nn(prob.astype(BF16), grad)
                dk_ref[keys, :] += dot_nn(score_grad, query)
                turned = turned + dot_nn(kt_ref[:, keys], score_grad)
            out_ref[rows, 0:HD] = unturn(rows, jnp.transpose(turned) * scale).astype(BF16)

        @pl.when(before >= length)
        def _(rows=rows):
            out_ref[rows, 0:HD] = jnp.zeros((BLOCK, HD), BF16)

    for index in range(SEQ // BLOCK):
        rows = pl.ds(index * BLOCK, BLOCK)
        out_ref[rows, HD : 2 * HD] = unturn(rows, dk_ref[rows, :]).astype(BF16)
        out_ref[rows, 2 * HD : 3 * HD] = dv_ref[rows, :].astype(BF16)


def attend_back(queries, key_rows, value_rows, grad, lse, length, tables):
    heads = queries.shape[1] // HD
    table_spec = pl.BlockSpec((SEQ, HD), lambda h, n: (0, 0), pipeline_mode=pl.Buffered(1))
    head_spec = pl.BlockSpec((SEQ, HD), lambda h, n: (0, h))
    pairs = heads * SEQ * SEQ // 2
    return pl.pallas_call(
        attend_back_kernel,
        out_shape=jax.ShapeDtypeStruct((SEQ, heads * 3 * HD), BF16),
        grid_spec=pltpu.PrefetchScalarGridSpec(
            num_scalar_prefetch=1,
            grid=(heads,),
            in_specs=[head_spec] * 4
            + [pl.BlockSpec((1, 1, SEQ), lambda h, n: (h, 0, 0))]
            + [table_spec] * 3,
            out_specs=pl.BlockSpec((SEQ, 3 * HD), lambda h, n: (0, h)),
            scratch_shapes=[
                pltpu.VMEM((HD, SEQ), BF16),
                pltpu.VMEM((SEQ, HD), F32),
                pltpu.VMEM((SEQ, HD), F32),
            ],
        ),
        compiler_params=pltpu.CompilerParams(vmem_limit_bytes=56 << 20),
        cost_estimate=pl.CostEstimate(
            flops=10 * pairs * HD, transcendentals=pairs, bytes_accessed=heads * SEQ * HD * 14
        ),
        name="attend_back",
    )(length, queries, key_rows, value_rows, grad, lse, *tables)


def swap_tensor(values, bit):
    count = lax.axis_size("tensor")
    return lax.ppermute(values, "tensor", [(t, t ^ bit) for t in range(count)])


def gather_rows(block):
    if lax.axis_size("tensor") != 4:
        return lax.all_gather(block, "tensor", axis=0, tiled=True)
    place = lax.axis_index("tensor")
    far = swap_tensor(block, 2)
    mate = swap_tensor(block, 1)
    far_mate = swap_tensor(far, 1)
    rows = block.shape[0]
    whole = jnp.zeros((4 * rows, block.shape[1]), block.dtype)
    for bits, part in ((0, block), (1, mate), (2, far), (3, far_mate)):
        whole = lax.dynamic_update_slice_in_dim(whole, part, (place ^ bits) * rows, 0)
    return whole


def scatter_rows(partial_rows):
    if lax.axis_size("tensor") != 4:
        return lax.psum_scatter(
            partial_rows.astype(BF16), "tensor", scatter_dimension=0, tiled=True
        ).astype(F32)
    place = lax.axis_index("tensor")
    chip, core = place // 2, place % 2
    blocks = partial_rows.reshape(2, 2, -1, partial_rows.shape[1])
    kept = lax.dynamic_index_in_dim(blocks, core, 1, False).astype(F32)
    sent = lax.dynamic_index_in_dim(blocks, 1 - core, 1, False).astype(BF16)
    both = kept + swap_tensor(sent, 1).astype(F32)
    sent = lax.dynamic_index_in_dim(both, 1 - chip, 0, False).astype(BF16)
    kept = lax.dynamic_index_in_dim(both, chip, 0, False)
    return kept + swap_tensor(sent, 2).astype(F32)


def gelu_parts(hidden):
    below = 0.5 * (1.0 + lax.erf(hidden * (0.5**0.5)))
    density = jnp.exp(-0.5 * hidden * hidden) * ((2.0 * jnp.pi) ** (-0.5))
    return hidden * below, below + hidden * density


def shards(
    inputs,
    lengths,
    ln1_gain,
    ln1_bias,
    ln2_gain,
    ln2_bias,
    w_qkv,
    b_qkv,
    w_dense,
    b_dense,
    w_fc1,
    b_fc1,
    w_fc2,
    b_fc2,
    out_grad,
):
    own_rows, width = inputs.shape
    tables = rotary_tables()
    gain_one, gain_two = ln1_gain.astype(F32), ln2_gain.astype(F32)

    def centred(rows):
        rows = rows.astype(F32)
        middle = rows - jnp.mean(rows, axis=-1, keepdims=True)
        spread = jnp.mean(middle * middle, axis=-1, keepdims=True)
        rate = lax.rsqrt(spread + EPS)
        return middle * rate, rate

    whole_in = gather_rows(inputs)
    xhat, _ = centred(whole_in)
    whole_one = (xhat * gain_one + ln1_bias.astype(F32)).astype(BF16)
    whole_two = (xhat * gain_two + ln2_bias.astype(F32)).astype(BF16)
    grad_rows = gather_rows(out_grad)

    hidden = dot_nn(whole_two, w_fc1) + b_fc1.astype(F32)
    active, slope = gelu_parts(hidden)
    active = active.astype(BF16)
    fc2_grad = dot_tn(active, grad_rows).astype(BF16)
    fc2_sum = lax.psum(fc2_grad, "dp")
    hidden_grad = (dot_nt(grad_rows, w_fc2) * slope).astype(BF16)
    fc1_grad = dot_tn(whole_two, hidden_grad).astype(BF16)
    fc1_grad, fc2_sum = lax.optimization_barrier((fc1_grad, fc2_sum))
    fc1_sum = lax.psum(fc1_grad, "dp")
    fc1_bias_grad = jnp.sum(hidden_grad, axis=0, dtype=F32)

    whole_one, fc1_grad = lax.optimization_barrier((whole_one, fc1_grad))
    packed = dot_nn(whole_one, w_qkv) + b_qkv.astype(F32)
    queries, key_rows, value_rows, context, lse = attend(packed, lengths, tables)
    context_grad = dot_nt(grad_rows, w_dense).astype(BF16)
    packed_grad = attend_back(queries, key_rows, value_rows, context_grad, lse, lengths, tables)
    dense_grad = dot_tn(context, grad_rows).astype(BF16)
    qkv_grad = dot_tn(whole_one, packed_grad).astype(BF16)
    dense_grad, qkv_grad, fc1_sum = lax.optimization_barrier((dense_grad, qkv_grad, fc1_sum))
    dense_sum, qkv_sum = lax.psum((dense_grad, qkv_grad), "dp")
    qkv_bias_grad = jnp.sum(packed_grad, axis=0, dtype=F32)

    branches = scatter_rows(dot_nn(context, w_dense) + dot_nn(active, w_fc2))
    outputs = inputs.astype(F32) + branches + (b_dense.astype(F32) + b_fc2.astype(F32))

    normed_two = scatter_rows(dot_nt(hidden_grad, w_fc1))
    normed_one = scatter_rows(dot_nt(packed_grad, w_qkv))
    own_hat, rate = centred(inputs)
    own_grad = out_grad.astype(F32)

    def norm_back(grad, gain):
        scaled = grad * gain
        return rate * (
            scaled
            - jnp.mean(scaled, axis=-1, keepdims=True)
            - own_hat * jnp.mean(scaled * own_hat, axis=-1, keepdims=True)
        )

    in_grad = own_grad + norm_back(normed_one, gain_one) + norm_back(normed_two, gain_two)
    shared = jnp.stack(
        [
            jnp.sum(normed_one * own_hat, axis=0),
            jnp.sum(normed_one, axis=0),
            jnp.sum(normed_two * own_hat, axis=0),
            jnp.sum(normed_two, axis=0),
            jnp.sum(own_grad, axis=0),
        ]
    ).reshape(-1)
    sliced = jnp.concatenate([qkv_bias_grad, fc1_bias_grad])
    place = lax.axis_index("tensor")
    slots = jnp.zeros((lax.axis_size("tensor"), sliced.shape[0]), F32)
    slots = lax.dynamic_update_slice_in_dim(slots, sliced[None], place, 0)
    sums = lax.psum(jnp.concatenate([shared, slots.reshape(-1)]), ("dp", "tensor"))
    vectors = sums[: shared.shape[0]].reshape(5, width)
    slots = sums[shared.shape[0] :].reshape(slots.shape)
    own_slot = lax.dynamic_index_in_dim(slots, place, 0, False)
    return (
        outputs.astype(BF16),
        in_grad,
        vectors[0],
        vectors[1],
        vectors[2],
        vectors[3],
        qkv_sum.astype(F32),
        own_slot[: b_qkv.shape[0]],
        dense_sum.astype(F32),
        vectors[4],
        fc1_sum.astype(F32),
        own_slot[b_qkv.shape[0] :],
        fc2_sum.astype(F32),
        vectors[4],
    )


def solution(mesh):
    rows = P(("dp", "tensor"), None)
    columns = P(None, "tensor")
    inner = P("tensor", None)
    split = P("tensor")
    return jax.shard_map(
        shards,
        mesh=mesh,
        in_specs=(
            rows,
            P("dp"),
            P(),
            P(),
            P(),
            P(),
            columns,
            split,
            inner,
            P(),
            columns,
            split,
            inner,
            P(),
            rows,
        ),
        out_specs=(
            rows,
            rows,
            P(),
            P(),
            P(),
            P(),
            columns,
            split,
            inner,
            P(),
            columns,
            split,
            inner,
            P(),
        ),
        check_vma=False,
    )
```

time: 1760 us -> 1300 us (0.74)
  matrix products: 489 us -> 241 us
  other arithmetic: 246 us -> 106 us
  blocking collectives: 80.3 us -> 0 us
  Pallas kernels: 0 us -> 75.9 us
  waiting for transfers between devices: 840 us -> 800 us
  local copies, waits for them, and re-layouts: 71.8 us -> 53.2 us
    dot_general x40 -> x12, matrix products: 489 us -> 241 us  [the longest x4 81.7 us: dot_nt(): lax.dot_general(left, right, (((1,), (1,)), ((), ())), preferred_element_...]
    reduce_scatter x2 -> x0, waiting for transfers between devices: 165 us -> none  [the longest x1 86.6 us: shards(): lax.psum_scatter(jnp.concatenate([times_transposed(packed_grad, w_qkv), t...]
    ppermute x0 -> x12, waiting for transfers between devices: none -> 150 us  [swap_tensor(): return lax.ppermute(values, 'tensor', [(t, t ^ bit) for t in range(count)])]
    psum x2 -> x0, blocking collectives: 80.3 us -> none  [the longest x1 40.6 us: shards(): lax.psum((gain_one, bias_one, gain_two, bias_two), ('dp', 'tensor'))]
    pallas_call x0 -> x2, Pallas kernels: none -> 75.9 us  [the longest x1 45.7 us: attend_back(): pl.pallas_call(attend_back_kernel, out_shape=jax.ShapeDtypeStruct((SEQ, h...]
    convert_element_type x24 -> x11, other arithmetic: 122 us -> 47.7 us  [the longest x1 12 us: shards(): fc1_sum.astype(F32)]
    all_gather x3 -> x0, waiting for transfers between devices: 52.4 us -> none  [the longest x1 52.4 us: shards(): lax.all_gather(normed_one.astype(jnp.bfloat16), 'tensor', axis=0, tiled=T...]
    psum x1 -> x4, waiting for transfers between devices: 621 us -> 650 us  [the longest x1 261 us: shards(): dense_sum, qkv_sum = lax.psum((dense_grad, qkv_grad), 'dp')]
  transfers between devices with their start and end apart: 6 -> 16, of which waited for: 4 -> 9; matrix products, arithmetic and copies ran while one was open for 35% -> 24% of each run, Pallas kernels for 0% -> 0%
where the time goes in v1:
time: 1300 us
  waiting for transfers between devices  800 us (62%)
  matrix products  241 us (19%)
  other arithmetic  106 us (8%)
  Pallas kernels  75.9 us (6%)
  local copies, waits for them, and re-layouts  53.2 us (4%)
  between operations  15.1 us (1%)
    psum x1, waiting for transfers between devices, shards(): dense_sum, qkv_sum = lax.psum((dense_grad, qkv_grad), 'dp')  261 us
    psum x1, waiting for transfers between devices, shards(): fc2_sum = lax.psum(fc2_grad, 'dp')  161 us
    ppermute x12, waiting for transfers between devices, swap_tensor(): return lax.ppermute(values, 'tensor', [(t, t ^ bit) for t in range(count)])  150 us
    psum x1, waiting for transfers between devices, shards(): lax.psum(jnp.concatenate([shared, slots.reshape(-1)]), ('dp', 'tensor'))  114 us
    psum x1, waiting for transfers between devices, shards(): fc1_sum = lax.psum(fc1_grad, 'dp')  114 us
    dot_general x4, matrix products, dot_nt(): lax.dot_general(left, right, (((1,), (1,)), ((), ())), preferred_element_...  81.7 us
    dot_general x4, matrix products, dot_nn(): lax.dot_general(left, right, (((1,), (0,)), ((), ())), preferred_element_...  81.3 us
    dot_general x4, matrix products, dot_tn(): lax.dot_general(left, right, (((0,), (0,)), ((), ())), preferred_element_...  78.2 us
  transfers between devices with their start and end apart: 16, of which 9 were waited for; matrix products, arithmetic and copies ran while one was open for 24% of the time, Pallas kernels for 0%

profile of v1, /device:TPU:0, one launch (start us, length us, event | category | flops | bytes accessed | tf_op | source)
XLA Modules:
  0.0 1298.1 jit_solution(15520028401235293074)
XLA Ops:
  17.5 39.5 %collective-permute-done.1 = bf16[512,2048]{1,0:T(8,128)(2,1)} collective-permute-done((bf16[512,2048]{1,0:T(8,128)(2,1)}, bf16[512,2048]{1,0:T(8,128)(2,1)}, u32[]{:S(2)}, u32[]{:S(2)}) %collective-permute-start.1) | collective-permute-done | bytes 2097184 | tf_op jit(solution)/shard_map/ppermute | solution.py:222
  73.3 27.9 %collective-permute-done.4 = bf16[512,2048]{1,0:T(8,128)(2,1)} collective-permute-done((bf16[512,2048]{1,0:T(8,128)(2,1)}, bf16[512,2048]{1,0:T(8,128)(2,1)}, u32[]{:S(2)}, u32[]{:S(2)}) %collective-permute-start.4) | collective-permute-done | bytes 2097184 | tf_op jit(solution)/shard_map/ppermute | solution.py:222
  113.1 26.4 %multiply_convert_fusion = (bf16[2048,2048]{1,0:T(8,128)(2,1)}, f32[2048,2048]{1,0:T(8,128)}) fusion(f32[2048]{0:T(1024)} %convert_element_type.161, bf16[2048,2048]{1,0:T(8,128)(2,1)} %param.25, bf16[2048,2048]{1,0:T(8,128)(2,1)S(1)} %constant_dynamic-update-slice_fusion.4, f32[2048]{0:T(1024)S(1)} %convert_element_type.159, ...), kind=kOutput, calls=%fused_computation.19 | convolution fusion | flops 17230200832 | bytes 41984000 | tf_op jit(solution)/shard_map/dot_general | solution.py:20
  143.1 22.1 %convolution_convert_fusion = bf16[2048,2048]{1,0:T(8,128)(2,1)} fusion(bf16[2048,2048]{1,0:T(8,128)(2,1)} %get-tuple-element.63, bf16[2048,2048]{1,0:T(8,128)(2,1)S(1)} %constant_dynamic-update-slice_fusion), kind=kOutput, calls=%fused_computation.30 | convolution fusion | flops 17184063488 | bytes 25165824 | tf_op jit(solution)/shard_map/dot_general | solution.py:28
  165.8 32.2 %convert_reduce_fusion.1 = (f32[2048]{0:T(1024)}, bf16[2048,2048]{1,0:T(8,128)(2,1)}) fusion(f32[2048,2048]{1,0:T(8,128)} %get-tuple-element.64, f32[2048]{0:T(1024)S(1)} %copy-done.22, bf16[2048,2048]{1,0:T(8,128)(2,1)} %copy-done.7, bf16[2048,2048]{1,0:T(8,128)(2,1)} %param.27), kind=kOutput, calls=%fused_computation.18 | convolution fusion | flops 17234393088 | bytes 41959424 | tf_op jit(solution)/shard_map/dot_general | solution.py:24
  198.1 24.6 %fusion.52 = f32[2048,2048]{1,0:T(8,128)} fusion(bf16[2048,2048]{1,0:T(8,128)(2,1)} %get-tuple-element.66, bf16[2048,2048]{1,0:T(8,128)(2,1)} %param.25), kind=kOutput, calls=%fused_computation.110 | convolution fusion | flops 17179869184 | bytes 33554432 | tf_op jit(solution)/shard_map/dot_general | solution.py:24
  222.7 6.3 fusion.37
  229.4 6.2 convolution_convert_fusion.4.grad_ref
  241.1 25.3 %convolution_convert_fusion.1 = bf16[2048,2048]{1,0:T(8,128)(2,1)} fusion(bf16[2048,2048]{1,0:T(8,128)(2,1)} %get-tuple-element.66, bf16[2048,2048]{1,0:T(8,128)(2,1)S(1)} %bitcast.72, f32[2048]{0:T(1024)S(1)} %convert_element_type.159, f32[2048]{0:T(1024)S(1)} %convert_element_type.158, f32[2048]{0:T(1024)S(1)} %add_rsqrt_fusion, ...), kind=kOutput, calls=%fused_computation.31 | convolution fusion | flops 17209229312 | bytes 25198592 | tf_op jit(solution)/shard_map/dot_general | solution.py:28
  266.4 10.1 bitcast_add_fusion
  276.5 160.9 %all-reduce.6.cloned.1.call-done = bf16[2048,2048]{1,0:T(8,128)(2,1)} async-done(((bf16[2048,2048]{1,0:T(8,128)(2,1)}), bf16[2048,2048]{1,0:T(8,128)(2,1)}) %all-reduce.6.cloned.1.call-update) | async-done | bytes 8388624 | tf_op jit(solution)/shard_map/psum | solution.py:299
  437.4 19.6 %convolution_add_fusion.packed_ref = f32[2048,1536]{1,0:T(8,128)} fusion(bf16[2048,2048]{1,0:T(8,128)(2,1)} %fusion.5, bf16[2048,1536]{1,0:T(8,128)(2,1)} %param.21, f32[1536]{0:T(1024)S(1)} %copy-done.21), kind=kOutput, calls=%fused_computation.22 | convolution fusion | flops 12888047616 | bytes 27269120 | tf_op jit(solution)/shard_map/dot_general | solution.py:20
  457.0 30.2 %attend.1 = (bf16[2048,512]{1,0:T(8,128)(2,1)}, bf16[2048,512]{1,0:T(8,128)(2,1)}, bf16[2048,512]{1,0:T(8,128)(2,1)}, bf16[2048,512]{1,0:T(8,128)(2,1)}, f32[4,1,2048]{2,1,0:T(1,128)}) custom-call(s32[1]{0:T(128)S(6)} %copy.50.length_ref, f32[2048,1536]{1,0:T(8,128)} %convolution_add_fusion.packed_ref, f32[2048,128]{1,0:T(8,128)} %get-tuple-element.62.cos_ref, ...), custom_call_target="tpu_custom_call" | custom-call | flops 4294967296 | bytes 20971520 | tf_op jit(solution)/shard_map/attend/pallas_call | solution.py:109
  487.2 45.7 %attend_back.1 = bf16[2048,1536]{1,0:T(8,128)(2,1)} custom-call(s32[1]{0:T(128)S(6)} %copy.50.length_ref, bf16[2048,512]{1,0:T(8,128)(2,1)} %get-tuple-element.28.q_ref, bf16[2048,512]{1,0:T(8,128)(2,1)} %get-tuple-element.29.k_ref, bf16[2048,512]{1,0:T(8,128)(2,1)} %get-tuple-element.30.v_ref, bf16[2048,512]{1,0:T(8,128)(2,1)} %convolution_convert_fusion.4.grad_ref, ...), custom_call_target="tpu_custom_call" | custom-call | flops 10737418240 | bytes 14680064 | tf_op jit(solution)/shard_map/attend_back/pallas_call | solution.py:196
  532.9 18.6 %fusion.51 = f32[2048,2048]{1,0:T(8,128)S(1)} fusion(bf16[2048,1536]{1,0:T(8,128)(2,1)} %attend_back.1, bf16[2048,1536]{1,0:T(8,128)(2,1)} %param.21), kind=kOutput, calls=%fused_computation.109 | convolution fusion | flops 12884901888 | bytes 29360128 | tf_op jit(solution)/shard_map/dot_general | solution.py:24
  551.6 6.3 copy-done.6
  560.5 8.6 fusion.50
  569.2 26.7 %convolution_add_fusion.1 = f32[2048,2048]{1,0:T(8,128)} fusion(f32[2048,2048]{1,0:T(8,128)} %fusion.50, bf16[2048,2048]{1,0:T(8,128)(2,1)} %get-tuple-element.63, bf16[2048,2048]{1,0:T(8,128)(2,1)} %param.27), kind=kOutput, calls=%fused_computation.23 | convolution fusion | flops 17184063488 | bytes 50331648 | tf_op jit(solution)/shard_map/dot_general | solution.py:20
  607.8 6.9 bitcast_add_fusion.1
  616.6 20.9 %convolution_convert_fusion.2 = bf16[2048,1536]{1,0:T(8,128)(2,1)} fusion(bf16[2048,2048]{1,0:T(8,128)(2,1)} %fusion.5, bf16[2048,1536]{1,0:T(8,128)(2,1)} %attend_back.1), kind=kOutput, calls=%fused_computation.32 | convolution fusion | flops 12888047616 | bytes 20971520 | tf_op jit(solution)/shard_map/dot_general | solution.py:28
  637.5 6.1 bitcast_add_fusion.2
  655.0 44.9 %collective-permute-done.9 = bf16[512,2048]{1,0:T(8,128)(2,1)} collective-permute-done((bf16[512,2048]{1,0:T(8,128)(2,1)}, bf16[512,2048]{1,0:T(8,128)(2,1)}, u32[]{:S(2)}, u32[]{:S(2)}) %collective-permute-start.9) | collective-permute-done | bytes 2097184 | tf_op jit(solution)/shard_map/ppermute | solution.py:222
  700.0 7.8 fusion.30
  707.9 36.1 %collective-permute-done.7 = bf16[512,2048]{1,0:T(8,128)(2,1)} collective-permute-done((bf16[512,2048]{1,0:T(8,128)(2,1)}, bf16[512,2048]{1,0:T(8,128)(2,1)}, u32[]{:S(2)}, u32[]{:S(2)}) %collective-permute-start.7) | collective-permute-done | bytes 2097184 | tf_op jit(solution)/shard_map/ppermute | solution.py:222
  744.0 7.8 convert_reduce_fusion.4
  752.8 9.9 convolution_convert_fusion.3
  762.7 113.7 %all-reduce.10.cloned.1.call-done = bf16[2048,2048]{1,0:T(8,128)(2,1)} async-done(((bf16[2048,2048]{1,0:T(8,128)(2,1)}), bf16[2048,2048]{1,0:T(8,128)(2,1)}) %all-reduce.10.cloned.1.call-update) | async-done | bytes 8388624 | tf_op jit(solution)/shard_map/psum | solution.py:303
  876.4 11.7 convert_element_type.198
  888.1 114.1 %all-reduce.8.cloned.1.call-done = f32[24576]{0:T(1024)} async-done(((f32[24576]{0:T(1024)}), f32[24576]{0:T(1024)}) %all-reduce.8.cloned.1.call-update) | async-done | bytes 98320 | tf_op jit(solution)/shard_map/psum | solution.py:347
  1005.8 12.0 convert_element_type.197
  1017.8 260.9 %all-reduce.12.cloned.1.call-done = (bf16[2048,1536]{1,0:T(8,128)(2,1)}, bf16[512,2048]{1,0:T(8,128)(2,1)}) async-done(((bf16[2048,1536]{1,0:T(8,128)(2,1)}, bf16[512,2048]{1,0:T(8,128)(2,1)}), (bf16[2048,1536]{1,0:T(8,128)(2,1)}, bf16[512,2048]{1,0:T(8,128)(2,1)})) %all-reduce.12.cloned.1.call-update) | async-done | bytes 8388624 | tf_op jit(solution)/shard_map/psum | solution.py:314
  1278.7 9.5 convert_element_type.195
  (141 shorter events, 83.4 us)
Async XLA Ops:
  7.2 222.2 %copy-start = (bf16[512,2048]{1,0:T(8,128)(2,1)S(1)}, bf16[512,2048]{1,0:T(8,128)(2,1)}, u32[]{:S(2)}) copy-start(bf16[512,2048]{1,0:T(8,128)(2,1)} %param.23) | copy-start | bytes 6291460
  7.2 430.2 %all-reduce.6.cloned.1.call-start = ((), (), s32[]{:S(2)}) async-start(), calls=%async_computation | async-start | bytes 16777216 | tf_op jit(solution)/shard_map/psum | solution.py:299
  7.2 49.8 %collective-permute-start.1 = (bf16[512,2048]{1,0:T(8,128)(2,1)}, bf16[512,2048]{1,0:T(8,128)(2,1)}, u32[]{:S(2)}, u32[]{:S(2)}) collective-permute-start(bf16[512,2048]{1,0:T(8,128)(2,1)} %param.15), channel_id=1, source_target_pairs={{0,2},{1,3},{2,0},{3,1},{4,6},{5,7},{6,4},{7,5},{8,10},{9,11},{10,... | collective-permute-start | bytes 6291464 | tf_op jit(solution)/shard_map/ppermute | solution.py:222
  10.2 90.9 %collective-permute-start.3 = (bf16[512,2048]{1,0:T(8,128)(2,1)}, bf16[512,2048]{1,0:T(8,128)(2,1)}, u32[]{:S(2)}, u32[]{:S(2)}) collective-permute-start(bf16[512,2048]{1,0:T(8,128)(2,1)} %param.29), channel_id=1, source_target_pairs={{0,1},{1,0},{2,3},{3,2},{4,5},{5,4},{6,7},{7,6},{8,9},{9,8},{10,11... | collective-permute-start | bytes 6291464 | tf_op jit(solution)/shard_map/ppermute | solution.py:222
  10.2 90.9 %collective-permute-start.4 = (bf16[512,2048]{1,0:T(8,128)(2,1)}, bf16[512,2048]{1,0:T(8,128)(2,1)}, u32[]{:S(2)}, u32[]{:S(2)}) collective-permute-start(bf16[512,2048]{1,0:T(8,128)(2,1)} %param.29), channel_id=1, source_target_pairs={{0,2},{1,3},{2,0},{3,1},{4,6},{5,7},{6,4},{7,5},{8,10},{9,11},{10,... | collective-permute-start | bytes 6291464 | tf_op jit(solution)/shard_map/ppermute | solution.py:222
  10.4 92.6 %collective-permute-start = (bf16[512,2048]{1,0:T(8,128)(2,1)}, bf16[512,2048]{1,0:T(8,128)(2,1)}, u32[]{:S(2)}, u32[]{:S(2)}) collective-permute-start(bf16[512,2048]{1,0:T(8,128)(2,1)} %param.15), channel_id=1, source_target_pairs={{0,1},{1,0},{2,3},{3,2},{4,5},{5,4},{6,7},{7,6},{8,9},{9,8},{10,11... | collective-permute-start | bytes 6291464 | tf_op jit(solution)/shard_map/ppermute | solution.py:222
  57.0 50.7 %collective-permute-start.2 = (bf16[512,2048]{1,0:T(8,128)(2,1)}, bf16[512,2048]{1,0:T(8,128)(2,1)}, u32[]{:S(2)}, u32[]{:S(2)}) collective-permute-start(bf16[512,2048]{1,0:T(8,128)(2,1)} %collective-permute-done.1), channel_id=1, source_target_pairs={{0,1},{1,0},{2,3},{3,2},{4,5},{5,4},{6,7},{7,6},{8,9},{9,8},{10,11... | collective-permute-start | bytes 6291464 | tf_op jit(solution)/shard_map/ppermute | solution.py:222
  59.0 182.1 %copy-start.13 = (f32[2048]{0:T(1024)}, f32[2048]{0:T(1024)S(1)}, u32[]{:S(2)}) copy-start(f32[2048]{0:T(1024)S(1)} %convert_element_type.158) | copy-start | bytes 24580
  101.1 38.4 %collective-permute-start.5 = (bf16[512,2048]{1,0:T(8,128)(2,1)}, bf16[512,2048]{1,0:T(8,128)(2,1)S(1)}, u32[]{:S(2)}, u32[]{:S(2)}) collective-permute-start(bf16[512,2048]{1,0:T(8,128)(2,1)} %collective-permute-done.4), channel_id=1, source_target_pairs={{0,1},{1,0},{2,3},{3,2},{4,5},{5,4},{6,7},{7,6},{8,9},{9,8},{10,11... | collective-permute-start | bytes 6291464 | tf_op jit(solution)/shard_map/ppermute | solution.py:222
  165.2 711.3 %all-reduce.10.cloned.1.call-start = ((), (), s32[]{:S(2)}) async-start(), calls=%async_computation.2 | async-start | bytes 16777216 | tf_op jit(solution)/shard_map/psum | solution.py:303
  165.8 63.6 %slice-start.2 = ((s8[8388608]{0:T(1024)(128)(4,1)}), s8[4194304]{0:T(1024)(128)(4,1)S(1)}, s32[]{:S(2)}) async-start(s8[8388608]{0:T(1024)(128)(4,1)} %bitcast.79), calls=%async_computation.6 | async-start | bytes 8388608
  198.1 31.3 %slice-start.3 = ((s8[8388608]{0:T(1024)(128)(4,1)}), s8[4194304]{0:T(1024)(128)(4,1)S(1)}, s32[]{:S(2)}) async-start(s8[8388608]{0:T(1024)(128)(4,1)} %bitcast.79), calls=%async_computation.7 | async-start | bytes 8388608
  222.7 13.0 slice-start
  229.0 37.4 %collective-permute-start.10 = (bf16[2,512,2048]{2,1,0:T(8,128)(2,1)}, bf16[2,512,2048]{2,1,0:T(8,128)(2,1)}, u32[]{:S(2)}, u32[]{:S(2)}) collective-permute-start(bf16[2,512,2048]{2,1,0:T(8,128)(2,1)} %fusion.37), channel_id=1, source_target_pairs={{0,1},{1,0},{2,3},{3,2},{4,5},{5,4},{6,7},{7,6},{8,9},{9,8},{10,11... | collective-permute-start | bytes 12582920 | tf_op jit(solution)/shard_map/ppermute | solution.py:222
  266.4 171.0 %copy-start.21 = (f32[1536]{0:T(1024)S(1)}, f32[1536]{0:T(1024)}, u32[]{:S(2)}) copy-start(f32[1536]{0:T(1024)} %convert_element_type.166) | copy-start | bytes 18436
  560.5 47.3 %collective-permute-start.8 = (bf16[2,512,2048]{2,1,0:T(8,128)(2,1)}, bf16[2,512,2048]{2,1,0:T(8,128)(2,1)}, u32[]{:S(2)}, u32[]{:S(2)}) collective-permute-start(bf16[2,512,2048]{2,1,0:T(8,128)(2,1)} %fusion.36), channel_id=1, source_target_pairs={{0,1},{1,0},{2,3},{3,2},{4,5},{5,4},{6,7},{7,6},{8,9},{9,8},{10,11... | collective-permute-start | bytes 12582920 | tf_op jit(solution)/shard_map/ppermute | solution.py:222
  601.9 35.6 %collective-permute-start.6 = (bf16[2,512,2048]{2,1,0:T(8,128)(2,1)}, bf16[2,512,2048]{2,1,0:T(8,128)(2,1)}, u32[]{:S(2)}, u32[]{:S(2)}) collective-permute-start(bf16[2,512,2048]{2,1,0:T(8,128)(2,1)} %fusion.35), channel_id=1, source_target_pairs={{0,1},{1,0},{2,3},{3,2},{4,5},{5,4},{6,7},{7,6},{8,9},{9,8},{10,11... | collective-permute-start | bytes 12582920 | tf_op jit(solution)/shard_map/ppermute | solution.py:222
  606.2 48.8 %collective-permute-start.11 = (bf16[512,2048]{1,0:T(8,128)(2,1)}, bf16[512,2048]{1,0:T(8,128)(2,1)}, u32[]{:S(2)}, u32[]{:S(2)}) collective-permute-start(bf16[512,2048]{1,0:T(8,128)(2,1)} %fusion.40), channel_id=1, source_target_pairs={{0,2},{1,3},{2,0},{3,1},{4,6},{5,7},{6,4},{7,5},{8,10},{9,11},{10,... | collective-permute-start | bytes 6291464 | tf_op jit(solution)/shard_map/ppermute | solution.py:222
  607.7 394.5 %all-reduce.8.cloned.1.call-start = ((), (), s32[]{:S(2)}) async-start(), calls=%async_computation.1 | async-start | bytes 196608 | tf_op jit(solution)/shard_map/psum | solution.py:347
  614.7 22.8 %copy-start.5 = (f32[2,512,2048]{2,1,0:T(8,128)}, f32[2,512,2048]{2,1,0:T(8,128)S(1)}, u32[]{:S(2)}) copy-start(f32[2,512,2048]{2,1,0:T(8,128)S(1)} %bitcast_add_fusion.1) | copy-start | bytes 25165828
  616.6 83.4 %collective-permute-start.9 = (bf16[512,2048]{1,0:T(8,128)(2,1)}, bf16[512,2048]{1,0:T(8,128)(2,1)}, u32[]{:S(2)}, u32[]{:S(2)}) collective-permute-start(bf16[512,2048]{1,0:T(8,128)(2,1)} %fusion.39), channel_id=1, source_target_pairs={{0,2},{1,3},{2,0},{3,1},{4,6},{5,7},{6,4},{7,5},{8,10},{9,11},{10,... | collective-permute-start | bytes 6291464 | tf_op jit(solution)/shard_map/ppermute | solution.py:222
  646.9 53.0 %copy-start.12 = (f32[2048]{0:T(1024)S(1)}, f32[2048]{0:T(1024)}, u32[]{:S(2)}) copy-start(f32[2048]{0:T(1024)} %convert_element_type.155) | copy-start | bytes 24580
  646.9 53.0 %copy-start.14 = (f32[2048]{0:T(1024)S(1)}, f32[2048]{0:T(1024)}, u32[]{:S(2)}) copy-start(f32[2048]{0:T(1024)} %copy-done.13) | copy-start | bytes 24580
  646.9 53.0 %copy-start.19 = (f32[512]{0:T(512)S(1)}, f32[512]{0:T(512)}, u32[]{:S(2)}) copy-start(f32[512]{0:T(512)} %copy-done.18) | copy-start | bytes 6148
  647.0 53.0 %copy-start.20 = (f32[512]{0:T(512)S(1)}, f32[512]{0:T(512)}, u32[]{:S(2)}) copy-start(f32[512]{0:T(512)} %add_rsqrt_fusion.1) | copy-start | bytes 6148
  648.6 95.4 %collective-permute-start.7 = (bf16[512,2048]{1,0:T(8,128)(2,1)}, bf16[512,2048]{1,0:T(8,128)(2,1)}, u32[]{:S(2)}, u32[]{:S(2)}) collective-permute-start(bf16[512,2048]{1,0:T(8,128)(2,1)} %fusion.38), channel_id=1, source_target_pairs={{0,2},{1,3},{2,0},{3,1},{4,6},{5,7},{6,4},{7,5},{8,10},{9,11},{10,... | collective-permute-start | bytes 6291464 | tf_op jit(solution)/shard_map/ppermute | solution.py:222
  653.5 90.5 %copy-start.3 = (bf16[512,2048]{1,0:T(8,128)(2,1)S(1)}, bf16[512,2048]{1,0:T(8,128)(2,1)}, u32[]{:S(2)}) copy-start(bf16[512,2048]{1,0:T(8,128)(2,1)} %param.15) | copy-start | bytes 6291460
  653.5 90.4 %copy-start.9 = (bf16[512,2048]{1,0:T(8,128)(2,1)S(1)}, bf16[512,2048]{1,0:T(8,128)(2,1)}, u32[]{:S(2)}) copy-start(bf16[512,2048]{1,0:T(8,128)(2,1)} %param.29) | copy-start | bytes 6291460
  653.5 90.4 %copy-start.15 = (f32[2048]{0:T(1024)S(1)}, f32[2048]{0:T(1024)}, u32[]{:S(2)}) copy-start(f32[2048]{0:T(1024)} %convert_add_fusion.2) | copy-start | bytes 24580
  752.5 526.2 %all-reduce.12.cloned.1.call-start = ((), (), s32[]{:S(2)}) async-start(), calls=%async_computation.3 | async-start | bytes 16777216 | tf_op jit(solution)/shard_map/psum | solution.py:314
  1004.5 286.3 %copy-start.17 = (f32[2048]{0:T(1024)}, f32[2048]{0:T(1024)S(1)}, u32[]{:S(2)}) copy-start(f32[2048]{0:T(1024)S(1)} %get-tuple-element.98) | copy-start | bytes 24580
  1278.7 9.5 copy-start.10
  (13 other events, 56.2 us)
Sparse Core Ops, SparseCore 0:
  165.3 272.0 all-reduce.5
  607.8 268.5 all-reduce.9
  882.6 119.6 all-reduce.7
  1006.8 271.9 all-reduce.11

commit v2 on v1

--- a/solution.py
+++ b/solution.py
@@ -5,6 +5,7 @@
 from jax import lax
 from jax.experimental import pallas as pl
 from jax.experimental.pallas import tpu as pltpu
+from jax.sharding import Mesh
 from jax.sharding import PartitionSpec as P
 
 HD = 128
@@ -26,6 +27,73 @@
 
 def dot_tn(left, right):
     return lax.dot_general(left, right, (((0,), (0,)), ((), ())), preferred_element_type=F32)
+
+
+FORMS = {"nn": (1, 0), "nt": (1, 1), "tn": (0, 0)}
+
+
+def matmul(form, pairs, kind, block, first=None, rows=None, extras=(), finish=None, chunk=None, name=None):
+    sides = FORMS[form]
+    height = pairs[0][0].shape[1 - sides[0]]
+    rows = height if rows is None else rows
+    block = min(block, rows)
+    width = pairs[0][1].shape[1 - sides[1]]
+    dims = (((sides[0],), (sides[1],)), ((), ()))
+    count = len(pairs)
+    chunk = width if chunk is None else min(chunk, width)
+
+    def kernel(first_ref, *refs):
+        for start in range(0, width, chunk):
+            part = slice(start, start + chunk)
+            rest = [ref[:, part] for ref in refs[2 * count : -1]]
+            total = None
+            for number in range(count):
+                right = refs[2 * number + 1]
+                product = lax.dot_general(
+                    refs[2 * number][...],
+                    right[part, :] if form == "nt" else right[:, part],
+                    dims,
+                    preferred_element_type=F32,
+                )
+                total = product if total is None else total + product
+            if finish is not None:
+                total = finish(total, *rest)
+            refs[-1][:, part] = total.astype(kind)
+
+    specs, flat = [], []
+    for left, right in pairs:
+        if form == "tn":
+            specs.append(pl.BlockSpec((left.shape[0], block), lambda i, b: (0, b[0] + i)))
+        else:
+            specs.append(pl.BlockSpec((block, left.shape[1]), lambda i, b: (b[0] + i, 0)))
+        specs.append(
+            pl.BlockSpec(right.shape, lambda i, b: (0, 0), pipeline_mode=pl.Buffered(1))
+        )
+        flat.extend([left, right])
+    for extra in extras:
+        if extra.shape[0] == 1:
+            specs.append(pl.BlockSpec(extra.shape, lambda i, b: (0, 0)))
+        else:
+            specs.append(pl.BlockSpec((block, width), lambda i, b: (b[0] + i, 0)))
+        flat.append(extra)
+    if first is None:
+        first = jnp.zeros((), jnp.int32)
+    inner = sum(left.shape[sides[0]] for left, _ in pairs)
+    return pl.pallas_call(
+        kernel,
+        out_shape=jax.ShapeDtypeStruct((rows, width), kind),
+        grid_spec=pltpu.PrefetchScalarGridSpec(
+            num_scalar_prefetch=1,
+            grid=(rows // block,),
+            in_specs=specs,
+            out_specs=pl.BlockSpec((block, width), lambda i, b: (i, 0)),
+        ),
+        compiler_params=pltpu.CompilerParams(vmem_limit_bytes=56 << 20),
+        cost_estimate=pl.CostEstimate(
+            flops=rows * width * inner // 8, transcendentals=0, bytes_accessed=rows * width
+        ),
+        name=name,
+    )(first[None], *flat)
 
 
 def rotary_tables():
@@ -51,17 +119,22 @@
     return lax.broadcasted_iota(jnp.int32, shape, 0) <= lax.broadcasted_iota(jnp.int32, shape, 1)
 
 
+def local_rows(index, place):
+    return pl.ds(pl.multiple_of(lax.bitwise_xor(index, place) * BLOCK, BLOCK), BLOCK)
+
+
 def attend_kernel(
     length_ref, packed_ref, cos_ref, low_ref, high_ref, q_ref, k_ref, v_ref, ctx_ref, lse_ref, vt_ref
 ):
-    length = length_ref[0]
+    length, place = length_ref[0], length_ref[1]
     scale = HD ** (-0.5)
     for index in range(SEQ // BLOCK):
         rows = pl.ds(index * BLOCK, BLOCK)
+        outside = local_rows(index, place)
         cos_rows, low_rows, high_rows = cos_ref[rows, :], low_ref[rows, :], high_ref[rows, :]
-        raw_query = packed_ref[rows, 0:HD]
-        raw_key = packed_ref[rows, HD : 2 * HD]
-        value = packed_ref[rows, 2 * HD : 3 * HD]
+        raw_query = packed_ref[outside, 0:HD]
+        raw_key = packed_ref[outside, HD : 2 * HD]
+        value = packed_ref[outside, 2 * HD : 3 * HD]
         query = (raw_query * cos_rows + shifted_mix(raw_query, low_rows, high_rows)) * scale
         q_ref[rows, :] = query.astype(BF16)
         key = raw_key * cos_rows + shifted_mix(raw_key, low_rows, high_rows)
@@ -71,9 +144,10 @@
     for index in range(SEQ // BLOCK):
         before = index * BLOCK
         rows = pl.ds(before, BLOCK)
+        outside = local_rows(index, place)
 
         @pl.when(before < length)
-        def _(before=before, rows=rows):
+        def _(before=before, rows=rows, outside=outside):
             query = q_ref[rows, :]
             near = jnp.where(diagonal((BLOCK, BLOCK)), dot_nt(k_ref[rows, :], query), -1e30)
             highest = jnp.max(near, axis=0, keepdims=True)
@@ -91,12 +165,12 @@
                 turned = turned + dot_nn(vt_ref[:, 0:before], (far * inverse).astype(BF16))
             context = jnp.transpose(turned)
             places = before + lax.broadcasted_iota(jnp.int32, (BLOCK, HD), 0)
-            ctx_ref[rows, :] = jnp.where(places < length, context, 0.0).astype(BF16)
+            ctx_ref[outside, :] = jnp.where(places < length, context, 0.0).astype(BF16)
             lse_ref[0, :, rows] = highest + jnp.log(totals)
 
         @pl.when(before >= length)
-        def _(rows=rows):
-            ctx_ref[rows, :] = jnp.zeros((BLOCK, HD), BF16)
+        def _(rows=rows, outside=outside):
+            ctx_ref[outside, :] = jnp.zeros((BLOCK, HD), BF16)
             lse_ref[0, :, rows] = jnp.zeros((1, BLOCK), F32)
 
 
@@ -139,7 +213,7 @@
     dk_ref,
     dv_ref,
 ):
-    length = length_ref[0]
+    length, place = length_ref[0], length_ref[1]
     scale = HD ** (-0.5)
     kt_ref[...] = jnp.transpose(k_ref[...].astype(F32)).astype(BF16)
     dk_ref[...] = jnp.zeros_like(dk_ref)
@@ -151,12 +225,13 @@
     for index in range(SEQ // BLOCK):
         before = index * BLOCK
         rows = pl.ds(before, BLOCK)
+        outside = local_rows(index, place)
 
         @pl.when(before < length)
-        def _(before=before, rows=rows):
+        def _(before=before, rows=rows, outside=outside):
             query = q_ref[rows, :]
             places = before + lax.broadcasted_iota(jnp.int32, (BLOCK, HD), 0)
-            grad = jnp.where(places < length, grad_ref[rows, :].astype(F32), 0.0).astype(BF16)
+            grad = jnp.where(places < length, grad_ref[outside, :].astype(F32), 0.0).astype(BF16)
             lse = lse_ref[0, :, rows]
             parts = [rows] + ([pl.ds(0, before)] if before else [])
             probs, grads = [], []
@@ -176,16 +251,17 @@
                 dv_ref[keys, :] += dot_nn(prob.astype(BF16), grad)
                 dk_ref[keys, :] += dot_nn(score_grad, query)
                 turned = turned + dot_nn(kt_ref[:, keys], score_grad)
-            out_ref[rows, 0:HD] = unturn(rows, jnp.transpose(turned) * scale).astype(BF16)
+            out_ref[outside, 0:HD] = unturn(rows, jnp.transpose(turned) * scale).astype(BF16)
 
         @pl.when(before >= length)
-        def _(rows=rows):
-            out_ref[rows, 0:HD] = jnp.zeros((BLOCK, HD), BF16)
+        def _(outside=outside):
+            out_ref[outside, 0:HD] = jnp.zeros((BLOCK, HD), BF16)
 
     for index in range(SEQ // BLOCK):
         rows = pl.ds(index * BLOCK, BLOCK)
-        out_ref[rows, HD : 2 * HD] = unturn(rows, dk_ref[rows, :]).astype(BF16)
-        out_ref[rows, 2 * HD : 3 * HD] = dv_ref[rows, :].astype(BF16)
+        outside = local_rows(index, place)
+        out_ref[outside, HD : 2 * HD] = unturn(rows, dk_ref[rows, :]).astype(BF16)
+        out_ref[outside, 2 * HD : 3 * HD] = dv_ref[rows, :].astype(BF16)
 
 
 def attend_back(queries, key_rows, value_rows, grad, lse, length, tables):
@@ -217,39 +293,184 @@
     )(length, queries, key_rows, value_rows, grad, lse, *tables)
 
 
+def hold(*values):
+    return lax.optimization_barrier(values)
+
+
 def swap_tensor(values, bit):
     count = lax.axis_size("tensor")
     return lax.ppermute(values, "tensor", [(t, t ^ bit) for t in range(count)])
 
 
-def gather_rows(block):
+def block_mask():
+    return lax.axis_index("tensor") if lax.axis_size("tensor") == 4 else jnp.int32(0)
+
+
+def gather_near(block):
     if lax.axis_size("tensor") != 4:
-        return lax.all_gather(block, "tensor", axis=0, tiled=True)
-    place = lax.axis_index("tensor")
-    far = swap_tensor(block, 2)
-    mate = swap_tensor(block, 1)
-    far_mate = swap_tensor(far, 1)
-    rows = block.shape[0]
-    whole = jnp.zeros((4 * rows, block.shape[1]), block.dtype)
-    for bits, part in ((0, block), (1, mate), (2, far), (3, far_mate)):
-        whole = lax.dynamic_update_slice_in_dim(whole, part, (place ^ bits) * rows, 0)
-    return whole
-
-
-def scatter_rows(partial_rows):
+        return lax.all_gather(block, "tensor", axis=0, tiled=True), None
+    return jnp.concatenate([block, swap_tensor(block, 1)]), swap_tensor(block, 2)
+
+
+def gather_far(near, far):
+    if far is None:
+        return near
+    return jnp.concatenate([near, far, swap_tensor(far, 1)])
+
+
+def scatter_stages(partial_rows):
     if lax.axis_size("tensor") != 4:
-        return lax.psum_scatter(
+        total = lax.psum_scatter(
             partial_rows.astype(BF16), "tensor", scatter_dimension=0, tiled=True
-        ).astype(F32)
-    place = lax.axis_index("tensor")
-    chip, core = place // 2, place % 2
-    blocks = partial_rows.reshape(2, 2, -1, partial_rows.shape[1])
-    kept = lax.dynamic_index_in_dim(blocks, core, 1, False).astype(F32)
-    sent = lax.dynamic_index_in_dim(blocks, 1 - core, 1, False).astype(BF16)
-    both = kept + swap_tensor(sent, 1).astype(F32)
-    sent = lax.dynamic_index_in_dim(both, 1 - chip, 0, False).astype(BF16)
-    kept = lax.dynamic_index_in_dim(both, chip, 0, False)
-    return kept + swap_tensor(sent, 2).astype(F32)
+        )
+        yield (total,)
+        yield (total,)
+        return total.astype(F32)
+    own, mate, far, far_mate = jnp.split(partial_rows, 4)
+    sent = jnp.concatenate([mate, far_mate]).astype(BF16)
+    own, far, got = yield own.astype(F32), far.astype(F32), swap_tensor(sent, 1)
+    rows = own.shape[0]
+    own, far = own + got[:rows].astype(F32), far + got[rows:].astype(F32)
+    own, got = yield own, swap_tensor(far.astype(BF16), 2)
+    return own + got.astype(F32)
+
+
+def add_rows(left, right):
+    return (left.astype(F32) + right.astype(F32)).astype(left.dtype)
+
+
+def move_z(values, pairs):
+    return lax.ppermute(values, "z", pairs)
+
+
+INWARD = ((0, 1), (3, 2))
+MIDDLE = ((1, 2), (2, 1))
+OUTWARD = ((1, 0), (2, 3))
+
+
+def on_edge():
+    z = lax.axis_index("z")
+    return (z == 0) | (z == 3)
+
+
+def sum_line(values):
+    values = add_rows(values, move_z(values, INWARD))
+    values = add_rows(values, move_z(values, MIDDLE))
+    return jnp.where(on_edge(), move_z(values, OUTWARD), values)
+
+
+PAIRS = ((0, 1), (1, 0))
+
+
+def line_stages(kept, sent):
+    if lax.axis_size("z") != 4:
+        for _ in range(5):
+            kept, sent = yield kept, sent
+        return lax.psum(kept, ("z", "y")), lax.psum(sent, ("z", "y"))
+    kept, got = yield kept, lax.ppermute(sent, "y", PAIRS)
+    kept = add_rows(kept, got)
+    kept, got = yield kept, move_z(kept, INWARD)
+    kept = add_rows(kept, got)
+    kept, got = yield kept, move_z(kept, MIDDLE)
+    kept = add_rows(kept, got)
+    kept, got = yield kept, move_z(kept, OUTWARD)
+    kept = jnp.where(on_edge(), got, kept)
+    kept, got = yield kept, lax.ppermute(kept, "y", PAIRS)
+    return kept, got
+
+
+def whole_rows(*pairs):
+    own, other = [pair[0] for pair in pairs], [pair[1] for pair in pairs]
+    upper = own_half()
+    return jnp.concatenate(
+        [jnp.where(upper == 0, x, y) for x, y in zip(own, other)]
+        + [jnp.where(upper == 0, y, x) for x, y in zip(own, other)]
+    ).astype(F32)
+
+
+def own_half():
+    return lax.axis_index("y") if lax.axis_size("z") == 4 else jnp.int32(0)
+
+
+GATES = {
+    "hidden_grad": "a",
+    "fc1_grad": "",
+    "packed_low": "b",
+    "packed_high": "a",
+    "attend_low": "",
+    "attend_high": "c b",
+    "dense_grad": "a",
+    "back_low": "d c b",
+    "qkv_low": "a e",
+    "back_high": "d f c",
+    "qkv_high": "b e",
+    "to_two": "a c f d",
+    "to_out": "e g n2",
+    "to_one": "d b f o",
+}
+TAIL = (
+    "e g",
+    "n1 n2",
+    "c",
+    "f",
+    "g",
+    "o",
+    "d",
+    "g",
+    "e",
+    "n1",
+    "f",
+    "g",
+)
+
+
+class Piece:
+    def __init__(self, stages):
+        self.stages = stages
+        self.waiting = next(stages)
+        self.value = None
+
+    def step(self, arrived):
+        try:
+            self.waiting = self.stages.send(arrived)
+        except StopIteration as end:
+            self.value, self.waiting = end.value, ()
+
+
+def gate(pieces, *values):
+    flat = list(values)
+    for piece in pieces:
+        flat.extend(piece.waiting)
+    flat = hold(*flat)
+    start = len(values)
+    for piece in pieces:
+        end = start + len(piece.waiting)
+        piece.step(tuple(flat[start:end]))
+        start = end
+    flat = flat[: len(values)]
+    moving = [piece for piece in pieces if len(piece.waiting) > 1]
+    if moving and values:
+        flat = list(hold(*flat, *[piece.waiting[0] for piece in moving]))
+        for piece, kept in zip(moving, flat[len(values) :]):
+            piece.waiting = (kept,) + piece.waiting[1:]
+        flat = flat[: len(values)]
+    return flat
+
+
+def finish(*pieces):
+    for piece in pieces:
+        while piece.value is None:
+            piece.step(piece.waiting)
+    return [piece.value for piece in pieces]
+
+
+def sum_small(values):
+    if lax.axis_size("z") != 4 or lax.axis_size("tensor") != 4:
+        return lax.psum(values, ("z", "y", "tensor"))
+    values = values + swap_tensor(values, 1)
+    values = values + swap_tensor(values, 2)
+    values = values + lax.ppermute(values, "y", ((0, 1), (1, 0)))
+    return sum_line(values)
 
 
 def gelu_parts(hidden):
@@ -286,39 +507,130 @@
         rate = lax.rsqrt(spread + EPS)
         return middle * rate, rate
 
-    whole_in = gather_rows(inputs)
-    xhat, _ = centred(whole_in)
+    scalars = jnp.stack([lengths[0], block_mask()])
+    near_in, far_in = gather_near(inputs)
+    near_out, far_out = gather_near(out_grad)
+    xhat, _ = centred(gather_far(near_in, far_in))
     whole_one = (xhat * gain_one + ln1_bias.astype(F32)).astype(BF16)
     whole_two = (xhat * gain_two + ln2_bias.astype(F32)).astype(BF16)
-    grad_rows = gather_rows(out_grad)
 
     hidden = dot_nn(whole_two, w_fc1) + b_fc1.astype(F32)
-    active, slope = gelu_parts(hidden)
-    active = active.astype(BF16)
-    fc2_grad = dot_tn(active, grad_rows).astype(BF16)
-    fc2_sum = lax.psum(fc2_grad, "dp")
-    hidden_grad = (dot_nt(grad_rows, w_fc2) * slope).astype(BF16)
-    fc1_grad = dot_tn(whole_two, hidden_grad).astype(BF16)
-    fc1_grad, fc2_sum = lax.optimization_barrier((fc1_grad, fc2_sum))
-    fc1_sum = lax.psum(fc1_grad, "dp")
+    active = gelu_parts(hidden)[0].astype(BF16)
+    if far_out is not None:
+        near_out, far_out, active = hold(near_out, far_out, active)
+    grad_rows = gather_far(near_out, far_out)
+    upper = own_half()
+
+    def half_gradient(left, right, side, number, parts):
+        rows = left.shape[1] // 2 // parts
+        part = lax.dynamic_slice_in_dim(left, (side * parts + number) * rows, rows, 1)
+        return dot_tn(part, right).astype(BF16)
+
+    def gradient(left, right, number, parts):
+        sent = half_gradient(left, right, 1 - upper, number, parts)
+        return hold(sent, left, right)
+
+    def keep(left, right, number, parts):
+        return half_gradient(left, right, upper, number, parts)
+
+    token = scalars
+    pieces = {}
+
+    def at(place, *values):
+        return gate([pieces[name] for name in GATES[place].split()], *values)
+
+    sent_a, active, grad_rows = gradient(active, grad_rows, 0, 2)
+    sent_b, active, grad_rows = gradient(active, grad_rows, 1, 2)
+    kept_a = keep(active, grad_rows, 0, 2)
+    kept_b = keep(active, grad_rows, 1, 2)
+    pieces["a"] = Piece(line_stages(kept_a, sent_a))
+    pieces["b"] = Piece(line_stages(kept_b, sent_b))
+    grad_rows, kept_a, kept_b = hold(grad_rows, kept_a, kept_b)
+    hidden_grad = matmul(
+        "nt",
+        [(grad_rows, w_fc2)],
+        BF16,
+        256,
+        extras=[hidden],
+        finish=lambda total, rows: total * gelu_parts(rows)[1],
+        chunk=512,
+        name="hidden_grad",
+    )
+    hidden_grad, whole_two = at("hidden_grad", hidden_grad, whole_two)
     fc1_bias_grad = jnp.sum(hidden_grad, axis=0, dtype=F32)
-
-    whole_one, fc1_grad = lax.optimization_barrier((whole_one, fc1_grad))
-    packed = dot_nn(whole_one, w_qkv) + b_qkv.astype(F32)
-    queries, key_rows, value_rows, context, lse = attend(packed, lengths, tables)
-    context_grad = dot_nt(grad_rows, w_dense).astype(BF16)
-    packed_grad = attend_back(queries, key_rows, value_rows, context_grad, lse, lengths, tables)
-    dense_grad = dot_tn(context, grad_rows).astype(BF16)
-    qkv_grad = dot_tn(whole_one, packed_grad).astype(BF16)
-    dense_grad, qkv_grad, fc1_sum = lax.optimization_barrier((dense_grad, qkv_grad, fc1_sum))
-    dense_sum, qkv_sum = lax.psum((dense_grad, qkv_grad), "dp")
+    sent_c, whole_two, hidden_grad = gradient(whole_two, hidden_grad, 0, 2)
+    sent_d, whole_two, hidden_grad = gradient(whole_two, hidden_grad, 1, 2)
+    kept_c = keep(whole_two, hidden_grad, 0, 2)
+    kept_d = keep(whole_two, hidden_grad, 1, 2)
+    pieces["c"] = Piece(line_stages(kept_c, sent_c))
+    pieces["d"] = Piece(line_stages(kept_d, sent_d))
+    kept_c, kept_d, whole_one = at("fc1_grad", kept_c, kept_d, whole_one)
+
+    columns = w_qkv.shape[1] // 2
+
+    def project(part, rows):
+        return matmul(
+            "nn",
+            [(rows, w_qkv[:, part * columns : (part + 1) * columns])],
+            F32,
+            512,
+            extras=[b_qkv[part * columns : (part + 1) * columns].astype(F32)[None]],
+            finish=jnp.add,
+            name="packed",
+        )
+
+    packed_low = project(0, whole_one)
+    packed_low, whole_one = at("packed_low", packed_low, whole_one)
+    packed_high = project(1, whole_one)
+    packed_low, packed_high = at("packed_high", packed_low, packed_high)
+    saved_low = attend(packed_low, scalars, tables)
+    packed_high, *saved_low = at("attend_low", packed_high, *saved_low)
+    saved_high = attend(packed_high, scalars, tables)
+    context = jnp.concatenate([saved_low[3], saved_high[3]], axis=1)
+    context, grad_rows = at("attend_high", context, grad_rows)
+    sent_e, context, grad_rows = gradient(context, grad_rows, 0, 1)
+    kept_e = keep(context, grad_rows, 0, 1)
+    pieces["e"] = Piece(line_stages(kept_e, sent_e))
+    inner = w_dense.shape[0] // 2
+    grad_rows, kept_e = at("dense_grad", grad_rows, kept_e)
+
+    def back(part, saved, rows):
+        grad = dot_nt(rows, w_dense[part * inner : (part + 1) * inner]).astype(BF16)
+        queries, key_rows, value_rows, _, lse = saved
+        return attend_back(queries, key_rows, value_rows, grad, lse, scalars, tables)
+
+    back_low = back(0, saved_low, grad_rows)
+    back_low, grad_rows, whole_one = at("back_low", back_low, grad_rows, whole_one)
+    sent_f, whole_one, back_low = gradient(whole_one, back_low, 0, 1)
+    kept_f = keep(whole_one, back_low, 0, 1)
+    pieces["f"] = Piece(line_stages(kept_f, sent_f))
+    kept_f, grad_rows = at("qkv_low", kept_f, grad_rows)
+    back_high = back(1, saved_high, grad_rows)
+    back_high, whole_one = at("back_high", back_high, whole_one)
+    sent_g, whole_one, back_high = gradient(whole_one, back_high, 0, 1)
+    kept_g = keep(whole_one, back_high, 0, 1)
+    pieces["g"] = Piece(line_stages(kept_g, sent_g))
+    packed_grad = jnp.concatenate([back_low, back_high], axis=1)
     qkv_bias_grad = jnp.sum(packed_grad, axis=0, dtype=F32)
-
-    branches = scatter_rows(dot_nn(context, w_dense) + dot_nn(active, w_fc2))
+    hidden_grad, kept_g, packed_grad = at("qkv_high", hidden_grad, kept_g, packed_grad)
+    to_two = matmul("nt", [(hidden_grad, w_fc1)], BF16, 512, name="to_two")
+    pieces["n2"] = Piece(scatter_stages(to_two))
+    to_two, context, active = at("to_two", to_two, context, active)
+    to_out = matmul("nn", [(context, w_dense), (active, w_fc2)], BF16, 512, name="to_out")
+    pieces["o"] = Piece(scatter_stages(to_out))
+    to_out, packed_grad = at("to_out", to_out, packed_grad)
+    to_one = matmul("nt", [(packed_grad, w_qkv)], BF16, 512, name="to_one")
+    pieces["n1"] = Piece(scatter_stages(to_one))
+    to_one, token = at("to_one", to_one, token)
+    for names in TAIL:
+        (token,) = gate([pieces[name] for name in names.split()], token)
+    sums = finish(*[pieces[name] for name in ("a", "b", "c", "d", "e", "f", "g", "n1", "n2", "o")])
+    fc2_sum, fc1_sum = whole_rows(*sums[0:2]), whole_rows(*sums[2:4])
+    qkv_sum = jnp.concatenate([whole_rows(sums[5]), whole_rows(sums[6])], axis=1)
+    sums[4] = whole_rows(sums[4])
+    dense_sum, normed_one, normed_two, branches = sums[4], sums[7], sums[8], sums[9]
     outputs = inputs.astype(F32) + branches + (b_dense.astype(F32) + b_fc2.astype(F32))
 
-    normed_two = scatter_rows(dot_nt(hidden_grad, w_fc1))
-    normed_one = scatter_rows(dot_nt(packed_grad, w_qkv))
     own_hat, rate = centred(inputs)
     own_grad = out_grad.astype(F32)
 
@@ -344,7 +656,7 @@
     place = lax.axis_index("tensor")
     slots = jnp.zeros((lax.axis_size("tensor"), sliced.shape[0]), F32)
     slots = lax.dynamic_update_slice_in_dim(slots, sliced[None], place, 0)
-    sums = lax.psum(jnp.concatenate([shared, slots.reshape(-1)]), ("dp", "tensor"))
+    sums = sum_small(jnp.concatenate([shared, slots.reshape(-1)]).reshape(-1, HD)).reshape(-1)
     vectors = sums[: shared.shape[0]].reshape(5, width)
     slots = sums[shared.shape[0] :].reshape(slots.shape)
     own_slot = lax.dynamic_index_in_dim(slots, place, 0, False)
@@ -355,19 +667,21 @@
         vectors[1],
         vectors[2],
         vectors[3],
-        qkv_sum.astype(F32),
+        qkv_sum,
         own_slot[: b_qkv.shape[0]],
-        dense_sum.astype(F32),
+        dense_sum,
         vectors[4],
-        fc1_sum.astype(F32),
+        fc1_sum,
         own_slot[b_qkv.shape[0] :],
-        fc2_sum.astype(F32),
+        fc2_sum,
         vectors[4],
     )
 
 
 def solution(mesh):
-    rows = P(("dp", "tensor"), None)
+    sequences, width = mesh.shape["dp"], mesh.shape["tensor"]
+    mesh = Mesh(mesh.devices.reshape(sequences // 2, 2, width), ("z", "y", "tensor"))
+    rows = P(("z", "y", "tensor"), None)
     columns = P(None, "tensor")
     inner = P("tensor", None)
     split = P("tensor")
@@ -376,7 +690,7 @@
         mesh=mesh,
         in_specs=(
             rows,
-            P("dp"),
+            P(("z", "y")),
             P(),
             P(),
             P(),

time: 1300 us -> 900 us (0.69)
  waiting for transfers between devices: 800 us -> 208 us
  other arithmetic: 106 us -> 249 us
  matrix products: 241 us -> 105 us
  starting transfers between devices: 6.88 us -> 138 us
  Pallas kernels: 75.9 us -> 171 us
  local copies, waits for them, and re-layouts: 53.2 us -> 12.9 us
    psum x4 -> x0, waiting for transfers between devices: 650 us -> none  [the longest x1 261 us: shards(): dense_sum, qkv_sum = lax.psum((dense_grad, qkv_grad), 'dp')]
    ppermute x0 -> x39, waiting for transfers between devices: none -> 130 us  [the longest x7 62 us: line_stages(): kept, got = (yield (kept, lax.ppermute(kept, 'y', PAIRS)))]
    ppermute x0 -> x39, starting transfers between devices: none -> 129 us  [the longest x24 115 us: move_z(): return lax.ppermute(values, 'z', pairs)]
    pallas_call x0 -> x6, Pallas kernels: none -> 122 us  [matmul(): pl.pallas_call(kernel, out_shape=jax.ShapeDtypeStruct((rows, width), kind...]
    dot_general x4 -> x2, matrix products: 81.7 us -> 6.73 us  [dot_nt(): lax.dot_general(left, right, (((1,), (1,)), ((), ())), preferred_element_...]
    ppermute x12 -> x14, waiting for transfers between devices: 150 us -> 77.2 us  [swap_tensor(): return lax.ppermute(values, 'tensor', [(t, t ^ bit) for t in range(count)])]
    convert_element_type x5 -> x27, other arithmetic: 37 us -> 102 us  [the longest x21 64.3 us: add_rows(): return (left.astype(F32) + right.astype(F32)).astype(left.dtype)]
    dot_general x4 -> x1, matrix products: 81.3 us -> 24.1 us  [dot_nn(): lax.dot_general(left, right, (((1,), (0,)), ((), ())), preferred_element_...]
  transfers between devices with their start and end apart: 16 -> 53, of which waited for: 9 -> 13; matrix products, arithmetic and copies ran while one was open for 24% -> 39% of each run, Pallas kernels for 0% -> 19%
where the time goes in v2:
time: 900 us; the launch traced here: 887 us
  other arithmetic  249 us (28%)
  waiting for transfers between devices  208 us (23%)
  Pallas kernels  171 us (19%)
  starting transfers between devices  138 us (15%)
  matrix products  105 us (12%)
  local copies, waits for them, and re-layouts  12.9 us (1%)
    pallas_call x6, Pallas kernels, matmul(): pl.pallas_call(kernel, out_shape=jax.ShapeDtypeStruct((rows, width), kind...  122 us
    ppermute x24, starting transfers between devices, move_z(): return lax.ppermute(values, 'z', pairs)  115 us
    ppermute x14, waiting for transfers between devices, swap_tensor(): return lax.ppermute(values, 'tensor', [(t, t ^ bit) for t in range(count)])  77.2 us
    dot_general x14, matrix products, dot_tn(): lax.dot_general(left, right, (((0,), (0,)), ((), ())), preferred_element_...  74.2 us
    convert_element_type x21, other arithmetic, add_rows(): return (left.astype(F32) + right.astype(F32)).astype(left.dtype)  64.3 us
    ppermute x7, waiting for transfers between devices, line_stages(): kept, got = (yield (kept, lax.ppermute(kept, 'y', PAIRS)))  62 us
    ppermute x24, waiting for transfers between devices, move_z(): return lax.ppermute(values, 'z', pairs)  31.1 us
    pallas_call x2, Pallas kernels, attend_back(): pl.pallas_call(attend_back_kernel, out_shape=jax.ShapeDtypeStruct((SEQ, h...  26.7 us
  transfers between devices with their start and end apart: 53, of which 13 were waited for; matrix products, arithmetic and copies ran while one was open for 39% of the time, Pallas kernels for 19%

profile of v2, /device:TPU:0, one launch (start us, length us, event | category | flops | bytes accessed | tf_op | source)
XLA Modules:
  0.0 887.1 jit_solution(9903145646506749140)
XLA Ops:
  4.2 45.3 %collective-permute-done.3 = bf16[512,2048]{1,0:T(8,128)(2,1)S(1)} collective-permute-done((bf16[512,2048]{1,0:T(8,128)(2,1)}, bf16[512,2048]{1,0:T(8,128)(2,1)S(1)}, u32[]{:S(2)}, u32[]{:S(2)}) %collective-permute-start.3) | collective-permute-done | bytes 2097184 | tf_op jit(solution)/shard_map/ppermute | solution.py:302
  72.3 19.4 %fusion.7 = (bf16[2048,2048]{1,0:T(8,128)(2,1)}, bf16[2048,2048]{1,0:T(8,128)(2,1)}) fusion(f32[2048]{0:T(1024)S(1)} %convert_element_type.401, f32[2048]{0:T(1024)S(1)} %convert_element_type.400, f32[2048]{0:T(1024)S(1)} %add_rsqrt_fusion, f32[2048]{0:T(1024)S(1)} %broadcast_multiply_fusion, bf16[512,2048]{1,0:T(8,128)(2,1)} %collective-permute-done.4, ...), kind=kLoop, calls=%fused_computation.9 | loop fusion | flops 67108864 | bytes 25214976 | tf_op jit(solution)/shard_map/convert_element_type | solution.py:514
  91.8 24.1 %multiply_convert_fusion = (bf16[2048,2048]{1,0:T(8,128)(2,1)}, f32[2048,2048]{1,0:T(8,128)}) fusion(f32[2048]{0:T(1024)S(1)} %convert_element_type.387, bf16[2048,2048]{1,0:T(8,128)(2,1)} %get-tuple-element.230, bf16[2048,2048]{1,0:T(8,128)(2,1)S(1)} %bitcast.58), kind=kOutput, calls=%fused_computation.12 | convolution fusion | flops 17205035008 | bytes 41951232 | tf_op jit(solution)/shard_map/dot_general | solution.py:21
  149.0 27.6 %hidden_grad.1.refs_0_ = bf16[2048,2048]{1,0:T(8,128)(2,1)} custom-call(s32[1]{0:T(128)} %constant.28.clone.1.first_ref, bf16[2048,2048]{1,0:T(8,128)(2,1)} %copy-done, bf16[2048,2048]{1,0:T(8,128)(2,1)} %refs_3_.1, f32[2048,2048]{1,0:T(8,128)} %get-tuple-element.472.refs_2_), custom_call_target="tpu_custom_call" | custom-call | flops 1073741824 | bytes 4194304 | tf_op jit(solution)/shard_map/hidden_grad/pallas_call | solution.py:82
  176.7 8.4 collective-permute-done.6
  189.0 15.3 %collective-permute-start.8 = (bf16[512,2048]{1,0:T(8,128)(2,1)}, bf16[512,2048]{1,0:T(8,128)(2,1)}, u32[]{:S(2)}, u32[]{:S(2)}) collective-permute-start(bf16[512,2048]{1,0:T(8,128)(2,1)} %add_convert_fusion.14), channel_id=1, source_target_pairs={{0,8},{24,16},{1,9},{25,17},{2,10},{26,18},{3,11},{27,19},{4,12},{... | collective-permute-start | bytes 6291464 | tf_op jit(solution)/shard_map/ppermute | solution.py:343
  204.4 9.9 %convolution_convert_fusion.3 = bf16[512,2048]{1,0:T(8,128)(2,1)} fusion(bf16[2048,2048]{1,0:T(8,128)(2,1)} %hidden_grad.1.refs_0_, bf16[2048,2048]{1,0:T(8,128)(2,1)} %get-tuple-element.230, s32[]{:T(128)S(6)} %select_n.202), kind=kOutput, calls=%fused_computation.87 | convolution fusion | flops 4296015872 | bytes 12582916 | tf_op jit(solution)/shard_map/dot_general | solution.py:29
  231.8 11.3 %packed.2.packed_ref = f32[2048,768]{1,0:T(8,128)} custom-call(s32[1]{0:T(128)} %constant.28.clone.1.first_ref, bf16[2048,2048]{1,0:T(8,128)(2,1)} %get-tuple-element.317.refs_0_, bf16[2048,768]{1,0:T(8,128)(2,1)} %get-tuple-element.437.refs_1_, f32[1,768]{1,0:T(1,128)} %reshape.135.refs_2_), custom_call_target="tpu_custom_call" | custom-call | flops 402653184 | bytes 1572864 | tf_op jit(solution)/shard_map/packed/pallas_call | solution.py:82
  255.4 11.3 %packed.3.packed_ref = f32[2048,768]{1,0:T(8,128)} custom-call(s32[1]{0:T(128)} %constant.28.clone.1.first_ref, bf16[2048,2048]{1,0:T(8,128)(2,1)} %get-tuple-element.317.refs_0_, bf16[2048,768]{1,0:T(8,128)(2,1)} %get-tuple-element.436.refs_1_, f32[1,768]{1,0:T(1,128)} %reshape.136.refs_2_), custom_call_target="tpu_custom_call" | custom-call | flops 402653184 | bytes 1572864 | tf_op jit(solution)/shard_map/packed/pallas_call | solution.py:82
  272.0 11.3 %attend.2 = (bf16[2048,256]{1,0:T(8,128)(2,1)}, bf16[2048,256]{1,0:T(8,128)(2,1)}, bf16[2048,256]{1,0:T(8,128)(2,1)}, bf16[2048,256]{1,0:T(8,128)(2,1)}, f32[2,1,2048]{2,1,0:T(1,128)}) custom-call(s32[2]{0:T(128)} %pad_add_fusion.length_ref, f32[2048,768]{1,0:T(8,128)} %packed.2.packed_ref, f32[2048,128]{1,0:T(8,128)} %get-tuple-element.470.cos_ref, ...), custom_call_target="tpu_custom_call" | custom-call | flops 2147483648 | bytes 10485760 | tf_op jit(solution)/shard_map/attend/pallas_call | solution.py:183
  283.4 11.8 %attend.3 = (bf16[2048,256]{1,0:T(8,128)(2,1)}, bf16[2048,256]{1,0:T(8,128)(2,1)}, bf16[2048,256]{1,0:T(8,128)(2,1)}, bf16[2048,256]{1,0:T(8,128)(2,1)}, f32[2,1,2048]{2,1,0:T(1,128)}) custom-call(s32[2]{0:T(128)} %pad_add_fusion.length_ref, f32[2048,768]{1,0:T(8,128)} %packed.3.packed_ref, f32[2048,128]{1,0:T(8,128)} %get-tuple-element.470.cos_ref, ...), custom_call_target="tpu_custom_call" | custom-call | flops 2147483648 | bytes 10485760 | tf_op jit(solution)/shard_map/attend/pallas_call | solution.py:183
  300.7 7.6 collective-permute-start.13
  327.3 13.3 %attend_back.2 = bf16[2048,768]{1,0:T(8,128)(2,1)} custom-call(s32[2]{0:T(128)} %pad_add_fusion.length_ref, bf16[2048,256]{1,0:T(8,128)(2,1)} %get-tuple-element.255.q_ref, bf16[2048,256]{1,0:T(8,128)(2,1)} %get-tuple-element.256.k_ref, bf16[2048,256]{1,0:T(8,128)(2,1)} %get-tuple-element.257.v_ref, bf16[2048,256]{1,0:T(8,128)(2,1)} %convolution_convert_fusion.9.grad_ref, ...), custom_call_target="tpu_custom_call" | custom-call | flops 5368709120 | bytes 7340032 | tf_op jit(solution)/shard_map/attend_back/pallas_call | solution.py:272
  340.6 9.5 %collective-permute-done.13 = bf16[512,2048]{1,0:T(8,128)(2,1)} collective-permute-done((bf16[512,2048]{1,0:T(8,128)(2,1)S(1)}, bf16[512,2048]{1,0:T(8,128)(2,1)}, u32[]{:S(2)}, u32[]{:S(2)}) %collective-permute-start.13) | collective-permute-done | bytes 2097184 | tf_op jit(solution)/shard_map/ppermute | solution.py:343
  354.1 17.1 %collective-permute-start.17 = (bf16[512,2048]{1,0:T(8,128)(2,1)}, bf16[512,2048]{1,0:T(8,128)(2,1)}, u32[]{:S(2)}, u32[]{:S(2)}) collective-permute-start(bf16[512,2048]{1,0:T(8,128)(2,1)} %add_convert_fusion.8), channel_id=1, source_target_pairs={{0,8},{24,16},{1,9},{25,17},{2,10},{26,18},{3,11},{27,19},{4,12},{... | collective-permute-start | bytes 6291464 | tf_op jit(solution)/shard_map/ppermute | solution.py:343
  396.2 6.9 collective-permute-start.21
  409.6 13.4 %attend_back.3 = bf16[2048,768]{1,0:T(8,128)(2,1)} custom-call(s32[2]{0:T(128)} %pad_add_fusion.length_ref, bf16[2048,256]{1,0:T(8,128)(2,1)} %get-tuple-element.252.q_ref, bf16[2048,256]{1,0:T(8,128)(2,1)} %get-tuple-element.253.k_ref, bf16[2048,256]{1,0:T(8,128)(2,1)} %get-tuple-element.254.v_ref, bf16[2048,256]{1,0:T(8,128)(2,1)} %convolution_convert_fusion.8.grad_ref, ...), custom_call_target="tpu_custom_call" | custom-call | flops 5368709120 | bytes 7340032 | tf_op jit(solution)/shard_map/attend_back/pallas_call | solution.py:272
  436.2 8.6 collective-permute-start.24
  467.1 23.6 %to_two.1 = bf16[2048,2048]{1,0:T(8,128)(2,1)} custom-call(s32[1]{0:T(128)} %constant.28.clone.1.first_ref, bf16[2048,2048]{1,0:T(8,128)(2,1)} %hidden_grad.1.refs_0_, bf16[2048,2048]{1,0:T(8,128)(2,1)} %refs_1_.5), custom_call_target="tpu_custom_call" | custom-call | flops 1073741824 | bytes 4194304 | tf_op jit(solution)/shard_map/to_two/pallas_call | solution.py:82
  514.7 29.1 %to_out.1 = bf16[2048,2048]{1,0:T(8,128)(2,1)} custom-call(s32[1]{0:T(128)} %constant.28.clone.1.first_ref, bf16[2048,512]{1,0:T(8,128)(2,1)} %copy-done.4, bf16[512,2048]{1,0:T(8,128)(2,1)} %refs_1_.6, bf16[2048,2048]{1,0:T(8,128)(2,1)} %get-tuple-element.341.refs_2_, bf16[2048,2048]{1,0:T(8,128)(2,1)} %refs_3_.1), custom_call_target="tpu_custom_call" | custom-call | flops 1342177280 | bytes 4194304 | tf_op jit(solution)/shard_map/to_out/pallas_call | solution.py:82
  556.7 28.1 %collective-permute-done.51 = bf16[512,2048]{1,0:T(8,128)(2,1)} collective-permute-done((bf16[512,2048]{1,0:T(8,128)(2,1)S(1)}, bf16[512,2048]{1,0:T(8,128)(2,1)}, u32[]{:S(2)}, u32[]{:S(2)}) %collective-permute-start.51) | collective-permute-done | bytes 2097184 | tf_op jit(solution)/shard_map/ppermute | solution.py:378
  591.3 12.3 %collective-permute-start.35 = (bf16[1024,768]{1,0:T(8,128)(2,1)}, bf16[1024,768]{1,0:T(8,128)(2,1)}, u32[]{:S(2)}, u32[]{:S(2)}) collective-permute-start(bf16[1024,768]{1,0:T(8,128)(2,1)} %add_convert_fusion.18), channel_id=1, source_target_pairs={{0,8},{24,16},{1,9},{25,17},{2,10},{26,18},{3,11},{27,19},{4,12},{... | collective-permute-start | bytes 4718600 | tf_op jit(solution)/shard_map/ppermute | solution.py:343
  611.7 18.4 %to_one.1 = bf16[2048,2048]{1,0:T(8,128)(2,1)} custom-call(s32[1]{0:T(128)} %constant.28.clone.1.first_ref, bf16[2048,1536]{1,0:T(8,128)(2,1)} %copy-done.3, bf16[2048,1536]{1,0:T(8,128)(2,1)} %refs_1_.7), custom_call_target="tpu_custom_call" | custom-call | flops 805306368 | bytes 4194304 | tf_op jit(solution)/shard_map/to_one/pallas_call | solution.py:82
  654.9 15.7 %collective-permute-done.34 = bf16[256,2048]{1,0:T(8,128)(2,1)S(1)} collective-permute-done((bf16[256,2048]{1,0:T(8,128)(2,1)}, bf16[256,2048]{1,0:T(8,128)(2,1)S(1)}, u32[]{:S(2)}, u32[]{:S(2)}) %collective-permute-start.34) | collective-permute-done | bytes 1048608 | tf_op jit(solution)/shard_map/ppermute | solution.py:343
  695.6 7.6 add_convert_fusion
  709.0 9.3 %maximum_convert_fusion.1 = f32[2048,2048]{1,0:T(8,128)} fusion(bf16[512,2048]{1,0:T(8,128)(2,1)} %get-tuple-element.441, bf16[512,2048]{1,0:T(8,128)(2,1)} %get-tuple-element.439, bf16[512,2048]{1,0:T(8,128)(2,1)} %get-tuple-element.440, bf16[512,2048]{1,0:T(8,128)(2,1)S(1)} %copy-done.13), kind=kLoop, calls=%fused_computation.17 | loop fusion | flops 33554432 | bytes 25165824 | tf_op jit(solution)/shard_map/convert_element_type | solution.py:388
  719.9 33.8 %collective-permute-done.50 = bf16[256,2048]{1,0:T(8,128)(2,1)} collective-permute-done((bf16[256,2048]{1,0:T(8,128)(2,1)}, bf16[256,2048]{1,0:T(8,128)(2,1)}, u32[]{:S(2)}, u32[]{:S(2)}) %collective-permute-start.50) | collective-permute-done | bytes 1048608 | tf_op jit(solution)/shard_map/ppermute | solution.py:378
  759.0 23.5 %collective-permute-done.38 = bf16[512,2048]{1,0:T(8,128)(2,1)S(1)} collective-permute-done((bf16[512,2048]{1,0:T(8,128)(2,1)}, bf16[512,2048]{1,0:T(8,128)(2,1)S(1)}, u32[]{:S(2)}, u32[]{:S(2)}) %collective-permute-start.38) | collective-permute-done | bytes 2097184 | tf_op jit(solution)/shard_map/ppermute | solution.py:302
  786.8 7.5 convert_reduce_fusion.4
  809.8 25.2 %collective-permute-done.41 = f32[192,128]{1,0:T(8,128)S(1)} collective-permute-done((f32[192,128]{1,0:T(8,128)S(1)}, f32[192,128]{1,0:T(8,128)S(1)}, u32[]{:S(2)}, u32[]{:S(2)}) %collective-permute-start.41) | collective-permute-done | bytes 98336 | tf_op jit(solution)/shard_map/ppermute | solution.py:472
  835.0 20.8 %collective-permute-start.42 = (f32[192,128]{1,0:T(8,128)S(1)}, f32[192,128]{1,0:T(8,128)S(1)}, u32[]{:S(2)}, u32[]{:S(2)}) collective-permute-start(f32[192,128]{1,0:T(8,128)S(1)} %add.307), channel_id=1, source_target_pairs={{0,8},{24,16},{1,9},{25,17},{2,10},{26,18},{3,11},{27,19},{4,12},{... | collective-permute-start | bytes 294920 | tf_op jit(solution)/shard_map/ppermute | solution.py:343
  860.5 23.8 %maximum_convert_fusion.2 = f32[2048,1536]{1,0:T(8,128)} fusion(bf16[1024,768]{1,0:T(8,128)(2,1)S(1)} %get-tuple-element.455, bf16[1024,768]{1,0:T(8,128)(2,1)S(1)} %get-tuple-element.454, bf16[1024,768]{1,0:T(8,128)(2,1)S(1)} %get-tuple-element.453, bf16[1024,768]{1,0:T(8,128)(2,1)S(1)} %get-tuple-element.452), kind=kLoop, calls=%fused_computation.18 | loop fusion | flops 25165824 | bytes 18874368 | tf_op jit(solution)/shard_map/concatenate | solution.py:629
  (357 shorter events, 333.2 us)
Async XLA Ops:
  3.6 56.7 %collective-permute-start = (bf16[512,2048]{1,0:T(8,128)(2,1)}, bf16[512,2048]{1,0:T(8,128)(2,1)}, u32[]{:S(2)}, u32[]{:S(2)}) collective-permute-start(bf16[512,2048]{1,0:T(8,128)(2,1)} %param.29), channel_id=1, source_target_pairs={{0,1},{1,0},{2,3},{3,2},{4,5},{5,4},{6,7},{7,6},{8,9},{9,8},{10,11... | collective-permute-start | bytes 6291464 | tf_op jit(solution)/shard_map/ppermute | solution.py:302
  3.7 59.7 %collective-permute-start.2 = (bf16[512,2048]{1,0:T(8,128)(2,1)}, bf16[512,2048]{1,0:T(8,128)(2,1)}, u32[]{:S(2)}, u32[]{:S(2)}) collective-permute-start(bf16[512,2048]{1,0:T(8,128)(2,1)} %param.15), channel_id=1, source_target_pairs={{0,1},{1,0},{2,3},{3,2},{4,5},{5,4},{6,7},{7,6},{8,9},{9,8},{10,11... | collective-permute-start | bytes 6291464 | tf_op jit(solution)/shard_map/ppermute | solution.py:302
  49.5 66.4 %collective-permute-start.1 = (bf16[512,2048]{1,0:T(8,128)(2,1)}, bf16[512,2048]{1,0:T(8,128)(2,1)}, u32[]{:S(2)}, u32[]{:S(2)}) collective-permute-start(bf16[512,2048]{1,0:T(8,128)(2,1)} %param.29), channel_id=1, source_target_pairs={{0,2},{1,3},{2,0},{3,1},{4,6},{5,7},{6,4},{7,5},{8,10},{9,11},{10,... | collective-permute-start | bytes 6291464 | tf_op jit(solution)/shard_map/ppermute | solution.py:302
  148.5 94.7 %collective-permute-start.7 = (bf16[512,2048]{1,0:T(8,128)(2,1)}, bf16[512,2048]{1,0:T(8,128)(2,1)S(1)}, u32[]{:S(2)}, u32[]{:S(2)}) collective-permute-start(bf16[512,2048]{1,0:T(8,128)(2,1)} %convolution_convert_fusion.6), channel_id=1, source_target_pairs={{0,4},{4,0},{1,5},{5,1},{2,6},{6,2},{3,7},{7,3},{8,12},{12,8},{9,1... | collective-permute-start | bytes 6291464 | tf_op jit(solution)/shard_map/ppermute | solution.py:370
  189.0 77.7 %collective-permute-start.8 = (bf16[512,2048]{1,0:T(8,128)(2,1)}, bf16[512,2048]{1,0:T(8,128)(2,1)}, u32[]{:S(2)}, u32[]{:S(2)}) collective-permute-start(bf16[512,2048]{1,0:T(8,128)(2,1)} %add_convert_fusion.14), channel_id=1, source_target_pairs={{0,8},{24,16},{1,9},{25,17},{2,10},{26,18},{3,11},{27,19},{4,12},{... | collective-permute-start | bytes 6291464 | tf_op jit(solution)/shard_map/ppermute | solution.py:343
  243.1 53.6 %collective-permute-start.9 = (bf16[512,2048]{1,0:T(8,128)(2,1)}, bf16[512,2048]{1,0:T(8,128)(2,1)}, u32[]{:S(2)}, u32[]{:S(2)}) collective-permute-start(bf16[512,2048]{1,0:T(8,128)(2,1)} %convolution_convert_fusion.3), channel_id=1, source_target_pairs={{0,4},{4,0},{1,5},{5,1},{2,6},{6,2},{3,7},{7,3},{8,12},{12,8},{9,1... | collective-permute-start | bytes 6291464 | tf_op jit(solution)/shard_map/ppermute | solution.py:370
  254.9 85.7 %collective-permute-start.12 = (bf16[512,2048]{1,0:T(8,128)(2,1)}, bf16[512,2048]{1,0:T(8,128)(2,1)}, u32[]{:S(2)}, u32[]{:S(2)}) collective-permute-start(bf16[512,2048]{1,0:T(8,128)(2,1)} %convolution_convert_fusion.2), channel_id=1, source_target_pairs={{0,4},{4,0},{1,5},{5,1},{2,6},{6,2},{3,7},{7,3},{8,12},{12,8},{9,1... | collective-permute-start | bytes 6291464 | tf_op jit(solution)/shard_map/ppermute | solution.py:370
  316.3 75.8 %collective-permute-start.16 = (bf16[256,2048]{1,0:T(8,128)(2,1)}, bf16[256,2048]{1,0:T(8,128)(2,1)}, u32[]{:S(2)}, u32[]{:S(2)}) collective-permute-start(bf16[256,2048]{1,0:T(8,128)(2,1)} %convolution_convert_fusion.11), channel_id=1, source_target_pairs={{0,4},{4,0},{1,5},{5,1},{2,6},{6,2},{3,7},{7,3},{8,12},{12,8},{9,1... | collective-permute-start | bytes 3145736 | tf_op jit(solution)/shard_map/ppermute | solution.py:370
  322.6 71.0 %collective-permute-start.15 = (bf16[512,2048]{1,0:T(8,128)(2,1)}, bf16[512,2048]{1,0:T(8,128)(2,1)}, u32[]{:S(2)}, u32[]{:S(2)}) collective-permute-start(bf16[512,2048]{1,0:T(8,128)(2,1)} %add_convert_fusion.9), channel_id=1, source_target_pairs={{8,0},{16,24},{9,1},{17,25},{10,2},{18,26},{11,3},{19,27},{12,4},{... | collective-permute-start | bytes 6291464 | tf_op jit(solution)/shard_map/ppermute | solution.py:343
  354.1 74.1 %collective-permute-start.17 = (bf16[512,2048]{1,0:T(8,128)(2,1)}, bf16[512,2048]{1,0:T(8,128)(2,1)}, u32[]{:S(2)}, u32[]{:S(2)}) collective-permute-start(bf16[512,2048]{1,0:T(8,128)(2,1)} %add_convert_fusion.8), channel_id=1, source_target_pairs={{0,8},{24,16},{1,9},{25,17},{2,10},{26,18},{3,11},{27,19},{4,12},{... | collective-permute-start | bytes 6291464 | tf_op jit(solution)/shard_map/ppermute | solution.py:343
  381.1 77.9 %collective-permute-start.20 = (bf16[512,2048]{1,0:T(8,128)(2,1)}, bf16[512,2048]{1,0:T(8,128)(2,1)}, u32[]{:S(2)}, u32[]{:S(2)}) collective-permute-start(bf16[512,2048]{1,0:T(8,128)(2,1)} %add_convert_fusion.6), channel_id=1, source_target_pairs={{8,0},{16,24},{9,1},{17,25},{10,2},{18,26},{11,3},{19,27},{12,4},{... | collective-permute-start | bytes 6291464 | tf_op jit(solution)/shard_map/ppermute | solution.py:343
  396.2 64.8 %collective-permute-start.21 = (bf16[256,2048]{1,0:T(8,128)(2,1)}, bf16[256,2048]{1,0:T(8,128)(2,1)}, u32[]{:S(2)}, u32[]{:S(2)}) collective-permute-start(bf16[256,2048]{1,0:T(8,128)(2,1)} %add_convert_fusion.23), channel_id=1, source_target_pairs={{0,8},{24,16},{1,9},{25,17},{2,10},{26,18},{3,11},{27,19},{4,12},{... | collective-permute-start | bytes 3145736 | tf_op jit(solution)/shard_map/ppermute | solution.py:343
  426.7 77.0 %collective-permute-start.22 = (bf16[512,2048]{1,0:T(8,128)(2,1)}, bf16[512,2048]{1,0:T(8,128)(2,1)}, u32[]{:S(2)}, u32[]{:S(2)}) collective-permute-start(bf16[512,2048]{1,0:T(8,128)(2,1)} %broadcast_select_fusion.11), channel_id=1, source_target_pairs={{0,4},{4,0},{1,5},{5,1},{2,6},{6,2},{3,7},{7,3},{8,12},{12,8},{9,1... | collective-permute-start | bytes 6291464 | tf_op jit(solution)/shard_map/ppermute | solution.py:378
  432.8 72.7 %collective-permute-start.23 = (bf16[512,2048]{1,0:T(8,128)(2,1)}, bf16[512,2048]{1,0:T(8,128)(2,1)}, u32[]{:S(2)}, u32[]{:S(2)}) collective-permute-start(bf16[512,2048]{1,0:T(8,128)(2,1)} %add_convert_fusion.4), channel_id=1, source_target_pairs={{8,0},{16,24},{9,1},{17,25},{10,2},{18,26},{11,3},{19,27},{12,4},{... | collective-permute-start | bytes 6291464 | tf_op jit(solution)/shard_map/ppermute | solution.py:343
  436.2 66.9 %collective-permute-start.24 = (bf16[1024,768]{1,0:T(8,128)(2,1)S(1)}, bf16[1024,768]{1,0:T(8,128)(2,1)}, u32[]{:S(2)}, u32[]{:S(2)}) collective-permute-start(bf16[1024,768]{1,0:T(8,128)(2,1)S(1)} %add_convert_fusion.20), channel_id=1, source_target_pairs={{0,8},{24,16},{1,9},{25,17},{2,10},{26,18},{3,11},{27,19},{4,12},{... | collective-permute-start | bytes 4718600 | tf_op jit(solution)/shard_map/ppermute | solution.py:343
  500.0 88.4 %collective-permute-start.28 = (bf16[1024,2048]{1,0:T(8,128)(2,1)}, bf16[1024,2048]{1,0:T(8,128)(2,1)}, u32[]{:S(2)}, u32[]{:S(2)}) collective-permute-start(bf16[1024,2048]{1,0:T(8,128)(2,1)} %pad_maximum_fusion.2), channel_id=1, source_target_pairs={{0,1},{1,0},{2,3},{3,2},{4,5},{5,4},{6,7},{7,6},{8,9},{9,8},{10,11... | collective-permute-start | bytes 12582920 | tf_op jit(solution)/shard_map/ppermute | solution.py:302
  503.1 82.1 %collective-permute-start.27 = (bf16[1024,768]{1,0:T(8,128)(2,1)}, bf16[1024,768]{1,0:T(8,128)(2,1)}, u32[]{:S(2)}, u32[]{:S(2)}) collective-permute-start(bf16[1024,768]{1,0:T(8,128)(2,1)} %fusion.51), channel_id=1, source_target_pairs={{0,4},{4,0},{1,5},{5,1},{2,6},{6,2},{3,7},{7,3},{8,12},{12,8},{9,1... | collective-permute-start | bytes 4718600 | tf_op jit(solution)/shard_map/ppermute | solution.py:370
  503.7 82.9 %collective-permute-start.26 = (bf16[256,2048]{1,0:T(8,128)(2,1)}, bf16[256,2048]{1,0:T(8,128)(2,1)}, u32[]{:S(2)}, u32[]{:S(2)}) collective-permute-start(bf16[256,2048]{1,0:T(8,128)(2,1)} %add_convert_fusion.22), channel_id=1, source_target_pairs={{8,16},{16,8},{9,17},{17,9},{10,18},{18,10},{11,19},{19,11},{12,20... | collective-permute-start | bytes 3145736 | tf_op jit(solution)/shard_map/ppermute | solution.py:343
  507.4 77.3 %collective-permute-start.51 = (bf16[512,2048]{1,0:T(8,128)(2,1)S(1)}, bf16[512,2048]{1,0:T(8,128)(2,1)}, u32[]{:S(2)}, u32[]{:S(2)}) collective-permute-start(bf16[512,2048]{1,0:T(8,128)(2,1)S(1)} %broadcast_select_fusion.9), channel_id=1, source_target_pairs={{0,4},{4,0},{1,5},{5,1},{2,6},{6,2},{3,7},{7,3},{8,12},{12,8},{9,1... | collective-permute-start | bytes 6291464 | tf_op jit(solution)/shard_map/ppermute | solution.py:378
  552.7 92.4 %collective-permute-start.32 = (bf16[1024,2048]{1,0:T(8,128)(2,1)}, bf16[1024,2048]{1,0:T(8,128)(2,1)}, u32[]{:S(2)}, u32[]{:S(2)}) collective-permute-start(bf16[1024,2048]{1,0:T(8,128)(2,1)} %pad_maximum_fusion.3), channel_id=1, source_target_pairs={{0,1},{1,0},{2,3},{3,2},{4,5},{5,4},{6,7},{7,6},{8,9},{9,8},{10,11... | collective-permute-start | bytes 12582920 | tf_op jit(solution)/shard_map/ppermute | solution.py:302
  584.7 54.4 %collective-permute-start.30 = (bf16[512,2048]{1,0:T(8,128)(2,1)}, bf16[512,2048]{1,0:T(8,128)(2,1)}, u32[]{:S(2)}, u32[]{:S(2)}) collective-permute-start(bf16[512,2048]{1,0:T(8,128)(2,1)} %broadcast_select_fusion.10), channel_id=1, source_target_pairs={{0,4},{4,0},{1,5},{5,1},{2,6},{6,2},{3,7},{7,3},{8,12},{12,8},{9,1... | collective-permute-start | bytes 6291464 | tf_op jit(solution)/shard_map/ppermute | solution.py:378
  585.2 59.2 %collective-permute-start.29 = (bf16[512,2048]{1,0:T(8,128)(2,1)S(1)}, bf16[512,2048]{1,0:T(8,128)(2,1)}, u32[]{:S(2)}, u32[]{:S(2)}) collective-permute-start(bf16[512,2048]{1,0:T(8,128)(2,1)S(1)} %add_convert_fusion.3), channel_id=1, source_target_pairs={{8,0},{16,24},{9,1},{17,25},{10,2},{18,26},{11,3},{19,27},{12,4},{... | collective-permute-start | bytes 6291464 | tf_op jit(solution)/shard_map/ppermute | solution.py:343
  586.6 56.6 %collective-permute-start.31 = (bf16[1024,768]{1,0:T(8,128)(2,1)S(1)}, bf16[1024,768]{1,0:T(8,128)(2,1)}, u32[]{:S(2)}, u32[]{:S(2)}) collective-permute-start(bf16[1024,768]{1,0:T(8,128)(2,1)S(1)} %add_convert_fusion.19), channel_id=1, source_target_pairs={{8,16},{16,8},{9,17},{17,9},{10,18},{18,10},{11,19},{19,11},{12,20... | collective-permute-start | bytes 4718600 | tf_op jit(solution)/shard_map/ppermute | solution.py:343
  591.3 80.6 %collective-permute-start.35 = (bf16[1024,768]{1,0:T(8,128)(2,1)}, bf16[1024,768]{1,0:T(8,128)(2,1)}, u32[]{:S(2)}, u32[]{:S(2)}) collective-permute-start(bf16[1024,768]{1,0:T(8,128)(2,1)} %add_convert_fusion.18), channel_id=1, source_target_pairs={{0,8},{24,16},{1,9},{25,17},{2,10},{26,18},{3,11},{27,19},{4,12},{... | collective-permute-start | bytes 4718600 | tf_op jit(solution)/shard_map/ppermute | solution.py:343
  639.1 55.0 %collective-permute-start.36 = (bf16[1024,2048]{1,0:T(8,128)(2,1)}, bf16[1024,2048]{1,0:T(8,128)(2,1)}, u32[]{:S(2)}, u32[]{:S(2)}) collective-permute-start(bf16[1024,2048]{1,0:T(8,128)(2,1)} %pad_maximum_fusion.4), channel_id=1, source_target_pairs={{0,1},{1,0},{2,3},{3,2},{4,5},{5,4},{6,7},{7,6},{8,9},{9,8},{10,11... | collective-permute-start | bytes 12582920 | tf_op jit(solution)/shard_map/ppermute | solution.py:302
  651.5 107.4 %collective-permute-start.33 = (bf16[512,2048]{1,0:T(8,128)(2,1)}, bf16[512,2048]{1,0:T(8,128)(2,1)}, u32[]{:S(2)}, u32[]{:S(2)}) collective-permute-start(bf16[512,2048]{1,0:T(8,128)(2,1)} %get-tuple-element.450), channel_id=1, source_target_pairs={{0,2},{1,3},{2,0},{3,1},{4,6},{5,7},{6,4},{7,5},{8,10},{9,11},{10,... | collective-permute-start | bytes 6291464 | tf_op jit(solution)/shard_map/ppermute | solution.py:302
  683.8 75.1 %collective-permute-start.52 = (bf16[512,2048]{1,0:T(8,128)(2,1)}, bf16[512,2048]{1,0:T(8,128)(2,1)}, u32[]{:S(2)}, u32[]{:S(2)}) collective-permute-start(bf16[512,2048]{1,0:T(8,128)(2,1)} %broadcast_select_fusion.8), channel_id=1, source_target_pairs={{0,4},{4,0},{1,5},{5,1},{2,6},{6,2},{3,7},{7,3},{8,12},{12,8},{9,1... | collective-permute-start | bytes 6291464 | tf_op jit(solution)/shard_map/ppermute | solution.py:378
  693.2 60.5 %collective-permute-start.50 = (bf16[256,2048]{1,0:T(8,128)(2,1)}, bf16[256,2048]{1,0:T(8,128)(2,1)}, u32[]{:S(2)}, u32[]{:S(2)}) collective-permute-start(bf16[256,2048]{1,0:T(8,128)(2,1)} %broadcast_select_fusion.20), channel_id=1, source_target_pairs={{0,4},{4,0},{1,5},{5,1},{2,6},{6,2},{3,7},{7,3},{8,12},{12,8},{9,1... | collective-permute-start | bytes 3145736 | tf_op jit(solution)/shard_map/ppermute | solution.py:378
  694.2 64.8 %collective-permute-start.48 = (bf16[1024,768]{1,0:T(8,128)(2,1)}, bf16[1024,768]{1,0:T(8,128)(2,1)}, u32[]{:S(2)}, u32[]{:S(2)}) collective-permute-start(bf16[1024,768]{1,0:T(8,128)(2,1)} %add_convert_fusion.15), channel_id=1, source_target_pairs={{8,0},{16,24},{9,1},{17,25},{10,2},{18,26},{11,3},{19,27},{12,4},{... | collective-permute-start | bytes 4718600 | tf_op jit(solution)/shard_map/ppermute | solution.py:343
  708.5 74.0 %collective-permute-start.38 = (bf16[512,2048]{1,0:T(8,128)(2,1)}, bf16[512,2048]{1,0:T(8,128)(2,1)S(1)}, u32[]{:S(2)}, u32[]{:S(2)}) collective-permute-start(bf16[512,2048]{1,0:T(8,128)(2,1)} %get-tuple-element.446), channel_id=1, source_target_pairs={{0,2},{1,3},{2,0},{3,1},{4,6},{5,7},{6,4},{7,5},{8,10},{9,11},{10,... | collective-permute-start | bytes 6291464 | tf_op jit(solution)/shard_map/ppermute | solution.py:302
  753.7 56.1 %collective-permute-start.46 = (bf16[1024,768]{1,0:T(8,128)(2,1)S(1)}, bf16[1024,768]{1,0:T(8,128)(2,1)}, u32[]{:S(2)}, u32[]{:S(2)}) collective-permute-start(bf16[1024,768]{1,0:T(8,128)(2,1)S(1)} %broadcast_select_fusion.13), channel_id=1, source_target_pairs={{0,4},{4,0},{1,5},{5,1},{2,6},{6,2},{3,7},{7,3},{8,12},{12,8},{9,1... | collective-permute-start | bytes 4718600 | tf_op jit(solution)/shard_map/ppermute | solution.py:378
  796.0 61.4 %collective-permute-start.49 = (bf16[1024,768]{1,0:T(8,128)(2,1)S(1)}, bf16[1024,768]{1,0:T(8,128)(2,1)S(1)}, u32[]{:S(2)}, u32[]{:S(2)}) collective-permute-start(bf16[1024,768]{1,0:T(8,128)(2,1)S(1)} %broadcast_select_fusion.12), channel_id=1, source_target_pairs={{0,4},{4,0},{1,5},{5,1},{2,6},{6,2},{3,7},{7,3},{8,12},{12,8},{9,1... | collective-permute-start | bytes 4718600 | tf_op jit(solution)/shard_map/ppermute | solution.py:378
  (90 other events, 1889.5 us)

commit v3 on v2

v3 whole, which is shorter than its diff:
```python
from functools import partial

import jax
import jax.numpy as jnp
from jax import lax
from jax.experimental import pallas as pl
from jax.experimental.pallas import tpu as pltpu
from jax.sharding import Mesh
from jax.sharding import PartitionSpec as P

HD = 128
ROT = 32
SEQ = 2048
BLOCK = 512
EPS = 1e-05
HINT = 7
F32 = jnp.float32
BF16 = jnp.bfloat16


def dot_nn(left, right):
    return lax.dot_general(left, right, (((1,), (0,)), ((), ())), preferred_element_type=F32)


def dot_nt(left, right):
    return lax.dot_general(left, right, (((1,), (1,)), ((), ())), preferred_element_type=F32)


def dot_tn(left, right):
    return lax.dot_general(left, right, (((0,), (0,)), ((), ())), preferred_element_type=F32)


FORMS = {"nn": (1, 0), "nt": (1, 1)}


def matmul(form, pairs, kind, block, extras=(), finish=None, chunk=None, split=False, name=None):
    sides = FORMS[form]
    rows = pairs[0][0].shape[0]
    block = min(block, rows)
    pairs = [
        (left, right if isinstance(right, tuple) else (right, right.shape, (0, 0)))
        for left, right in pairs
    ]
    width = pairs[0][1][1][1 - sides[1]]
    dims = (((sides[0],), (sides[1],)), ((), ()))
    count = len(pairs)
    chunk = width if chunk is None else min(chunk, width)

    outs = 2 if split else 1

    def kernel(*refs):
        if split:
            for number in range(2):
                pl.when(pl.program_id(0) // 2 == number)(partial(fill, refs[:-2], refs[number - 2]))
        else:
            fill(refs[:-1], refs[-1])

    def fill(refs, out_ref):
        for start in range(0, width, chunk):
            part = slice(start, start + chunk)
            rest = [ref[:, part] for ref in refs[2 * count :]]
            total = None
            for number in range(count):
                right = refs[2 * number + 1]
                product = lax.dot_general(
                    refs[2 * number][...],
                    right[part, :] if form == "nt" else right[:, part],
                    dims,
                    preferred_element_type=F32,
                )
                total = product if total is None else total + product
            if finish is not None:
                total = finish(total, *rest)
            out_ref[:, part] = total.astype(kind)

    def at_row(i):
        return jnp.where(i < 2, 2 * i + 1, 2 * i - 4) if split else i

    specs, flat = [], []
    for left, (right, shape, index) in pairs:
        specs.append(pl.BlockSpec((block, left.shape[1]), lambda i: (at_row(i), 0)))
        specs.append(
            pl.BlockSpec(shape, lambda i, index=index: index, pipeline_mode=pl.Buffered(1))
        )
        flat.extend([left, right])
    for extra in extras:
        if isinstance(extra, tuple):
            extra, column = extra
            specs.append(pl.BlockSpec((block, width), lambda i, column=column: (i, column)))
        else:
            specs.append(pl.BlockSpec(extra.shape, lambda i: (0, 0)))
        flat.append(extra)
    inner = sum(left.shape[1] for left, _ in pairs)
    if split:
        out_specs = (
            pl.BlockSpec((block, width), lambda i: (jnp.minimum(i, 1), 0)),
            pl.BlockSpec((block, width), lambda i: (jnp.maximum(i - 2, 0), 0)),
        )
    else:
        out_specs = (pl.BlockSpec((block, width), lambda i: (i, 0)),)
    results = pl.pallas_call(
        kernel,
        out_shape=(jax.ShapeDtypeStruct((rows // outs, width), kind),) * outs,
        grid=(rows // block,),
        in_specs=specs,
        out_specs=out_specs,
        compiler_params=pltpu.CompilerParams(vmem_limit_bytes=56 << 20),
        cost_estimate=pl.CostEstimate(
            flops=rows * width * inner * HINT // 8, transcendentals=0, bytes_accessed=rows * width
        ),
        name=name,
    )(*flat)
    return results if split else results[0]


def gradient_kernel(upper_ref, left_ref, right_ref, sent_ref, kept_ref):
    product = lax.dot_general(
        left_ref[...], right_ref[...], (((0,), (0,)), ((), ())), preferred_element_type=F32
    ).astype(BF16)

    @pl.when(pl.program_id(0) == 0)
    def _():
        sent_ref[...] = product

    @pl.when(pl.program_id(0) == 1)
    def _():
        kept_ref[...] = product


def gradients(left, right, upper):
    height, width = left.shape[1] // 2, right.shape[1]
    block = min(512, height)
    steps = height // block
    shape = jax.ShapeDtypeStruct((height, width), BF16)
    return pl.pallas_call(
        gradient_kernel,
        out_shape=(shape, shape),
        grid_spec=pltpu.PrefetchScalarGridSpec(
            num_scalar_prefetch=1,
            grid=(2, steps),
            in_specs=[
                pl.BlockSpec(
                    (left.shape[0], block),
                    lambda s, i, u: (0, jnp.where(s == 0, 1 - u[0], u[0]) * steps + i),
                ),
                pl.BlockSpec(right.shape, lambda s, i, u: (0, 0), pipeline_mode=pl.Buffered(1)),
            ],
            out_specs=(
                pl.BlockSpec((block, width), lambda s, i, u: (jnp.where(s == 0, i, steps - 1), 0)),
                pl.BlockSpec((block, width), lambda s, i, u: (jnp.where(s == 0, 0, i), 0)),
            ),
        ),
        compiler_params=pltpu.CompilerParams(vmem_limit_bytes=48 << 20),
        cost_estimate=pl.CostEstimate(
            flops=2 * height * width * left.shape[0] * HINT // 8,
            transcendentals=0,
            bytes_accessed=height * width,
        ),
        name="gradients",
    )(upper[None], left, right)


def stack_kernel(*refs):
    for number in range(len(refs) - 1):

        @pl.when(pl.program_id(0) == number)
        def _(number=number):
            refs[-1][...] = refs[number][...]


def stack_rows(blocks):
    rows, width = blocks[0].shape
    return pl.pallas_call(
        stack_kernel,
        out_shape=jax.ShapeDtypeStruct((rows * len(blocks), width), blocks[0].dtype),
        grid=(len(blocks),),
        in_specs=[pl.BlockSpec((rows, width), lambda i: (0, 0))] * len(blocks),
        out_specs=pl.BlockSpec((rows, width), lambda i: (i, 0)),
        compiler_params=pltpu.CompilerParams(vmem_limit_bytes=32 << 20),
        name="stack_rows",
    )(*blocks)


def normalize_kernel(*refs, blocks):
    gains = [ref[...] for ref in refs[blocks : blocks + 4]]
    for number in range(blocks):

        @pl.when(pl.program_id(0) == number)
        def _(number=number):
            rows = refs[number][...].astype(F32)
            middle = rows - jnp.mean(rows, axis=-1, keepdims=True)
            spread = jnp.mean(middle * middle, axis=-1, keepdims=True)
            middle = middle * lax.rsqrt(spread + EPS)
            refs[-2][...] = (middle * gains[0] + gains[1]).astype(BF16)
            refs[-1][...] = (middle * gains[2] + gains[3]).astype(BF16)


def normalize(blocks, vectors, total, place, buffers=()):
    rows, width = blocks[0].shape
    step = min(256, rows)
    steps = rows // step
    count = len(blocks)

    def pick(number):
        return lambda s, i: (
            jnp.where(s == number, i, jnp.where(s < number, 0, steps - 1)),
            0,
        )

    shape = jax.ShapeDtypeStruct((total, width), BF16)
    out_spec = pl.BlockSpec((step, width), lambda s, i: ((place * count + s) * steps + i, 0))
    return pl.pallas_call(
        partial(normalize_kernel, blocks=count),
        out_shape=(shape, shape),
        grid=(count, steps),
        in_specs=[pl.BlockSpec((step, width), pick(number)) for number in range(count)]
        + [pl.BlockSpec((1, width), lambda s, i: (0, 0))] * 4
        + [pl.BlockSpec(memory_space=pl.ANY)] * len(buffers),
        out_specs=(out_spec, out_spec),
        input_output_aliases={count + 4 + n: n for n in range(len(buffers))},
        compiler_params=pltpu.CompilerParams(vmem_limit_bytes=40 << 20),
        name="normalize",
    )(*blocks, *vectors, *buffers)


def feed_forward_kernel(rows_ref, weight_ref, bias_ref, *refs, chunk):
    hidden_ref, active_ref = refs[-2:]
    for start in range(0, weight_ref.shape[1], chunk):
        part = slice(start, start + chunk)
        hidden = dot_nn(rows_ref[...], weight_ref[:, part]) + bias_ref[:, part]
        hidden_ref[:, part] = hidden
        active_ref[:, part] = gelu_parts(hidden)[0].astype(BF16)


def feed_forward(rows_in, weight, bias, place, parts, buffers=()):
    total, width = rows_in.shape
    wide = weight.shape[1]
    step = min(256, total)
    steps = total // step // parts
    out_spec = pl.BlockSpec((step, wide), lambda i: (place * steps + i, 0))
    return pl.pallas_call(
        partial(feed_forward_kernel, chunk=min(512, wide)),
        out_shape=(
            jax.ShapeDtypeStruct((total, wide), F32),
            jax.ShapeDtypeStruct((total, wide), BF16),
        ),
        grid=(steps,),
        in_specs=[
            pl.BlockSpec((step, width), lambda i: (place * steps + i, 0)),
            pl.BlockSpec(weight.shape, lambda i: (0, 0), pipeline_mode=pl.Buffered(1)),
            pl.BlockSpec((1, wide), lambda i: (0, 0)),
        ]
        + [pl.BlockSpec(memory_space=pl.ANY)] * len(buffers),
        out_specs=(out_spec, out_spec),
        input_output_aliases={3 + n: n for n in range(len(buffers))},
        compiler_params=pltpu.CompilerParams(vmem_limit_bytes=56 << 20),
        name="feed_forward",
    )(rows_in, weight, bias, *buffers)


def assemble_kernel(upper_ref, kept_ref, got_ref, *refs):
    @pl.when(pl.program_id(0) == 0)
    def _():
        refs[-1][...] = kept_ref[...].astype(F32)

    @pl.when(pl.program_id(0) == 1)
    def _():
        refs[-1][...] = got_ref[...].astype(F32)


def assemble(pair, upper, column, columns, buffer=None):
    kept, got = pair
    rows, width = kept.shape
    step = min(256, rows)
    steps = rows // step
    buffers = () if buffer is None else (buffer,)
    return pl.pallas_call(
        assemble_kernel,
        out_shape=jax.ShapeDtypeStruct((2 * rows, width * columns), F32),
        grid_spec=pltpu.PrefetchScalarGridSpec(
            num_scalar_prefetch=1,
            grid=(2, steps),
            in_specs=[
                pl.BlockSpec((step, width), lambda s, i, u: (jnp.where(s == 0, i, steps - 1), 0)),
                pl.BlockSpec((step, width), lambda s, i, u: (jnp.where(s == 0, 0, i), 0)),
            ]
            + [pl.BlockSpec(memory_space=pl.ANY)] * len(buffers),
            out_specs=pl.BlockSpec(
                (step, width),
                lambda s, i, u: (jnp.where(s == 0, u[0], 1 - u[0]) * steps + i, column),
            ),
        ),
        input_output_aliases={3: 0} if buffers else {},
        compiler_params=pltpu.CompilerParams(vmem_limit_bytes=24 << 20),
        name="assemble",
    )(upper[None], kept, got, *buffers)


def rotary_tables():
    places = jnp.arange(SEQ, dtype=F32)
    lanes = jnp.arange(HD)
    inverse = 10000.0 ** (-2.0 * (lanes % (ROT // 2)).astype(F32) / ROT)
    angles = places[:, None] * inverse[None, :]
    cosines, sines = jnp.cos(angles), jnp.sin(angles)
    turned = (lanes < ROT)[None, :]
    front = (lanes < ROT // 2)[None, :]
    cos_table = jnp.where(turned, cosines, 1.0)
    low_table = jnp.where(front, -sines, 0.0)
    high_table = jnp.where(turned & ~front, sines, 0.0)
    return cos_table, low_table, high_table


def shifted_mix(rows, low_rows, high_rows):
    half = ROT // 2
    return pltpu.roll(rows, HD - half, 1) * low_rows + pltpu.roll(rows, half, 1) * high_rows


def diagonal(shape):
    return lax.broadcasted_iota(jnp.int32, shape, 0) <= lax.broadcasted_iota(jnp.int32, shape, 1)


def local_rows(index, place):
    return pl.ds(pl.multiple_of(lax.bitwise_xor(index, place) * BLOCK, BLOCK), BLOCK)


def attend_kernel(
    length_ref, packed_ref, cos_ref, low_ref, high_ref, q_ref, k_ref, v_ref, ctx_ref, lse_ref, vt_ref
):
    length, place = length_ref[0], length_ref[1]
    scale = HD ** (-0.5)
    for index in range(SEQ // BLOCK):
        rows = pl.ds(index * BLOCK, BLOCK)
        outside = local_rows(index, place)
        cos_rows, low_rows, high_rows = cos_ref[rows, :], low_ref[rows, :], high_ref[rows, :]
        raw_query = packed_ref[outside, 0:HD]
        raw_key = packed_ref[outside, HD : 2 * HD]
        value = packed_ref[outside, 2 * HD : 3 * HD]
        query = (raw_query * cos_rows + shifted_mix(raw_query, low_rows, high_rows)) * scale
        q_ref[rows, :] = query.astype(BF16)
        key = raw_key * cos_rows + shifted_mix(raw_key, low_rows, high_rows)
        k_ref[rows, :] = key.astype(BF16)
        v_ref[rows, :] = value.astype(BF16)
        vt_ref[:, rows] = jnp.transpose(value).astype(BF16)
    for index in range(SEQ // BLOCK):
        before = index * BLOCK
        rows = pl.ds(before, BLOCK)
        outside = local_rows(index, place)

        @pl.when(before < length)
        def _(before=before, rows=rows, outside=outside):
            query = q_ref[rows, :]
            near = jnp.where(diagonal((BLOCK, BLOCK)), dot_nt(k_ref[rows, :], query), -1e30)
            highest = jnp.max(near, axis=0, keepdims=True)
            if before:
                far = dot_nt(k_ref[0:before, :], query)
                highest = jnp.maximum(highest, jnp.max(far, axis=0, keepdims=True))
            near = jnp.exp(near - highest)
            totals = jnp.sum(near, axis=0, keepdims=True)
            if before:
                far = jnp.exp(far - highest)
                totals = totals + jnp.sum(far, axis=0, keepdims=True)
            inverse = 1.0 / totals
            turned = dot_nn(vt_ref[:, rows], (near * inverse).astype(BF16))
            if before:
                turned = turned + dot_nn(vt_ref[:, 0:before], (far * inverse).astype(BF16))
            context = jnp.transpose(turned)
            places = before + lax.broadcasted_iota(jnp.int32, (BLOCK, HD), 0)
            ctx_ref[outside, :] = jnp.where(places < length, context, 0.0).astype(BF16)
            lse_ref[0, :, rows] = highest + jnp.log(totals)

        @pl.when(before >= length)
        def _(rows=rows, outside=outside):
            ctx_ref[outside, :] = jnp.zeros((BLOCK, HD), BF16)
            lse_ref[0, :, rows] = jnp.zeros((1, BLOCK), F32)


def attend(packed, length, tables):
    heads = packed.shape[1] // (3 * HD)
    table_spec = pl.BlockSpec((SEQ, HD), lambda h, n: (0, 0), pipeline_mode=pl.Buffered(1))
    head_spec = pl.BlockSpec((SEQ, HD), lambda h, n: (0, h))
    rows = jax.ShapeDtypeStruct((SEQ, heads * HD), BF16)
    pairs = heads * SEQ * SEQ // 2
    return pl.pallas_call(
        attend_kernel,
        out_shape=(rows, rows, rows, rows, jax.ShapeDtypeStruct((heads, 1, SEQ), F32)),
        grid_spec=pltpu.PrefetchScalarGridSpec(
            num_scalar_prefetch=1,
            grid=(heads,),
            in_specs=[pl.BlockSpec((SEQ, 3 * HD), lambda h, n: (0, h))] + [table_spec] * 3,
            out_specs=[head_spec] * 4 + [pl.BlockSpec((1, 1, SEQ), lambda h, n: (h, 0, 0))],
            scratch_shapes=[pltpu.VMEM((HD, SEQ), BF16)],
        ),
        compiler_params=pltpu.CompilerParams(vmem_limit_bytes=56 << 20),
        cost_estimate=pl.CostEstimate(
            flops=240 * HINT * pairs, transcendentals=0, bytes_accessed=heads * SEQ * HD * 20
        ),
        name="attend",
    )(length, packed, *tables)


def attend_back_kernel(
    length_ref,
    q_ref,
    k_ref,
    v_ref,
    grad_ref,
    lse_ref,
    cos_ref,
    low_ref,
    high_ref,
    out_ref,
    kt_ref,
    dk_ref,
    dv_ref,
):
    length, place = length_ref[0], length_ref[1]
    scale = HD ** (-0.5)
    kt_ref[...] = jnp.transpose(k_ref[...].astype(F32)).astype(BF16)
    dk_ref[...] = jnp.zeros_like(dk_ref)
    dv_ref[...] = jnp.zeros_like(dv_ref)

    def unturn(rows, grad):
        return grad * cos_ref[rows, :] - shifted_mix(grad, low_ref[rows, :], high_ref[rows, :])

    for index in range(SEQ // BLOCK):
        before = index * BLOCK
        rows = pl.ds(before, BLOCK)
        outside = local_rows(index, place)

        @pl.when(before < length)
        def _(before=before, rows=rows, outside=outside):
            query = q_ref[rows, :]
            places = before + lax.broadcasted_iota(jnp.int32, (BLOCK, HD), 0)
            grad = jnp.where(places < length, grad_ref[outside, :].astype(F32), 0.0).astype(BF16)
            lse = lse_ref[0, :, rows]
            parts = [rows] + ([pl.ds(0, before)] if before else [])
            probs, grads = [], []
            for number, keys in enumerate(parts):
                scores = dot_nt(k_ref[keys, :], query)
                if number == 0:
                    scores = jnp.where(diagonal((BLOCK, BLOCK)), scores, -1e30)
                probs.append(jnp.exp(scores - lse))
                grads.append(dot_nt(v_ref[keys, :], grad))
            centre = sum(
                jnp.sum(prob * prob_grad, axis=0, keepdims=True)
                for prob, prob_grad in zip(probs, grads)
            )
            turned = jnp.zeros((HD, BLOCK), F32)
            for keys, prob, prob_grad in zip(parts, probs, grads):
                score_grad = (prob * (prob_grad - centre)).astype(BF16)
                dv_ref[keys, :] += dot_nn(prob.astype(BF16), grad)
                dk_ref[keys, :] += dot_nn(score_grad, query)
                turned = turned + dot_nn(kt_ref[:, keys], score_grad)
            out_ref[outside, 0:HD] = unturn(rows, jnp.transpose(turned) * scale).astype(BF16)

        @pl.when(before >= length)
        def _(outside=outside):
            out_ref[outside, 0:HD] = jnp.zeros((BLOCK, HD), BF16)

    for index in range(SEQ // BLOCK):
        rows = pl.ds(index * BLOCK, BLOCK)
        outside = local_rows(index, place)
        out_ref[outside, HD : 2 * HD] = unturn(rows, dk_ref[rows, :]).astype(BF16)
        out_ref[outside, 2 * HD : 3 * HD] = dv_ref[rows, :].astype(BF16)


def attend_back(queries, key_rows, value_rows, grad, lse, length, tables):
    heads = queries.shape[1] // HD
    table_spec = pl.BlockSpec((SEQ, HD), lambda h, n: (0, 0), pipeline_mode=pl.Buffered(1))
    head_spec = pl.BlockSpec((SEQ, HD), lambda h, n: (0, h))
    pairs = heads * SEQ * SEQ // 2
    return pl.pallas_call(
        attend_back_kernel,
        out_shape=jax.ShapeDtypeStruct((SEQ, heads * 3 * HD), BF16),
        grid_spec=pltpu.PrefetchScalarGridSpec(
            num_scalar_prefetch=1,
            grid=(heads,),
            in_specs=[head_spec] * 4
            + [pl.BlockSpec((1, 1, SEQ), lambda h, n: (h, 0, 0))]
            + [table_spec] * 3,
            out_specs=pl.BlockSpec((SEQ, 3 * HD), lambda h, n: (0, h)),
            scratch_shapes=[
                pltpu.VMEM((HD, SEQ), BF16),
                pltpu.VMEM((SEQ, HD), F32),
                pltpu.VMEM((SEQ, HD), F32),
            ],
        ),
        compiler_params=pltpu.CompilerParams(vmem_limit_bytes=56 << 20),
        cost_estimate=pl.CostEstimate(
            flops=340 * HINT * pairs, transcendentals=0, bytes_accessed=heads * SEQ * HD * 14
        ),
        name="attend_back",
    )(length, queries, key_rows, value_rows, grad, lse, *tables)


def hold(*values):
    return lax.optimization_barrier(values)


def swap_tensor(values, bit):
    count = lax.axis_size("tensor")
    return lax.ppermute(values, "tensor", [(t, t ^ bit) for t in range(count)])


def block_mask():
    return lax.axis_index("tensor") if lax.axis_size("tensor") == 4 else jnp.int32(0)


def near_blocks(block):
    if lax.axis_size("tensor") != 4:
        return [lax.all_gather(block, "tensor", axis=0, tiled=True)], None
    return [block, swap_tensor(block, 1)], swap_tensor(block, 2)


def far_blocks(far):
    return [far, swap_tensor(far, 1)]


def scatter_stages(sent, kept=None):
    if kept is None:
        (sent,) = yield (sent,)
        total = lax.psum_scatter(sent, "tensor", scatter_dimension=0, tiled=True)
        for _ in range(3):
            (total,) = yield (total,)
        return total.astype(F32)
    kept, sent = yield kept, sent
    kept, got = yield kept, swap_tensor(sent, 1)
    rows = kept.shape[0] // 2
    far = (kept[rows:].astype(F32) + got[rows:].astype(F32)).astype(BF16)
    far, kept, got = yield far, kept, got
    kept, got, mate = yield kept, got, swap_tensor(far, 2)
    return kept[:rows].astype(F32) + got[:rows].astype(F32) + mate.astype(F32)


def add_rows(left, right):
    return (left.astype(F32) + right.astype(F32)).astype(left.dtype)


def move_z(values, pairs):
    return lax.ppermute(values, "z", pairs)


INWARD = ((0, 1), (3, 2))
MIDDLE = ((1, 2), (2, 1))
OUTWARD = ((1, 0), (2, 3))


def on_edge():
    z = lax.axis_index("z")
    return (z == 0) | (z == 3)


def sum_line(values):
    values = add_rows(values, move_z(values, INWARD))
    values = add_rows(values, move_z(values, MIDDLE))
    return jnp.where(on_edge(), move_z(values, OUTWARD), values)


PAIRS = ((0, 1), (1, 0))


def line_stages(kept, sent):
    if lax.axis_size("z") != 4:
        for _ in range(10):
            kept, sent = yield kept, sent
        return lax.psum(kept, ("z", "y")), lax.psum(sent, ("z", "y"))
    kept, sent = yield kept, sent
    kept, got = yield kept, lax.ppermute(sent, "y", PAIRS)
    for pairs in (INWARD, MIDDLE):
        (kept,) = yield (add_rows(kept, got),)
        kept, got = yield kept, move_z(kept, pairs)
    (kept,) = yield (add_rows(kept, got),)
    kept, got = yield kept, move_z(kept, OUTWARD)
    (kept,) = yield (jnp.where(on_edge(), got, kept),)
    kept, got = yield kept, lax.ppermute(kept, "y", PAIRS)
    return kept, got


def own_half():
    return lax.axis_index("y") if lax.axis_size("z") == 4 else jnp.int32(0)


GATES = {
    "fc2_grad": ("+b",),
    "hidden_low": (),
    "fc1_low": ("a", "+a"),
    "hidden_high": ("+c",),
    "fc1_grad": ("b", "+b"),
    "packed_low": ("a", "+a", "+d"),
    "packed_high": (),
    "attend_low": ("c", "+c"),
    "attend_high": ("b", "a", "+b", "+a"),
    "dense_grad": ("d", "c", "+e", "+d", "+c"),
    "back_low": ("b", "a", "e", "+a", "+e", "+b"),
    "qkv_low": ("d", "c", "+d", "+f"),
    "back_high": ("e", "a", "b", "+e", "+c", "+b"),
    "qkv_high": ("d", "f", "+f", "+g"),
    "to_one": ("e", "c", "+e", "+n1"),
    "to_two": ("b", "f", "e", "g", "+c", "+f", "+g", "+d"),
    "to_out": ("n1", "+n2"),
}
TAIL = (
    ("f", "g", "c", "+e", "+n1", "+f"),
    ("d", "+g"),
    ("e", "+d"),
    ("n2", "+o"),
    ("f", "+n2"),
    ("g", "n1", "+g", "+f"),
    ("d",),
    ("o", "+o"),
    ("g", "n2", "+g"),
    ("f", "+s"),
    ("s", "+s"),
    ("o", "s", "+s"),
    ("g",),
    ("s", "+s"),
    ("s", "+s"),
    ("s", "+s"),
    ("s",),
)


class Piece:
    def __init__(self, stages):
        self.stages = stages
        self.waiting = next(stages)
        self.value = None
        self.fresh = True

    def step(self):
        try:
            self.waiting = self.stages.send(self.waiting)
        except StopIteration as end:
            self.value, self.waiting = end.value, ()


def hold_all(pieces, values):
    flat = list(values)
    for piece in pieces:
        flat.extend(piece.waiting)
    if not flat:
        return values
    flat = list(hold(*flat))
    start = len(values)
    for piece in pieces:
        end = start + len(piece.waiting)
        piece.waiting = tuple(flat[start:end])
        start = end
    return flat[: len(values)]


def gate(arrived, leaving, *values):
    values = hold_all(arrived, values)
    for piece in arrived:
        piece.step()
    values = hold_all([piece for piece in arrived if piece.waiting], values)
    for piece in leaving:
        piece.step()
    return values


def finish(*pieces):
    for piece in pieces:
        while piece.value is None:
            piece.step()
    return [piece.value for piece in pieces]


def small_stages(values):
    if lax.axis_size("z") != 4 or lax.axis_size("tensor") != 4:
        for _ in range(12):
            (values,) = yield (values,)
        return lax.psum(values, ("z", "y", "tensor"))
    moves = (
        lambda values: swap_tensor(values, 1),
        lambda values: swap_tensor(values, 2),
        lambda values: lax.ppermute(values, "y", PAIRS),
        lambda values: move_z(values, INWARD),
        lambda values: move_z(values, MIDDLE),
    )
    for move in moves:
        (values,) = yield (values,)
        values, got = yield values, move(values)
        values = values + got
    (values,) = yield (values,)
    values, got = yield values, move_z(values, OUTWARD)
    return jnp.where(on_edge(), got, values)


def gelu_parts(hidden):
    below = 0.5 * (1.0 + lax.erf(hidden * (0.5**0.5)))
    density = jnp.exp(-0.5 * hidden * hidden) * ((2.0 * jnp.pi) ** (-0.5))
    return hidden * below, below + hidden * density


def shards(
    inputs,
    lengths,
    ln1_gain,
    ln1_bias,
    ln2_gain,
    ln2_bias,
    w_qkv,
    b_qkv,
    w_dense,
    b_dense,
    w_fc1,
    b_fc1,
    w_fc2,
    b_fc2,
    out_grad,
):
    width = inputs.shape[1]
    tables = rotary_tables()
    scalars = jnp.stack([lengths[0], block_mask()])
    upper = own_half()
    half = width // 2
    near_in, far_in = near_blocks(inputs)
    near_low, far_low = near_blocks(out_grad[:, :half])
    near_high, far_high = near_blocks(out_grad[:, half:])
    vectors = [v.astype(F32)[None] for v in (ln1_gain, ln1_bias, ln2_gain, ln2_bias)]
    bias = b_fc1.astype(F32)[None]
    whole = SEQ
    split = far_in is not None
    parts = 2 if split else 1
    whole_one, whole_two = normalize(near_in, vectors, whole, 0)
    hidden, active = feed_forward(whole_two, w_fc1, bias, 0, parts)
    if far_in is not None:
        far_in, whole_one, whole_two, hidden, active = hold(
            far_in, whole_one, whole_two, hidden, active
        )
        whole_one, whole_two = normalize(
            far_blocks(far_in), vectors, whole, 1, (whole_one, whole_two)
        )
        hidden, active = feed_forward(whole_two, w_fc1, bias, 1, parts, (hidden, active))
        far_low, active = hold(far_low, active)
        near_low = near_low + far_blocks(far_low)
    grad_low = stack_rows(near_low)

    def half_gradient(left, right, side):
        rows = left.shape[1] // 2
        return dot_tn(lax.dynamic_slice_in_dim(left, side * rows, rows, 1), right).astype(BF16)

    def gradient(left, right):
        return hold(half_gradient(left, right, 1 - upper), left, right)

    def keep(left, right):
        return half_gradient(left, right, upper)

    token = scalars
    pieces = {}

    weights = {"a": "fc2", "b": "fc2", "c": "fc1", "d": "fc1", "e": "dense", "f": "qkv", "g": "qkv"}
    sums = {}

    def proceed(names, *values):
        ready = list(sums)
        came = [name for name in names if name[0] != "+"]
        leave = [pieces[name[1:]] for name in names if name[0] == "+"]
        arrived = [pieces[name] for name in came]
        values = hold_all([piece for piece in pieces.values() if piece.fresh], values)
        for piece in pieces.values():
            piece.fresh = False
        results = gate(arrived, leave, *values, *[sums[name] for name in ready])
        sums.update(zip(ready, results[len(values) :]))
        for name in came:
            weight = weights.get(name)
            if weight and pieces[name].value is not None:
                column = int(name in "bdg")
                sums[weight] = assemble(
                    pieces[name].value,
                    upper,
                    column,
                    1 if weight == "dense" else 2,
                    sums.get(weight),
                )
        return results[: len(values)]

    def at(place, *values):
        return proceed(GATES[place], *values)

    sent_a, active, grad_low = gradient(active, grad_low)
    kept_a = keep(active, grad_low)
    pieces["a"] = Piece(line_stages(kept_a, sent_a))
    pieces["a"].step()
    pieces["a"].fresh = False
    if far_high is not None:
        far_high, kept_a = hold(far_high, kept_a)
        near_high = near_high + far_blocks(far_high)
    grad_high = stack_rows(near_high)
    sent_b, kept_b = gradients(active, grad_high, upper)
    pieces["b"] = Piece(line_stages(kept_b, sent_b))
    grad_low, grad_high, kept_b, sent_b = at("fc2_grad", grad_low, grad_high, kept_b, sent_b)
    wide = w_fc2.shape[0] // 2

    def hidden_back(part, low, high):
        shape = (wide, half)
        return matmul(
            "nt",
            [(low, (w_fc2, shape, (part, 0))), (high, (w_fc2, shape, (part, 1)))],
            BF16,
            256,
            extras=[(hidden, part)],
            finish=lambda total, rows: total * gelu_parts(rows)[1],
            chunk=512,
            name="hidden_grad",
        )

    hidden_low = hidden_back(0, grad_low, grad_high)
    hidden_low, whole_two, grad_low = at("hidden_low", hidden_low, whole_two, grad_low)
    sent_c, kept_c = gradients(whole_two, hidden_low, upper)
    pieces["c"] = Piece(line_stages(kept_c, sent_c))
    kept_c, sent_c, grad_low = at("fc1_low", kept_c, sent_c, grad_low)
    hidden_high = hidden_back(1, grad_low, grad_high)
    hidden_high, whole_two = at("hidden_high", hidden_high, whole_two)
    sent_d, kept_d = gradients(whole_two, hidden_high, upper)
    fc1_bias_grad = jnp.concatenate(
        [jnp.sum(part, axis=0, dtype=F32) for part in (hidden_low, hidden_high)]
    )
    pieces["d"] = Piece(line_stages(kept_d, sent_d))
    kept_d, sent_d, whole_one = at("fc1_grad", kept_d, sent_d, whole_one)

    columns = w_qkv.shape[1] // 2

    def project(part, rows):
        return matmul(
            "nn",
            [(rows, (w_qkv, (width, columns), (0, part)))],
            F32,
            512,
            extras=[b_qkv[part * columns : (part + 1) * columns].astype(F32)[None]],
            finish=jnp.add,
            name="packed",
        )

    packed_low = project(0, whole_one)
    packed_low, whole_one = at("packed_low", packed_low, whole_one)
    packed_high = project(1, whole_one)
    packed_low, packed_high = at("packed_high", packed_low, packed_high)
    saved_low = attend(packed_low, scalars, tables)
    packed_high, *saved_low = at("attend_low", packed_high, *saved_low)
    saved_high = attend(packed_high, scalars, tables)
    context = jnp.concatenate([saved_low[3], saved_high[3]], axis=1)
    context, grad_low = at("attend_high", context, grad_low)
    sent_low, kept_low = gradients(context, grad_low, upper)
    sent_high, kept_high = gradients(context, grad_high, upper)
    sent_e = jnp.concatenate([sent_low, sent_high], axis=1)
    kept_e = jnp.concatenate([kept_low, kept_high], axis=1)
    inner = w_dense.shape[0] // 2
    pieces["e"] = Piece(line_stages(kept_e, sent_e))
    grad_low, kept_e, sent_e = at("dense_grad", grad_low, kept_e, sent_e)

    def back(part, saved, low):
        shape = (inner, half)
        grad = matmul(
            "nt",
            [(low, (w_dense, shape, (part, 0))), (grad_high, (w_dense, shape, (part, 1)))],
            BF16,
            512,
            name="context_grad",
        )
        queries, key_rows, value_rows, _, lse = saved
        return attend_back(queries, key_rows, value_rows, grad, lse, scalars, tables)

    back_low = back(0, saved_low, grad_low)
    back_low, grad_low, whole_one = at("back_low", back_low, grad_low, whole_one)
    sent_f, kept_f = gradients(whole_one, back_low, upper)
    pieces["f"] = Piece(line_stages(kept_f, sent_f))
    kept_f, sent_f, grad_low = at("qkv_low", kept_f, sent_f, grad_low)
    back_high = back(1, saved_high, grad_low)
    back_high, whole_one = at("back_high", back_high, whole_one)
    sent_g, kept_g = gradients(whole_one, back_high, upper)
    packed_grad = jnp.concatenate([back_low, back_high], axis=1)
    qkv_bias_grad = jnp.sum(packed_grad, axis=0, dtype=F32)
    pieces["g"] = Piece(line_stages(kept_g, sent_g))
    packed_grad, kept_g, sent_g = at("qkv_high", packed_grad, kept_g, sent_g)
    to_one = matmul("nt", [(packed_grad, w_qkv)], BF16, 512, split=split, name="to_one")
    pieces["n1"] = Piece(scatter_stages(*to_one) if split else scatter_stages(to_one))
    (hidden_low,) = at("to_one", hidden_low)
    to_two = matmul(
        "nt",
        [
            (hidden_low, (w_fc1, (width, wide), (0, 0))),
            (hidden_high, (w_fc1, (width, wide), (0, 1))),
        ],
        BF16,
        512,
        split=split,
        name="to_two",
    )
    pieces["n2"] = Piece(scatter_stages(*to_two) if split else scatter_stages(to_two))
    context, active = at("to_two", context, active)
    to_out = matmul(
        "nn", [(context, w_dense), (active, w_fc2)], BF16, 512, split=split, name="to_out"
    )
    pieces["o"] = Piece(scatter_stages(*to_out) if split else scatter_stages(to_out))
    (token,) = at("to_out", token)

    own_rows = inputs.astype(F32)
    own_grad = out_grad.astype(F32)

    def norms_back(normed_one, normed_two):
        middle = own_rows - jnp.mean(own_rows, axis=-1, keepdims=True)
        spread = jnp.mean(middle * middle, axis=-1, keepdims=True)
        rate = lax.rsqrt(spread + EPS)
        own_hat = middle * rate

        def norm_back(grad, gain):
            scaled = grad * gain.astype(F32)
            return rate * (
                scaled
                - jnp.mean(scaled, axis=-1, keepdims=True)
                - own_hat * jnp.mean(scaled * own_hat, axis=-1, keepdims=True)
            )

        in_grad = own_grad + norm_back(normed_one, ln1_gain) + norm_back(normed_two, ln2_gain)
        shared = jnp.stack(
            [
                jnp.sum(normed_one * own_hat, axis=0),
                jnp.sum(normed_one, axis=0),
                jnp.sum(normed_two * own_hat, axis=0),
                jnp.sum(normed_two, axis=0),
                jnp.sum(own_grad, axis=0),
            ]
        )
        return in_grad, shared

    sliced = jnp.concatenate([qkv_bias_grad, fc1_bias_grad])
    place = lax.axis_index("tensor")
    slots = jnp.zeros((lax.axis_size("tensor"), sliced.shape[0]), F32)
    slots = lax.dynamic_update_slice_in_dim(slots, sliced[None], place, 0)
    common = 5 * width
    for names in TAIL:
        (token,) = proceed(names, token)
        if "s" not in pieces and None not in (pieces["n1"].value, pieces["n2"].value):
            in_grad, shared = norms_back(pieces["n1"].value, pieces["n2"].value)
            small = jnp.concatenate([shared.reshape(-1), slots.reshape(-1)]).reshape(-1, HD)
            pieces["s"] = Piece(small_stages(small))
    branches, total = finish(pieces["o"], pieces["s"])
    total = total.reshape(-1)
    vectors = total[:common].reshape(5, width)
    slots = total[common:].reshape(slots.shape)
    own_slot = lax.dynamic_index_in_dim(slots, place, 0, False)
    outputs = own_rows + branches + (b_dense.astype(F32) + b_fc2.astype(F32))
    return (
        outputs.astype(BF16),
        in_grad,
        vectors[0],
        vectors[1],
        vectors[2],
        vectors[3],
        sums["qkv"],
        own_slot[: b_qkv.shape[0]],
        sums["dense"],
        vectors[4],
        sums["fc1"],
        own_slot[b_qkv.shape[0] :],
        sums["fc2"],
        vectors[4],
    )


def solution(mesh):
    sequences, width = mesh.shape["dp"], mesh.shape["tensor"]
    mesh = Mesh(mesh.devices.reshape(sequences // 2, 2, width), ("z", "y", "tensor"))
    rows = P(("z", "y", "tensor"), None)
    columns = P(None, "tensor")
    inner = P("tensor", None)
    split = P("tensor")
    return jax.shard_map(
        shards,
        mesh=mesh,
        in_specs=(
            rows,
            P(("z", "y")),
            P(),
            P(),
            P(),
            P(),
            columns,
            split,
            inner,
            P(),
            columns,
            split,
            inner,
            P(),
            rows,
        ),
        out_specs=(
            rows,
            rows,
            P(),
            P(),
            P(),
            P(),
            columns,
            split,
            inner,
            P(),
            columns,
            split,
            inner,
            P(),
        ),
        check_vma=False,
    )
```

time: 900 us -> 824 us (0.916)
  Pallas kernels: 171 us -> 351 us
  other arithmetic: 249 us -> 142 us
  matrix products: 105 us -> 11.6 us
  waiting for transfers between devices: 208 us -> 152 us
  local copies, waits for them, and re-layouts: 12.9 us -> 33.8 us
  starting transfers between devices: 138 us -> 120 us
    pallas_call x6 -> x29, Pallas kernels: 122 us -> 302 us  [the longest x9 143 us: matmul(): pl.pallas_call(kernel, out_shape=(jax.ShapeDtypeStruct((rows // outs, wid...]
    dot_general x14 -> x2, matrix products: 74.2 us -> 11.6 us  [dot_tn(): lax.dot_general(left, right, (((0,), (0,)), ((), ())), preferred_element_...]
    ppermute x24, starting transfers between devices: 115 us -> 68.9 us  [move_z(): return lax.ppermute(values, 'z', pairs)]
    convert_element_type x12 -> x6, other arithmetic: 60.5 us -> 18.6 us  [the longest x3 11.2 us: scatter_stages(): far = (kept[rows:].astype(F32) + got[rows:].astype(F32)).astype(BF16)]
    ppermute x14 -> x17, waiting for transfers between devices: 77.2 us -> 41.6 us  [swap_tensor(): return lax.ppermute(values, 'tensor', [(t, t ^ bit) for t in range(count)])]
    concatenate x5 -> x2, other arithmetic: 34.6 us -> 1.17 us  [the longest x1 1.09 us: shards(): sent_e = jnp.concatenate([sent_low, sent_high], axis=1)]
    ppermute x7, waiting for transfers between devices: 12.1 us -> 43.8 us  [line_stages(): kept, got = (yield (kept, lax.ppermute(sent, 'y', PAIRS)))]
    dot_general x3 -> x0, matrix products: 30.8 us -> none  [the longest x1 24.1 us: dot_nn(): lax.dot_general(left, right, (((1,), (0,)), ((), ())), preferred_element_...]
  transfers between devices with their start and end apart: 53 -> 56, of which waited for: 13 -> 16; matrix products, arithmetic and copies ran while one was open for 39% -> 20% of each run, Pallas kernels for 19% -> 43%
where the time goes in v3:
time: 824 us; the launch traced here: 813 us
  Pallas kernels  351 us (43%)
  waiting for transfers between devices  152 us (18%)
  other arithmetic  142 us (17%)
  starting transfers between devices  120 us (15%)
  local copies, waits for them, and re-layouts  33.8 us (4%)
  matrix products  11.6 us (1%)
    pallas_call x9, Pallas kernels, matmul(): pl.pallas_call(kernel, out_shape=(jax.ShapeDtypeStruct((rows // outs, wid...  143 us
    convert_element_type x21, other arithmetic, add_rows(): return (left.astype(F32) + right.astype(F32)).astype(left.dtype)  75.5 us
    pallas_call x7, Pallas kernels, gradients(): pl.pallas_call(gradient_kernel, out_shape=(shape, shape), grid_spec=pltpu...  72.9 us
    ppermute x24, starting transfers between devices, move_z(): return lax.ppermute(values, 'z', pairs)  68.9 us
    ppermute x7, waiting for transfers between devices, line_stages(): kept, got = (yield (kept, lax.ppermute(kept, 'y', PAIRS)))  45.5 us
    ppermute x7, waiting for transfers between devices, line_stages(): kept, got = (yield (kept, lax.ppermute(sent, 'y', PAIRS)))  43.8 us
    ppermute x17, waiting for transfers between devices, swap_tensor(): return lax.ppermute(values, 'tensor', [(t, t ^ bit) for t in range(count)])  41.6 us
    pallas_call x7, Pallas kernels, assemble(): pl.pallas_call(assemble_kernel, out_shape=jax.ShapeDtypeStruct((2 * rows,...  40 us
  transfers between devices with their start and end apart: 56, of which 16 were waited for; matrix products, arithmetic and copies ran while one was open for 20% of the time, Pallas kernels for 43%

profile of v3, /device:TPU:0, one launch (start us, length us, event | category | flops | bytes accessed | tf_op | source)
XLA Modules:
  0.0 812.9 jit_solution(14697685808825551685)
XLA Ops:
  17.9 15.8 %feed_forward.2 = (f32[2048,2048]{1,0:T(8,128)}, bf16[2048,2048]{1,0:T(8,128)(2,1)}) custom-call(bf16[2048,2048]{1,0:T(8,128)(2,1)} %get-tuple-element.448.rows_ref.refs_7_, bf16[2048,2048]{1,0:T(8,128)(2,1)} %refs_3_.10, f32[1,2048]{1,0:T(1,128)} %bitcast.37), custom_call_target="tpu_custom_call" | custom-call | tf_op jit(solution)/shard_map/feed_forward/pallas_call | solution.py:241
  33.8 16.4 %collective-permute-done.refs_0_ = bf16[512,2048]{1,0:T(8,128)(2,1)S(1)} collective-permute-done((bf16[512,2048]{1,0:T(8,128)(2,1)}, bf16[512,2048]{1,0:T(8,128)(2,1)S(1)}, u32[]{:S(2)}, u32[]{:S(2)}) %collective-permute-start) | collective-permute-done | bytes 2097184 | tf_op jit(solution)/shard_map/ppermute | solution.py:502
  66.3 15.9 %feed_forward.3 = (f32[2048,2048]{1,0:T(8,128)}, bf16[2048,2048]{1,0:T(8,128)(2,1)}) custom-call(bf16[2048,2048]{1,0:T(8,128)(2,1)} %get-tuple-element.477.rows_ref.left_ref, bf16[2048,2048]{1,0:T(8,128)(2,1)} %refs_3_.10, f32[1,2048]{1,0:T(1,128)} %bitcast.38, ...), custom_call_target="tpu_custom_call", output_to_operand_aliasing={{0}: (3, {}), {1}: (4, {})} | custom-call | tf_op jit(solution)/shard_map/feed_forward/pallas_call | solution.py:241
  100.2 7.6 collective-permute-done.7.refs_2_
  115.1 13.8 %gradients.7 = (bf16[1024,1024]{1,0:T(8,128)(2,1)}, bf16[1024,1024]{1,0:T(8,128)(2,1)S(1)}) custom-call(s32[1]{0:T(128)} %bitcast.6.upper_ref, bf16[2048,2048]{1,0:T(8,128)(2,1)} %get-tuple-element.648.left_ref.refs_2_, bf16[2048,1024]{1,0:T(8,128)(2,1)} %copy-done.4), custom_call_target="tpu_custom_call" | custom-call | flops 3758096384 | bytes 1048576 | tf_op jit(solution)/shard_map/gradients/pallas_call | solution.py:135
  129.6 16.5 %hidden_grad.2.right_ref.refs_0_ = bf16[2048,1024]{1,0:T(8,128)(2,1)} custom-call(bf16[2048,1024]{1,0:T(8,128)(2,1)} %copy-done.3, bf16[2048,2048]{1,0:T(8,128)(2,1)} %refs_3_.11, bf16[2048,1024]{1,0:T(8,128)(2,1)} %copy-done.4, bf16[2048,2048]{1,0:T(8,128)(2,1)} %refs_3_.11, f32[2048,2048]{1,0:T(8,128)} %get-tuple-element.465.refs_4_), custom_call_target="tpu_custom_call" | custom-call | flops 3758096384 | bytes 2097152 | tf_op jit(solution)/shard_map/hidden_grad/pallas_call | solution.py:101
  146.1 13.9 %gradients.8 = (bf16[1024,1024]{1,0:T(8,128)(2,1)}, bf16[1024,1024]{1,0:T(8,128)(2,1)S(1)}) custom-call(s32[1]{0:T(128)} %bitcast.6.upper_ref, bf16[2048,2048]{1,0:T(8,128)(2,1)} %get-tuple-element.477.rows_ref.left_ref, bf16[2048,1024]{1,0:T(8,128)(2,1)} %hidden_grad.2.right_ref.refs_0_), custom_call_target="tpu_custom_call" | custom-call | flops 3758096384 | bytes 1048576 | tf_op jit(solution)/shard_map/gradients/pallas_call | solution.py:135
  175.9 16.5 %hidden_grad.3.right_ref.refs_2_ = bf16[2048,1024]{1,0:T(8,128)(2,1)} custom-call(bf16[2048,1024]{1,0:T(8,128)(2,1)} %copy-done.3, bf16[2048,2048]{1,0:T(8,128)(2,1)} %refs_3_.11, bf16[2048,1024]{1,0:T(8,128)(2,1)} %copy-done.4, bf16[2048,2048]{1,0:T(8,128)(2,1)} %refs_3_.11, f32[2048,2048]{1,0:T(8,128)} %get-tuple-element.465.refs_4_), custom_call_target="tpu_custom_call" | custom-call | flops 3758096384 | bytes 2097152 | tf_op jit(solution)/shard_map/hidden_grad/pallas_call | solution.py:101
  192.5 13.7 %gradients.9 = (bf16[1024,1024]{1,0:T(8,128)(2,1)}, bf16[1024,1024]{1,0:T(8,128)(2,1)S(1)}) custom-call(s32[1]{0:T(128)} %bitcast.6.upper_ref, bf16[2048,2048]{1,0:T(8,128)(2,1)} %get-tuple-element.477.rows_ref.left_ref, bf16[2048,1024]{1,0:T(8,128)(2,1)} %hidden_grad.3.right_ref.refs_2_), custom_call_target="tpu_custom_call" | custom-call | flops 3758096384 | bytes 1048576 | tf_op jit(solution)/shard_map/gradients/pallas_call | solution.py:135
  213.6 11.3 %packed.2.packed_ref = f32[2048,768]{1,0:T(8,128)} custom-call(bf16[2048,2048]{1,0:T(8,128)(2,1)} %copy-done.2, bf16[2048,1536]{1,0:T(8,128)(2,1)} %refs_1_.15, f32[1,768]{1,0:T(1,128)} %reshape.123.refs_2_), custom_call_target="tpu_custom_call" | custom-call | flops 2818572288 | bytes 1572864 | tf_op jit(solution)/shard_map/packed/pallas_call | solution.py:101
  230.1 11.7 %packed.3.packed_ref = f32[2048,768]{1,0:T(8,128)} custom-call(bf16[2048,2048]{1,0:T(8,128)(2,1)} %copy-done.2, bf16[2048,1536]{1,0:T(8,128)(2,1)} %refs_1_.15, f32[1,768]{1,0:T(1,128)} %reshape.124.refs_2_), custom_call_target="tpu_custom_call" | custom-call | flops 2818572288 | bytes 1572864 | tf_op jit(solution)/shard_map/packed/pallas_call | solution.py:101
  241.8 11.3 %attend.2 = (bf16[2048,256]{1,0:T(8,128)(2,1)}, bf16[2048,256]{1,0:T(8,128)(2,1)}, bf16[2048,256]{1,0:T(8,128)(2,1)}, bf16[2048,256]{1,0:T(8,128)(2,1)}, f32[2,1,2048]{2,1,0:T(1,128)}) custom-call(s32[2]{0:T(128)} %pad_add_fusion.length_ref, f32[2048,768]{1,0:T(8,128)} %packed.2.packed_ref, f32[2048,128]{1,0:T(8,128)} %get-tuple-element.893.cos_ref, ...), custom_call_target="tpu_custom_call" | custom-call | flops 7046430720 | bytes 10485760 | tf_op jit(solution)/shard_map/attend/pallas_call | solution.py:383
  259.9 11.5 %attend.3 = (bf16[2048,256]{1,0:T(8,128)(2,1)}, bf16[2048,256]{1,0:T(8,128)(2,1)}, bf16[2048,256]{1,0:T(8,128)(2,1)}, bf16[2048,256]{1,0:T(8,128)(2,1)}, f32[2,1,2048]{2,1,0:T(1,128)}) custom-call(s32[2]{0:T(128)} %pad_add_fusion.length_ref, f32[2048,768]{1,0:T(8,128)} %packed.3.packed_ref, f32[2048,128]{1,0:T(8,128)} %get-tuple-element.893.cos_ref, ...), custom_call_target="tpu_custom_call" | custom-call | flops 7046430720 | bytes 10485760 | tf_op jit(solution)/shard_map/attend/pallas_call | solution.py:383
  293.8 9.3 %collective-permute-done.16 = bf16[1024,1024]{1,0:T(8,128)(2,1)} collective-permute-done((bf16[1024,1024]{1,0:T(8,128)(2,1)}, bf16[1024,1024]{1,0:T(8,128)(2,1)}, u32[]{:S(2)}, u32[]{:S(2)}) %collective-permute-start.16) | collective-permute-done | bytes 2097184 | tf_op jit(solution)/shard_map/ppermute | solution.py:540
  303.1 7.9 collective-permute-start.19
  334.2 13.0 %attend_back.2.right_ref = bf16[2048,768]{1,0:T(8,128)(2,1)} custom-call(s32[2]{0:T(128)} %pad_add_fusion.length_ref, bf16[2048,256]{1,0:T(8,128)(2,1)} %get-tuple-element.534.q_ref, bf16[2048,256]{1,0:T(8,128)(2,1)} %get-tuple-element.535.k_ref, bf16[2048,256]{1,0:T(8,128)(2,1)} %get-tuple-element.536.v_ref, bf16[2048,256]{1,0:T(8,128)(2,1)} %context_grad.2.grad_ref, ...), custom_call_target="tpu_custom_call" | custom-call | flops 9982443520 | bytes 7340032 | tf_op jit(solution)/shard_map/attend_back/pallas_call | solution.py:472
  357.3 12.2 %collective-permute-start.23 = (bf16[1024,1024]{1,0:T(8,128)(2,1)S(1)}, bf16[1024,1024]{1,0:T(8,128)(2,1)S(1)}, u32[]{:S(2)}, u32[]{:S(2)}) collective-permute-start(bf16[1024,1024]{1,0:T(8,128)(2,1)S(1)} %broadcast_select_fusion.3.kept_ref), channel_id=1, source_target_pairs={{0,4},{4,0},{1,5},{5,1},{2,6},{6,2},{3,7},{7,3},{8,12},{12,8},{9,1... | collective-permute-start | bytes 6291464 | tf_op jit(solution)/shard_map/ppermute | solution.py:575
  370.9 11.3 %gradients.12 = (bf16[1024,768]{1,0:T(8,128)(2,1)}, bf16[1024,768]{1,0:T(8,128)(2,1)S(1)}) custom-call(s32[1]{0:T(128)} %bitcast.6.upper_ref, bf16[2048,2048]{1,0:T(8,128)(2,1)} %copy-done.2, bf16[2048,768]{1,0:T(8,128)(2,1)} %attend_back.2.right_ref), custom_call_target="tpu_custom_call" | custom-call | flops 2818572288 | bytes 786432 | tf_op jit(solution)/shard_map/gradients/pallas_call | solution.py:135
  400.0 13.0 %attend_back.3.right_ref = bf16[2048,768]{1,0:T(8,128)(2,1)} custom-call(s32[2]{0:T(128)} %pad_add_fusion.length_ref, bf16[2048,256]{1,0:T(8,128)(2,1)} %get-tuple-element.570.q_ref, bf16[2048,256]{1,0:T(8,128)(2,1)} %get-tuple-element.571.k_ref, bf16[2048,256]{1,0:T(8,128)(2,1)} %get-tuple-element.572.v_ref, bf16[2048,256]{1,0:T(8,128)(2,1)} %context_grad.3.grad_ref, ...), custom_call_target="tpu_custom_call" | custom-call | flops 9982443520 | bytes 7340032 | tf_op jit(solution)/shard_map/attend_back/pallas_call | solution.py:472
  424.9 10.3 %gradients.13 = (bf16[1024,768]{1,0:T(8,128)(2,1)S(1)}, bf16[1024,768]{1,0:T(8,128)(2,1)S(1)}) custom-call(s32[1]{0:T(128)} %bitcast.6.upper_ref, bf16[2048,2048]{1,0:T(8,128)(2,1)} %copy-done.2, bf16[2048,768]{1,0:T(8,128)(2,1)} %attend_back.3.right_ref), custom_call_target="tpu_custom_call" | custom-call | flops 2818572288 | bytes 786432 | tf_op jit(solution)/shard_map/gradients/pallas_call | solution.py:135
  454.8 19.4 %to_one.1 = (bf16[1024,2048]{1,0:T(8,128)(2,1)}, bf16[1024,2048]{1,0:T(8,128)(2,1)}) custom-call(bf16[2048,1536]{1,0:T(8,128)(2,1)} %constant_dynamic-update-slice_fusion.refs_0_, bf16[2048,1536]{1,0:T(8,128)(2,1)} %refs_1_.15), custom_call_target="tpu_custom_call" | custom-call | flops 5637144576 | bytes 4194304 | tf_op jit(solution)/shard_map/to_one/pallas_call | solution.py:101
  474.2 9.4 %collective-permute-start.29 = (bf16[1024,1024]{1,0:T(8,128)(2,1)S(1)}, bf16[1024,1024]{1,0:T(8,128)(2,1)S(1)}, u32[]{:S(2)}, u32[]{:S(2)}) collective-permute-start(bf16[1024,1024]{1,0:T(8,128)(2,1)S(1)} %broadcast_select_fusion.2.kept_ref), channel_id=1, source_target_pairs={{0,4},{4,0},{1,5},{5,1},{2,6},{6,2},{3,7},{7,3},{8,12},{12,8},{9,1... | collective-permute-start | bytes 6291464 | tf_op jit(solution)/shard_map/ppermute | solution.py:575
  483.7 9.2 %collective-permute-start.30 = (bf16[1024,768]{1,0:T(8,128)(2,1)}, bf16[1024,768]{1,0:T(8,128)(2,1)}, u32[]{:S(2)}, u32[]{:S(2)}) collective-permute-start(bf16[1024,768]{1,0:T(8,128)(2,1)} %add_convert_fusion.20), channel_id=1, source_target_pairs={{0,8},{24,16},{1,9},{25,17},{2,10},{26,18},{3,11},{27,19},{4,12},{... | collective-permute-start | bytes 4718600 | tf_op jit(solution)/shard_map/ppermute | solution.py:540
  500.1 24.5 %to_two.1 = (bf16[1024,2048]{1,0:T(8,128)(2,1)}, bf16[1024,2048]{1,0:T(8,128)(2,1)}) custom-call(bf16[2048,1024]{1,0:T(8,128)(2,1)} %hidden_grad.2.right_ref.refs_0_, bf16[2048,2048]{1,0:T(8,128)(2,1)} %refs_3_.10, bf16[2048,1024]{1,0:T(8,128)(2,1)} %hidden_grad.3.right_ref.refs_2_, bf16[2048,2048]{1,0:T(8,128)(2,1)} %refs_3_.10), custom_call_target="tpu_custom_call" | custom-call | flops 7516192768 | bytes 4194304 | tf_op jit(solution)/shard_map/to_two/pallas_call | solution.py:101
  524.6 39.1 %collective-permute-done.32 = bf16[1024,768]{1,0:T(8,128)(2,1)} collective-permute-done((bf16[1024,768]{1,0:T(8,128)(2,1)S(1)}, bf16[1024,768]{1,0:T(8,128)(2,1)}, u32[]{:S(2)}, u32[]{:S(2)}) %collective-permute-start.32) | collective-permute-done | bytes 1572896 | tf_op jit(solution)/shard_map/ppermute | solution.py:568
  576.2 9.3 %collective-permute-start.35 = (bf16[1024,768]{1,0:T(8,128)(2,1)}, bf16[1024,768]{1,0:T(8,128)(2,1)}, u32[]{:S(2)}, u32[]{:S(2)}) collective-permute-start(bf16[1024,768]{1,0:T(8,128)(2,1)} %add_convert_fusion.18), channel_id=1, source_target_pairs={{0,8},{24,16},{1,9},{25,17},{2,10},{26,18},{3,11},{27,19},{4,12},{... | collective-permute-start | bytes 4718600 | tf_op jit(solution)/shard_map/ppermute | solution.py:540
  587.3 29.4 %to_out.1 = (bf16[1024,2048]{1,0:T(8,128)(2,1)}, bf16[1024,2048]{1,0:T(8,128)(2,1)}) custom-call(bf16[2048,512]{1,0:T(8,128)(2,1)} %copy-done.7, bf16[512,2048]{1,0:T(8,128)(2,1)} %refs_1_.17, bf16[2048,2048]{1,0:T(8,128)(2,1)} %get-tuple-element.648.left_ref.refs_2_, bf16[2048,2048]{1,0:T(8,128)(2,1)} %refs_3_.11), custom_call_target="tpu_custom_call" | custom-call | flops 9395240960 | bytes 4194304 | tf_op jit(solution)/shard_map/to_out/pallas_call | solution.py:101
  637.1 11.0 %collective-permute-done.38.got_ref = bf16[256,2048]{1,0:T(8,128)(2,1)S(1)} collective-permute-done((bf16[256,2048]{1,0:T(8,128)(2,1)S(1)}, bf16[256,2048]{1,0:T(8,128)(2,1)S(1)}, u32[]{:S(2)}, u32[]{:S(2)}) %collective-permute-start.38) | collective-permute-done | bytes 1048608 | tf_op jit(solution)/shard_map/ppermute | solution.py:575
  688.8 26.0 %collective-permute-done.43.got_ref = bf16[1024,1024]{1,0:T(8,128)(2,1)} collective-permute-done((bf16[1024,1024]{1,0:T(8,128)(2,1)}, bf16[1024,1024]{1,0:T(8,128)(2,1)}, u32[]{:S(2)}, u32[]{:S(2)}) %collective-permute-start.43) | collective-permute-done | bytes 2097184 | tf_op jit(solution)/shard_map/ppermute | solution.py:575
  714.8 8.4 %assemble.11 = f32[2048,2048]{1,0:T(8,128)} custom-call(s32[1]{0:T(128)} %bitcast.6.upper_ref, bf16[1024,1024]{1,0:T(8,128)(2,1)} %broadcast_select_fusion.kept_ref, bf16[1024,1024]{1,0:T(8,128)(2,1)} %collective-permute-done.43.got_ref, f32[2048,2048]{1,0:T(8,128)} %assemble.9.refs_0_), custom_call_target="tpu_custom_call", output_to_operand_aliasing={{}: (3, {})} | custom-call | tf_op jit(solution)/shard_map/assemble/pallas_call | solution.py:277
  739.3 8.0 fusion.16
  757.8 16.2 %collective-permute-done.50 = f32[192,128]{1,0:T(8,128)S(1)} collective-permute-done((f32[192,128]{1,0:T(8,128)S(1)}, f32[192,128]{1,0:T(8,128)S(1)}, u32[]{:S(2)}, u32[]{:S(2)}) %collective-permute-start.50) | collective-permute-done | bytes 98336 | tf_op jit(solution)/shard_map/ppermute | solution.py:502
  (290 shorter events, 347.6 us)
Async XLA Ops:
  1.2 49.0 %collective-permute-start = (bf16[512,2048]{1,0:T(8,128)(2,1)}, bf16[512,2048]{1,0:T(8,128)(2,1)S(1)}, u32[]{:S(2)}, u32[]{:S(2)}) collective-permute-start(bf16[512,2048]{1,0:T(8,128)(2,1)} %refs_0_.1), channel_id=1, source_target_pairs={{0,2},{1,3},{2,0},{3,1},{4,6},{5,7},{6,4},{7,5},{8,10},{9,11},{10,... | collective-permute-start | bytes 6291464 | tf_op jit(solution)/shard_map/ppermute | solution.py:502
  107.8 52.2 %collective-permute-start.9 = (bf16[1024,1024]{1,0:T(8,128)(2,1)}, bf16[1024,1024]{1,0:T(8,128)(2,1)}, u32[]{:S(2)}, u32[]{:S(2)}) collective-permute-start(bf16[1024,1024]{1,0:T(8,128)(2,1)} %fusion.24), channel_id=1, source_target_pairs={{0,4},{4,0},{1,5},{5,1},{2,6},{6,2},{3,7},{7,3},{8,12},{12,8},{9,1... | collective-permute-start | bytes 6291464 | tf_op jit(solution)/shard_map/ppermute | solution.py:568
  128.8 78.2 %collective-permute-start.10 = (bf16[1024,1024]{1,0:T(8,128)(2,1)}, bf16[1024,1024]{1,0:T(8,128)(2,1)}, u32[]{:S(2)}, u32[]{:S(2)}) collective-permute-start(bf16[1024,1024]{1,0:T(8,128)(2,1)} %get-tuple-element.483), channel_id=1, source_target_pairs={{0,4},{4,0},{1,5},{5,1},{2,6},{6,2},{3,7},{7,3},{8,12},{12,8},{9,1... | collective-permute-start | bytes 6291464 | tf_op jit(solution)/shard_map/ppermute | solution.py:568
  164.0 60.9 %collective-permute-start.11 = (bf16[1024,1024]{1,0:T(8,128)(2,1)}, bf16[1024,1024]{1,0:T(8,128)(2,1)}, u32[]{:S(2)}, u32[]{:S(2)}) collective-permute-start(bf16[1024,1024]{1,0:T(8,128)(2,1)} %add_convert_fusion.14), channel_id=1, source_target_pairs={{0,8},{24,16},{1,9},{25,17},{2,10},{26,18},{3,11},{27,19},{4,12},{... | collective-permute-start | bytes 6291464 | tf_op jit(solution)/shard_map/ppermute | solution.py:540
  174.7 78.5 %collective-permute-start.12 = (bf16[1024,1024]{1,0:T(8,128)(2,1)}, bf16[1024,1024]{1,0:T(8,128)(2,1)}, u32[]{:S(2)}, u32[]{:S(2)}) collective-permute-start(bf16[1024,1024]{1,0:T(8,128)(2,1)} %get-tuple-element.511), channel_id=1, source_target_pairs={{0,4},{4,0},{1,5},{5,1},{2,6},{6,2},{3,7},{7,3},{8,12},{12,8},{9,1... | collective-permute-start | bytes 6291464 | tf_op jit(solution)/shard_map/ppermute | solution.py:568
  206.2 87.5 %collective-permute-start.15 = (bf16[1024,1024]{1,0:T(8,128)(2,1)}, bf16[1024,1024]{1,0:T(8,128)(2,1)}, u32[]{:S(2)}, u32[]{:S(2)}) collective-permute-start(bf16[1024,1024]{1,0:T(8,128)(2,1)} %get-tuple-element.544), channel_id=1, source_target_pairs={{0,4},{4,0},{1,5},{5,1},{2,6},{6,2},{3,7},{7,3},{8,12},{12,8},{9,1... | collective-permute-start | bytes 6291464 | tf_op jit(solution)/shard_map/ppermute | solution.py:568
  210.9 61.9 %collective-permute-start.13 = (bf16[1024,1024]{1,0:T(8,128)(2,1)}, bf16[1024,1024]{1,0:T(8,128)(2,1)}, u32[]{:S(2)}, u32[]{:S(2)}) collective-permute-start(bf16[1024,1024]{1,0:T(8,128)(2,1)} %add_convert_fusion.13), channel_id=1, source_target_pairs={{0,8},{24,16},{1,9},{25,17},{2,10},{26,18},{3,11},{27,19},{4,12},{... | collective-permute-start | bytes 6291464 | tf_op jit(solution)/shard_map/ppermute | solution.py:540
  279.3 67.8 %collective-permute-start.17 = (bf16[1024,1024]{1,0:T(8,128)(2,1)S(1)}, bf16[1024,1024]{1,0:T(8,128)(2,1)}, u32[]{:S(2)}, u32[]{:S(2)}) collective-permute-start(bf16[1024,1024]{1,0:T(8,128)(2,1)S(1)} %add_convert_fusion.10), channel_id=1, source_target_pairs={{8,16},{16,8},{9,17},{17,9},{10,18},{18,10},{11,19},{19,11},{12,20... | collective-permute-start | bytes 6291464 | tf_op jit(solution)/shard_map/ppermute | solution.py:540
  281.3 65.9 %collective-permute-start.18 = (bf16[1024,1024]{1,0:T(8,128)(2,1)S(1)}, bf16[1024,1024]{1,0:T(8,128)(2,1)}, u32[]{:S(2)}, u32[]{:S(2)}) collective-permute-start(bf16[1024,1024]{1,0:T(8,128)(2,1)S(1)} %add_convert_fusion.9), channel_id=1, source_target_pairs={{8,0},{16,24},{9,1},{17,25},{10,2},{18,26},{11,3},{19,27},{12,4},{... | collective-permute-start | bytes 6291464 | tf_op jit(solution)/shard_map/ppermute | solution.py:540
  319.4 62.8 %collective-permute-start.20 = (bf16[1024,1024]{1,0:T(8,128)(2,1)}, bf16[1024,1024]{1,0:T(8,128)(2,1)}, u32[]{:S(2)}, u32[]{:S(2)}) collective-permute-start(bf16[1024,1024]{1,0:T(8,128)(2,1)} %add_convert_fusion.8), channel_id=1, source_target_pairs={{0,8},{24,16},{1,9},{25,17},{2,10},{26,18},{3,11},{27,19},{4,12},{... | collective-permute-start | bytes 6291464 | tf_op jit(solution)/shard_map/ppermute | solution.py:540
  325.2 57.0 %collective-permute-start.21 = (bf16[1024,1024]{1,0:T(8,128)(2,1)}, bf16[1024,1024]{1,0:T(8,128)(2,1)}, u32[]{:S(2)}, u32[]{:S(2)}) collective-permute-start(bf16[1024,1024]{1,0:T(8,128)(2,1)} %add_convert_fusion.7), channel_id=1, source_target_pairs={{8,16},{16,8},{9,17},{17,9},{10,18},{18,10},{11,19},{19,11},{12,20... | collective-permute-start | bytes 6291464 | tf_op jit(solution)/shard_map/ppermute | solution.py:540
  355.0 61.9 %collective-permute-start.22 = (bf16[256,2048]{1,0:T(8,128)(2,1)}, bf16[256,2048]{1,0:T(8,128)(2,1)}, u32[]{:S(2)}, u32[]{:S(2)}) collective-permute-start(bf16[256,2048]{1,0:T(8,128)(2,1)} %add_convert_fusion.23), channel_id=1, source_target_pairs={{0,8},{24,16},{1,9},{25,17},{2,10},{26,18},{3,11},{27,19},{4,12},{... | collective-permute-start | bytes 3145736 | tf_op jit(solution)/shard_map/ppermute | solution.py:540
  357.3 60.9 %collective-permute-start.23 = (bf16[1024,1024]{1,0:T(8,128)(2,1)S(1)}, bf16[1024,1024]{1,0:T(8,128)(2,1)S(1)}, u32[]{:S(2)}, u32[]{:S(2)}) collective-permute-start(bf16[1024,1024]{1,0:T(8,128)(2,1)S(1)} %broadcast_select_fusion.3.kept_ref), channel_id=1, source_target_pairs={{0,4},{4,0},{1,5},{5,1},{2,6},{6,2},{3,7},{7,3},{8,12},{12,8},{9,1... | collective-permute-start | bytes 6291464 | tf_op jit(solution)/shard_map/ppermute | solution.py:575
  382.2 65.0 %collective-permute-start.26 = (bf16[1024,768]{1,0:T(8,128)(2,1)}, bf16[1024,768]{1,0:T(8,128)(2,1)}, u32[]{:S(2)}, u32[]{:S(2)}) collective-permute-start(bf16[1024,768]{1,0:T(8,128)(2,1)} %get-tuple-element.607), channel_id=1, source_target_pairs={{0,4},{4,0},{1,5},{5,1},{2,6},{6,2},{3,7},{7,3},{8,12},{12,8},{9,1... | collective-permute-start | bytes 4718600 | tf_op jit(solution)/shard_map/ppermute | solution.py:568
  391.3 55.9 %collective-permute-start.25 = (bf16[1024,1024]{1,0:T(8,128)(2,1)}, bf16[1024,1024]{1,0:T(8,128)(2,1)}, u32[]{:S(2)}, u32[]{:S(2)}) collective-permute-start(bf16[1024,1024]{1,0:T(8,128)(2,1)} %add_convert_fusion.5), channel_id=1, source_target_pairs={{8,16},{16,8},{9,17},{17,9},{10,18},{18,10},{11,19},{19,11},{12,20... | collective-permute-start | bytes 6291464 | tf_op jit(solution)/shard_map/ppermute | solution.py:540
  416.9 66.8 %collective-permute-start.28 = (bf16[1024,1024]{1,0:T(8,128)(2,1)}, bf16[1024,1024]{1,0:T(8,128)(2,1)}, u32[]{:S(2)}, u32[]{:S(2)}) collective-permute-start(bf16[1024,1024]{1,0:T(8,128)(2,1)} %add_convert_fusion.4), channel_id=1, source_target_pairs={{8,0},{16,24},{9,1},{17,25},{10,2},{18,26},{11,3},{19,27},{12,4},{... | collective-permute-start | bytes 6291464 | tf_op jit(solution)/shard_map/ppermute | solution.py:540
  422.9 70.0 %collective-permute-start.27 = (bf16[256,2048]{1,0:T(8,128)(2,1)}, bf16[256,2048]{1,0:T(8,128)(2,1)}, u32[]{:S(2)}, u32[]{:S(2)}) collective-permute-start(bf16[256,2048]{1,0:T(8,128)(2,1)} %add_convert_fusion.22), channel_id=1, source_target_pairs={{8,16},{16,8},{9,17},{17,9},{10,18},{18,10},{11,19},{19,11},{12,20... | collective-permute-start | bytes 3145736 | tf_op jit(solution)/shard_map/ppermute | solution.py:540
  474.2 111.7 %collective-permute-start.33 = (bf16[1024,2048]{1,0:T(8,128)(2,1)}, bf16[1024,2048]{1,0:T(8,128)(2,1)}, u32[]{:S(2)}, u32[]{:S(2)}) collective-permute-start(bf16[1024,2048]{1,0:T(8,128)(2,1)} %get-tuple-element.656), channel_id=1, source_target_pairs={{0,1},{1,0},{2,3},{3,2},{4,5},{5,4},{6,7},{7,6},{8,9},{9,8},{10,11... | collective-permute-start | bytes 12582920 | tf_op jit(solution)/shard_map/ppermute | solution.py:502
  474.2 91.3 %collective-permute-start.29 = (bf16[1024,1024]{1,0:T(8,128)(2,1)S(1)}, bf16[1024,1024]{1,0:T(8,128)(2,1)S(1)}, u32[]{:S(2)}, u32[]{:S(2)}) collective-permute-start(bf16[1024,1024]{1,0:T(8,128)(2,1)S(1)} %broadcast_select_fusion.2.kept_ref), channel_id=1, source_target_pairs={{0,4},{4,0},{1,5},{5,1},{2,6},{6,2},{3,7},{7,3},{8,12},{12,8},{9,1... | collective-permute-start | bytes 6291464 | tf_op jit(solution)/shard_map/ppermute | solution.py:575
  483.6 80.1 %collective-permute-start.32 = (bf16[1024,768]{1,0:T(8,128)(2,1)S(1)}, bf16[1024,768]{1,0:T(8,128)(2,1)}, u32[]{:S(2)}, u32[]{:S(2)}) collective-permute-start(bf16[1024,768]{1,0:T(8,128)(2,1)S(1)} %copy-done.22), channel_id=1, source_target_pairs={{0,4},{4,0},{1,5},{5,1},{2,6},{6,2},{3,7},{7,3},{8,12},{12,8},{9,1... | collective-permute-start | bytes 4718600 | tf_op jit(solution)/shard_map/ppermute | solution.py:568
  483.7 81.8 %collective-permute-start.30 = (bf16[1024,768]{1,0:T(8,128)(2,1)}, bf16[1024,768]{1,0:T(8,128)(2,1)}, u32[]{:S(2)}, u32[]{:S(2)}) collective-permute-start(bf16[1024,768]{1,0:T(8,128)(2,1)} %add_convert_fusion.20), channel_id=1, source_target_pairs={{0,8},{24,16},{1,9},{25,17},{2,10},{26,18},{3,11},{27,19},{4,12},{... | collective-permute-start | bytes 4718600 | tf_op jit(solution)/shard_map/ppermute | solution.py:540
  498.4 67.1 %collective-permute-start.31 = (bf16[256,2048]{1,0:T(8,128)(2,1)}, bf16[256,2048]{1,0:T(8,128)(2,1)}, u32[]{:S(2)}, u32[]{:S(2)}) collective-permute-start(bf16[256,2048]{1,0:T(8,128)(2,1)} %add_convert_fusion.21), channel_id=1, source_target_pairs={{8,0},{16,24},{9,1},{17,25},{10,2},{18,26},{11,3},{19,27},{12,4},{... | collective-permute-start | bytes 3145736 | tf_op jit(solution)/shard_map/ppermute | solution.py:540
  563.7 59.1 %collective-permute-start.36 = (bf16[1024,1024]{1,0:T(8,128)(2,1)S(1)}, bf16[1024,1024]{1,0:T(8,128)(2,1)}, u32[]{:S(2)}, u32[]{:S(2)}) collective-permute-start(bf16[1024,1024]{1,0:T(8,128)(2,1)S(1)} %broadcast_select_fusion.1.kept_ref), channel_id=1, source_target_pairs={{0,4},{4,0},{1,5},{5,1},{2,6},{6,2},{3,7},{7,3},{8,12},{12,8},{9,1... | collective-permute-start | bytes 6291464 | tf_op jit(solution)/shard_map/ppermute | solution.py:575
  565.5 100.5 %collective-permute-start.39 = (bf16[1024,2048]{1,0:T(8,128)(2,1)}, bf16[1024,2048]{1,0:T(8,128)(2,1)}, u32[]{:S(2)}, u32[]{:S(2)}) collective-permute-start(bf16[1024,2048]{1,0:T(8,128)(2,1)} %get-tuple-element.695), channel_id=1, source_target_pairs={{0,1},{1,0},{2,3},{3,2},{4,5},{5,4},{6,7},{7,6},{8,9},{9,8},{10,11... | collective-permute-start | bytes 12582920 | tf_op jit(solution)/shard_map/ppermute | solution.py:502
  574.4 48.7 %collective-permute-start.34 = (bf16[1024,768]{1,0:T(8,128)(2,1)}, bf16[1024,768]{1,0:T(8,128)(2,1)}, u32[]{:S(2)}, u32[]{:S(2)}) collective-permute-start(bf16[1024,768]{1,0:T(8,128)(2,1)} %add_convert_fusion.19), channel_id=1, source_target_pairs={{8,16},{16,8},{9,17},{17,9},{10,18},{18,10},{11,19},{19,11},{12,20... | collective-permute-start | bytes 4718600 | tf_op jit(solution)/shard_map/ppermute | solution.py:540
  576.2 50.8 %collective-permute-start.35 = (bf16[1024,768]{1,0:T(8,128)(2,1)}, bf16[1024,768]{1,0:T(8,128)(2,1)}, u32[]{:S(2)}, u32[]{:S(2)}) collective-permute-start(bf16[1024,768]{1,0:T(8,128)(2,1)} %add_convert_fusion.18), channel_id=1, source_target_pairs={{0,8},{24,16},{1,9},{25,17},{2,10},{26,18},{3,11},{27,19},{4,12},{... | collective-permute-start | bytes 4718600 | tf_op jit(solution)/shard_map/ppermute | solution.py:540
  585.9 50.0 %collective-permute-start.37 = (bf16[1024,1024]{1,0:T(8,128)(2,1)}, bf16[1024,1024]{1,0:T(8,128)(2,1)}, u32[]{:S(2)}, u32[]{:S(2)}) collective-permute-start(bf16[1024,1024]{1,0:T(8,128)(2,1)} %add_convert_fusion.3), channel_id=1, source_target_pairs={{8,0},{16,24},{9,1},{17,25},{10,2},{18,26},{11,3},{19,27},{12,4},{... | collective-permute-start | bytes 6291464 | tf_op jit(solution)/shard_map/ppermute | solution.py:540
  623.1 100.1 %collective-permute-start.44 = (bf16[1024,2048]{1,0:T(8,128)(2,1)}, bf16[1024,2048]{1,0:T(8,128)(2,1)}, u32[]{:S(2)}, u32[]{:S(2)}) collective-permute-start(bf16[1024,2048]{1,0:T(8,128)(2,1)} %get-tuple-element.743), channel_id=1, source_target_pairs={{0,1},{1,0},{2,3},{3,2},{4,5},{5,4},{6,7},{7,6},{8,9},{9,8},{10,11... | collective-permute-start | bytes 12582920 | tf_op jit(solution)/shard_map/ppermute | solution.py:502
  627.0 51.9 %collective-permute-start.42 = (bf16[512,2048]{1,0:T(8,128)(2,1)}, bf16[512,2048]{1,0:T(8,128)(2,1)}, u32[]{:S(2)}, u32[]{:S(2)}) collective-permute-start(bf16[512,2048]{1,0:T(8,128)(2,1)} %add_convert_fusion.2), channel_id=1, source_target_pairs={{0,2},{1,3},{2,0},{3,1},{4,6},{5,7},{6,4},{7,5},{8,10},{9,11},{10,... | collective-permute-start | bytes 6291464 | tf_op jit(solution)/shard_map/ppermute | solution.py:502
  666.0 48.9 %collective-permute-start.43 = (bf16[1024,1024]{1,0:T(8,128)(2,1)}, bf16[1024,1024]{1,0:T(8,128)(2,1)}, u32[]{:S(2)}, u32[]{:S(2)}) collective-permute-start(bf16[1024,1024]{1,0:T(8,128)(2,1)} %broadcast_select_fusion.kept_ref), channel_id=1, source_target_pairs={{0,4},{4,0},{1,5},{5,1},{2,6},{6,2},{3,7},{7,3},{8,12},{12,8},{9,1... | collective-permute-start | bytes 6291464 | tf_op jit(solution)/shard_map/ppermute | solution.py:575
  675.5 53.1 %collective-permute-start.46 = (bf16[512,2048]{1,0:T(8,128)(2,1)}, bf16[512,2048]{1,0:T(8,128)(2,1)}, u32[]{:S(2)}, u32[]{:S(2)}) collective-permute-start(bf16[512,2048]{1,0:T(8,128)(2,1)} %add_convert_fusion.1), channel_id=1, source_target_pairs={{0,2},{1,3},{2,0},{3,1},{4,6},{5,7},{6,4},{7,5},{8,10},{9,11},{10,... | collective-permute-start | bytes 6291464 | tf_op jit(solution)/shard_map/ppermute | solution.py:502
  687.0 61.6 %collective-permute-start.47 = (bf16[1024,768]{1,0:T(8,128)(2,1)}, bf16[1024,768]{1,0:T(8,128)(2,1)}, u32[]{:S(2)}, u32[]{:S(2)}) collective-permute-start(bf16[1024,768]{1,0:T(8,128)(2,1)} %broadcast_select_fusion.5.kept_ref), channel_id=1, source_target_pairs={{0,4},{4,0},{1,5},{5,1},{2,6},{6,2},{3,7},{7,3},{8,12},{12,8},{9,1... | collective-permute-start | bytes 4718600 | tf_op jit(solution)/shard_map/ppermute | solution.py:575
  (69 other events, 1172.6 us)
